TPU v7x, 32 devices: a whole 2x2x4 slice. The times are simulated.
32 devices in a mesh: gx: 4 (over y, core), gy: 2 (over x), gz: 4 (over z).
Axes of the slice: x: 2, y: 2, z: 4, core: 2. Of those that a mesh axis runs over, the one named last changes fastest.
Arguments:
- offsets: float32 [4, 2, 8, 3, 128], P('gx', 'gy', 'gz'), may hold values from 0 to 1
- velocity: float32 [4, 2, 8, 3, 128], P('gx', 'gy', 'gz'), may hold values from -6 to 6
- masses: float32 [4, 2, 8, 128], P('gx', 'gy', 'gz'), may hold values from 0.004 to 0.016
- volumes: float32 [4, 2, 8, 128], P('gx', 'gy', 'gz'), may hold values from 0.004 to 0.016
- energies: float32 [4, 2, 8, 128], P('gx', 'gy', 'gz'), may hold values from 0.5 to 2
- smoothing: float32 [4, 2, 8, 128], P('gx', 'gy', 'gz'), may hold values from 0.35 to 0.6
- neighbours: int32 [4, 2, 8, 13], P('gx', 'gy', 'gz'), may hold values from 0 to 25, as said below
- counts: int32 [4, 2, 8], P('gx', 'gy', 'gz'), may hold values from 7 to 13, as said below
Outputs:
- acceleration: float32 [4, 2, 8, 3, 128], P('gx', 'gy', 'gz')
- heating: float32 [4, 2, 8, 128], P('gx', 'gy', 'gz')
Inputs may be any that keep to these rules, and one draw needn't show every extreme that they name: `neighbours`: the entries of one leaf are distinct codes. A leaf uses its first counts entries; the leaf at the grid's anchor uses all 13.
All inputs are finite; a program needn't handle non-finite values.
Results may differ from a plain program's by a relative error of at most 0.0003.
Values sent between devices are 32-bit elements; how exact they have to be, the bound alone decides.
No kernel may reach another device: no remote copies, remote signals or barrier semaphores. Data moves between devices by JAX's collectives and lax.ppermute only.
A program may use at most 64 MiB of HBM per device.

v0:
```python
import math

import jax
import jax.numpy as jnp
from jax import lax
from jax.sharding import PartitionSpec as P

kernel_norm = 21.0 / (16.0 * math.pi)
pressure_factor = 2.0 / 3.0
ridge_factor = 0.1


def extended(array, sides, width):
    for axis, dim in sides:
        count, length = (lax.axis_size(axis), array.shape[dim])
        up = [(i, (i + 1) % count) for i in range(count)]
        down = [(j, i) for i, j in up]
        last = lax.slice_in_dim(array, length - width, length, axis=dim)
        leading = lax.slice_in_dim(array, 0, width, axis=dim)
        before = lax.ppermute(last, axis, up)
        after = lax.ppermute(leading, axis, down)
        array = jnp.concatenate([before, array, after], axis=dim)
    return array


def directions(codes):
    shifted = codes + (codes >= 13).astype(jnp.int32)
    return (shifted // 9 - 1, shifted // 3 % 3 - 1, shifted % 3 - 1)


def kernel_parts(left_side, right_side, offset_shift):
    separation = (
        left_side[:, 0:3, :, None] - right_side[:, 0:3, None, :] - offset_shift[:, :, None, None]
    )
    dist_sq = jnp.sum(separation * separation, axis=1)
    smooth = 0.5 * (left_side[:, 9, :, None] + right_side[:, 9, None, :])
    inverse = 1.0 / smooth
    q_ratio = jnp.sqrt(dist_sq) * inverse
    remain = jnp.maximum(1.0 - 0.5 * q_ratio, 0.0)
    remain_cubed = remain * remain * remain
    scale_cubed = kernel_norm * inverse**3
    kernel_value = scale_cubed * remain_cubed * remain * (2.0 * q_ratio + 1.0)
    kernel_slope = -5.0 * scale_cubed * inverse * inverse * remain_cubed
    return (separation, kernel_value, kernel_slope)


def density_terms(left_side, left_extra, right_side, right_extra, offset_shift):
    separation, kernel_value, kernel_slope = kernel_parts(left_side, right_side, offset_shift)
    with_left = kernel_value * left_side[:, 7, :, None]
    with_right = kernel_value * right_side[:, 7, None, :]
    second_terms = [
        separation[:, 0] * separation[:, 0],
        separation[:, 0] * separation[:, 1],
        separation[:, 0] * separation[:, 2],
        separation[:, 1] * separation[:, 1],
        separation[:, 1] * separation[:, 2],
        separation[:, 2] * separation[:, 2],
    ]
    left_rows = [
        jnp.sum(kernel_value * right_side[:, 6, None, :], axis=2),
        jnp.sum(with_right, axis=2),
    ]
    left_rows += [jnp.sum(with_right * separation[:, column], axis=2) for column in range(3)]
    left_rows += [jnp.sum(with_right * moment_term, axis=2) for moment_term in second_terms]
    right_rows = [
        jnp.sum(kernel_value * left_side[:, 6, :, None], axis=1),
        jnp.sum(with_left, axis=1),
    ]
    right_rows += [-jnp.sum(with_left * separation[:, column], axis=1) for column in range(3)]
    right_rows += [jnp.sum(with_left * moment_term, axis=1) for moment_term in second_terms]
    return (jnp.stack(left_rows, axis=1), jnp.stack(right_rows, axis=1))


def corrections(moments, smooth, energy):
    density = moments[..., 0, :]
    zeroth = moments[..., 1, :]
    first_x = moments[..., 2, :]
    first_y = moments[..., 3, :]
    first_z = moments[..., 4, :]
    ridge_term = ridge_factor * smooth * smooth * zeroth
    s_xx = moments[..., 5, :] + ridge_term
    s_xy = moments[..., 6, :]
    s_xz = moments[..., 7, :]
    s_yy = moments[..., 8, :] + ridge_term
    s_yz = moments[..., 9, :]
    s_zz = moments[..., 10, :] + ridge_term
    c_xx = s_yy * s_zz - s_yz * s_yz
    c_xy = s_yz * s_xz - s_xy * s_zz
    c_xz = s_xy * s_yz - s_yy * s_xz
    c_yy = s_xx * s_zz - s_xz * s_xz
    c_yz = s_xy * s_xz - s_xx * s_yz
    c_zz = s_xx * s_yy - s_xy * s_xy
    determinant = s_xx * c_xx + s_xy * c_xy + s_xz * c_xz
    solve_x = (c_xx * first_x + c_xy * first_y + c_xz * first_z) / determinant
    solve_y = (c_xy * first_x + c_yy * first_y + c_yz * first_z) / determinant
    solve_z = (c_xz * first_x + c_yz * first_y + c_zz * first_z) / determinant
    coef_a = 1.0 / (zeroth - (first_x * solve_x + first_y * solve_y + first_z * solve_z))
    pressure = pressure_factor * density * energy
    return jnp.stack([pressure, coef_a, -solve_x, -solve_y, -solve_z], axis=-2)


def force_pair(left_side, left_fields, right_side, right_fields, offset_shift):
    separation, kernel_value, kernel_slope = kernel_parts(left_side, right_side, offset_shift)
    coef_left = left_fields[:, 1, :, None]
    coef_right = right_fields[:, 1, None, :]
    tilt_left = left_fields[:, 2:5, :, None]
    tilt_right = right_fields[:, 2:5, None, :]
    along_left = jnp.sum(tilt_left * separation, axis=1)
    along_right = jnp.sum(tilt_right * separation, axis=1)
    radial = kernel_slope * (coef_left * (1.0 + along_left) + coef_right * (1.0 - along_right))
    strength = (
        0.5
        * left_side[:, 7, :, None]
        * right_side[:, 7, None, :]
        * (left_fields[:, 0, :, None] + right_fields[:, 0, None, :])
    )
    gradient = (
        kernel_value[:, None] * (coef_left[:, None] * tilt_left - coef_right[:, None] * tilt_right)
        + radial[:, None] * separation
    )
    pair_force = strength[:, None] * gradient
    relative = left_side[:, 3:6, :, None] - right_side[:, 3:6, None, :]
    pair_work = 0.5 * jnp.sum(pair_force * relative, axis=1)
    left_sum = jnp.concatenate(
        [-jnp.sum(pair_force, axis=3), jnp.sum(pair_work, axis=2)[:, None]], axis=1
    )
    right_sum = jnp.concatenate(
        [jnp.sum(pair_force, axis=2), jnp.sum(pair_work, axis=1)[:, None]], axis=1
    )
    return (left_sum, right_sum)


def scatter_rows(values, row_index, row_count):
    item_count = values.shape[0]
    one_hot = (
        lax.broadcasted_iota(jnp.int32, (row_count, item_count), 0) == row_index[None, :]
    ).astype(jnp.float32)
    flattened = values.reshape(item_count, -1)
    summed = jnp.dot(
        one_hot, flattened, precision=lax.Precision.HIGHEST, preferred_element_type=jnp.float32
    )
    return summed.reshape((row_count,) + values.shape[1:])


def listed_sums(pair_fn, own_flat, own_extra, pad_flat, pad_extra, target, shifts, active):
    left_total = jnp.zeros((own_flat.shape[0],), jnp.float32)[:, None, None]
    right_parts = []
    for slot_index in range(target.shape[1]):
        right_side = jnp.take(pad_flat, target[:, slot_index], axis=0)
        right_extra = jnp.take(pad_extra, target[:, slot_index], axis=0)
        one_left, one_right = pair_fn(
            own_flat, own_extra, right_side, right_extra, shifts[:, slot_index]
        )
        scale_part = active[:, slot_index][:, None, None]
        left_total = left_total + one_left * scale_part
        right_parts.append(one_right * scale_part)
    return (left_total, right_parts)


def fold_back(collected):
    widened = extended(collected, (("gx", 0), ("gy", 1), ("gz", 2)), 1)
    for dim_index in range(3):
        length = widened.shape[dim_index]
        inner_part = lax.slice_in_dim(widened, 2, length - 2, axis=dim_index)
        before_rim = lax.slice_in_dim(widened, 0, 1, axis=dim_index)
        after_rim = lax.slice_in_dim(widened, length - 1, length, axis=dim_index)
        inner_length = length - 4
        if inner_length == 1:
            widened = inner_part + before_rim + after_rim
        else:
            head_part = lax.slice_in_dim(inner_part, 0, 1, axis=dim_index) + before_rim
            middle_part = lax.slice_in_dim(inner_part, 1, inner_length - 1, axis=dim_index)
            tail_part = (
                lax.slice_in_dim(inner_part, inner_length - 1, inner_length, axis=dim_index)
                + after_rim
            )
            widened = jnp.concatenate([head_part, middle_part, tail_part], axis=dim_index)
    return widened


def returned_sums(
    pair_fn,
    own_flat,
    own_extra,
    pad_flat,
    pad_extra,
    target,
    shifts,
    active,
    home,
    self_sum,
    grid_shape,
):
    left_total, right_parts = listed_sums(
        pair_fn, own_flat, own_extra, pad_flat, pad_extra, target, shifts, active
    )
    values = jnp.concatenate([self_sum + left_total] + right_parts, axis=0)
    indices = jnp.concatenate(
        [home] + [target[:, slot_index] for slot_index in range(target.shape[1])], axis=0
    )
    pad_count = grid_shape[0] * grid_shape[1] * grid_shape[2]
    collected = scatter_rows(values, indices, pad_count)
    folded = fold_back(collected.reshape(grid_shape + collected.shape[1:]))
    return folded.reshape((own_flat.shape[0],) + folded.shape[3:])


def per_device(offsets, velocity, masses, volumes, energies, smoothing, neighbours, counts):
    size_x, size_y, size_z = (masses.shape[0], masses.shape[1], masses.shape[2])
    per_leaf = masses.shape[3]
    slot_count = neighbours.shape[3]
    own_count = size_x * size_y * size_z
    pad_x, pad_y, pad_z = (size_x + 2, size_y + 2, size_z + 2)
    pad_count = pad_x * pad_y * pad_z
    grid_shape = (pad_x, pad_y, pad_z)
    own_state = jnp.concatenate(
        [
            offsets,
            velocity,
            masses[..., None, :],
            volumes[..., None, :],
            energies[..., None, :],
            smoothing[..., None, :],
        ],
        axis=3,
    )
    padded = extended(own_state, (("gx", 0), ("gy", 1), ("gz", 2)), 1)
    pad_flat = padded.reshape(pad_count, 10, per_leaf)
    own_flat = own_state.reshape(own_count, 10, per_leaf)
    coord_x = lax.broadcasted_iota(jnp.int32, (size_x, size_y, size_z), 0).reshape(own_count)
    coord_y = lax.broadcasted_iota(jnp.int32, (size_x, size_y, size_z), 1).reshape(own_count)
    coord_z = lax.broadcasted_iota(jnp.int32, (size_x, size_y, size_z), 2).reshape(own_count)
    home = ((coord_x + 1) * pad_y + coord_y + 1) * pad_z + coord_z + 1
    step_x, step_y, step_z = directions(neighbours.reshape(own_count, slot_count))
    target = home[:, None] + (step_x * pad_y + step_y) * pad_z + step_z
    shifts = jnp.stack([step_x, step_y, step_z], axis=-1).astype(jnp.float32)
    active = (
        lax.broadcasted_iota(jnp.int32, (own_count, slot_count), 1)
        < counts.reshape(own_count)[:, None]
    ).astype(jnp.float32)
    zero_shift = jnp.zeros((own_count, 3), jnp.float32)
    self_moments = density_terms(own_flat, own_flat, own_flat, own_flat, zero_shift)[0]
    moments = returned_sums(
        density_terms,
        own_flat,
        own_flat,
        pad_flat,
        pad_flat,
        target,
        shifts,
        active,
        home,
        self_moments,
        grid_shape,
    )
    own_fields = corrections(moments, own_flat[:, 9], own_flat[:, 8])
    pad_fields = extended(
        own_fields.reshape(size_x, size_y, size_z, 5, per_leaf),
        (("gx", 0), ("gy", 1), ("gz", 2)),
        1,
    )
    pad_fields = pad_fields.reshape(pad_count, 5, per_leaf)
    self_forces = force_pair(own_flat, own_fields, own_flat, own_fields, zero_shift)[0]
    pair_sums = returned_sums(
        force_pair,
        own_flat,
        own_fields,
        pad_flat,
        pad_fields,
        target,
        shifts,
        active,
        home,
        self_forces,
        grid_shape,
    )
    mass_flat = own_flat[:, 6]
    acceleration = (pair_sums[:, 0:3] / mass_flat[:, None]).reshape(
        size_x, size_y, size_z, 3, per_leaf
    )
    heating = (pair_sums[:, 3] / mass_flat).reshape(size_x, size_y, size_z, per_leaf)
    return (acceleration, heating)


def solution(mesh):
    in_specs = (
        P("gx", "gy", "gz", None, None),
        P("gx", "gy", "gz", None, None),
        P("gx", "gy", "gz", None),
        P("gx", "gy", "gz", None),
        P("gx", "gy", "gz", None),
        P("gx", "gy", "gz", None),
        P("gx", "gy", "gz", None),
        P("gx", "gy", "gz"),
    )
    out_specs = (P("gx", "gy", "gz", None, None), P("gx", "gy", "gz", None))
    return jax.shard_map(
        per_device, mesh=mesh, in_specs=in_specs, out_specs=out_specs, check_vma=False
    )
```

profile of v0, /device:TPU:0, one launch (start us, length us, event | category | flops | bytes accessed | tf_op | source)
XLA Modules:
  0.0 196.5 jit_solution(3531679891411780199)
XLA Ops:
  4.1 2.4 %collective-permute-start.1 = (f32[1,1,2,10,128]{4,2,3,1,0:T(2,128)S(1)}, f32[1,1,2,10,128]{4,2,3,1,0:T(2,128)S(1)}, u32[]{:S(2)}, u32[]{:S(2)}) collective-permute-start(f32[1,1,2,10,128]{4,2,3,1,0:T(2,128)S(1)} %constant_dynamic-update-slice_fusion), channel_id=1, source_target_pairs={{8,0},{16,8},{24,16},{0,24},{9,1},{17,9},{25,17},{1,25},{10,2},{18... | collective-permute-start | bytes 30728 | tf_op jit(solution)/shard_map/ppermute | solution.py:21
  12.3 1.6 collective-permute-start.3
  14.9 1.4 collective-permute-done.3
  16.3 1.4 collective-permute-done.2
  17.8 3.7 %collective-permute-start.5 = (f32[3,3,1,10,128]{4,2,3,1,0:T(1,128)S(1)}, f32[3,3,1,10,128]{4,2,3,1,0:T(1,128)S(1)}, u32[]{:S(2)}, u32[]{:S(2)}) collective-permute-start(f32[3,3,1,10,128]{4,2,3,1,0:T(1,128)S(1)} %get-tuple-element.499), channel_id=1, source_target_pairs={{1,0},{2,1},{3,2},{0,3},{5,4},{6,5},{7,6},{4,7},{9,8},{10,9},{11,1... | collective-permute-start | bytes 138248 | tf_op jit(solution)/shard_map/ppermute | solution.py:21
  25.3 2.1 %collective-permute-done.4 = f32[3,3,1,10,128]{4,2,3,1,0:T(1,128)S(1)} collective-permute-done((f32[3,3,1,10,128]{4,2,3,1,0:T(1,128)S(1)}, f32[3,3,1,10,128]{4,2,3,1,0:T(1,128)S(1)}, u32[]{:S(2)}, u32[]{:S(2)}) %collective-permute-start.4) | collective-permute-done | bytes 46112 | tf_op jit(solution)/shard_map/ppermute | solution.py:20
  57.6 1.3 multiply_reduce_fusion.184
  59.0 1.5 multiply_reduce_fusion.244
  62.2 2.2 %multiply_reduce_fusion.274 = (f32[2,128]{1,0:T(2,128)S(1)}, f32[2,128]{1,0:T(2,128)S(1)}, f32[2,128]{1,0:T(2,128)S(1)}, f32[2,128]{1,0:T(2,128)S(1)}, f32[2,128...) fusion(f32[2,3,128,128]{3,2,0,1:T(8,128)S(1)} %get-tuple-elemen, ...), kind=kLoop, calls=%fused_computation.843 | loop fusion | flops 4219392 | bytes 2003968 | tf_op jit(solution)/shard_map/reduce_sum | solution.py:64
  64.5 2.2 %multiply_reduce_fusion.214 = (f32[2,128]{1,0:T(2,128)S(1)}, f32[2,128]{1,0:T(2,128)S(1)}, f32[2,128]{1,0:T(2,128)S(1)}, f32[2,128]{1,0:T(2,128)S(1)}, f32[2,128...) fusion(f32[2,3,128,128]{3,2,0,1:T(8,128)S(1)} %get-tuple-elemen, ...), kind=kLoop, calls=%fused_computation.759 | loop fusion | flops 4219392 | bytes 2003968 | tf_op jit(solution)/shard_map/reduce_sum | solution.py:64
  66.7 0.8 multiply_reduce_fusion.144
  67.5 2.2 %multiply_reduce_fusion.304 = (f32[2,128]{1,0:T(2,128)S(1)}, f32[2,128]{1,0:T(2,128)S(1)}, f32[2,128]{1,0:T(2,128)S(1)}, f32[2,128]{1,0:T(2,128)S(1)}, f32[2,128...) fusion(f32[2,3,128,128]{3,2,0,1:T(8,128)S(1)} %get-tuple-elemen, ...), kind=kLoop, calls=%fused_computation.885 | loop fusion | flops 4219392 | bytes 2003968 | tf_op jit(solution)/shard_map/reduce_sum | solution.py:64
  70.6 1.5 multiply_reduce_fusion.314
  72.2 0.9 multiply_reduce_fusion.164
  82.6 0.8 fusion.135
  83.6 0.9 fusion.130
  85.9 0.9 slice.639
  86.8 1.8 collective-permute-start.7
  88.6 1.2 collective-permute-done.6
  89.8 0.9 constant_dynamic-update-slice_fusion.305
  90.9 0.8 collective-permute-start.9
  91.7 1.3 collective-permute-start.8
  93.0 3.9 %collective-permute-done.9 = f32[5,1,4,11,128]{4,2,3,1,0:T(4,128)S(1)} collective-permute-done((f32[5,1,4,11,128]{4,2,3,1,0:T(4,128)S(1)}, f32[5,1,4,11,128]{4,2,3,1,0:T(4,128)S(1)}, u32[]{:S(2)}, u32[]{:S(2)}) %collective-permute-start.9) | collective-permute-done | bytes 112672 | tf_op jit(solution)/shard_map/ppermute | solution.py:21
  96.8 2.4 %collective-permute-done.8 = f32[5,1,4,11,128]{4,2,3,1,0:T(4,128)S(1)} collective-permute-done((f32[5,1,4,11,128]{4,2,3,1,0:T(4,128)S(1)}, f32[5,1,4,11,128]{4,2,3,1,0:T(4,128)S(1)}, u32[]{:S(2)}, u32[]{:S(2)}) %collective-permute-start.8) | collective-permute-done | bytes 112672 | tf_op jit(solution)/shard_map/ppermute | solution.py:20
  99.5 1.8 collective-permute-start.11
  101.6 3.9 %collective-permute-done.11 = f32[5,5,1,11,128]{4,2,3,1,0:T(1,128)S(1)} collective-permute-done((f32[5,5,1,11,128]{4,2,3,1,0:T(1,128)S(1)}, f32[5,5,1,11,128]{4,2,3,1,0:T(1,128)S(1)}, u32[]{:S(2)}, u32[]{:S(2)}) %collective-permute-start.11) | collective-permute-done | bytes 140832 | tf_op jit(solution)/shard_map/ppermute | solution.py:21
  105.4 3.1 %collective-permute-done.10 = f32[5,5,1,11,128]{4,2,3,1,0:T(1,128)S(1)} collective-permute-done((f32[5,5,1,11,128]{4,2,3,1,0:T(1,128)S(1)}, f32[5,5,1,11,128]{4,2,3,1,0:T(1,128)S(1)}, u32[]{:S(2)}, u32[]{:S(2)}) %collective-permute-start.10) | collective-permute-done | bytes 140832 | tf_op jit(solution)/shard_map/ppermute | solution.py:20
  118.3 1.5 collective-permute-start.14
  119.7 1.7 collective-permute-done.15
  122.0 1.6 collective-permute-start.17
  124.1 1.8 collective-permute-done.17
  125.9 3.4 %collective-permute-done.16 = f32[3,3,1,5,128]{4,2,3,1,0:T(1,128)S(1)} collective-permute-done((f32[3,3,1,5,128]{4,2,3,1,0:T(1,128)S(1)}, f32[3,3,1,5,128]{4,2,3,1,0:T(1,128)S(1)}, u32[]{:S(2)}, u32[]{:S(2)}) %collective-permute-start.16) | collective-permute-done | bytes 23072 | tf_op jit(solution)/shard_map/ppermute | solution.py:20
  150.4 1.0 fusion.59
  151.4 0.9 add_multiply_fusion.16
  152.9 1.0 add_multiply_fusion.19
  156.8 1.1 fusion.47
  157.9 1.1 fusion.53
  161.5 1.1 fusion.45
  164.2 1.1 fusion.49
  177.9 0.8 fusion.150
  179.7 1.8 collective-permute-start.19
  181.4 1.4 collective-permute-done.18
  183.0 1.5 collective-permute-start.21
  185.1 2.3 %collective-permute-done.21 = f32[5,1,4,4,128]{4,2,3,1,0:T(4,128)S(1)} collective-permute-done((f32[5,1,4,4,128]{4,2,3,1,0:T(4,128)S(1)}, f32[5,1,4,4,128]{4,2,3,1,0:T(4,128)S(1)}, u32[]{:S(2)}, u32[]{:S(2)}) %collective-permute-start.21) | collective-permute-done | bytes 40992 | tf_op jit(solution)/shard_map/ppermute | solution.py:21
  187.4 1.2 collective-permute-done.20
  188.7 2.0 %collective-permute-start.22 = (f32[5,5,1,4,128]{4,2,3,1,0:T(1,128)S(1)}, f32[5,5,1,4,128]{4,2,3,1,0:T(1,128)S(1)}, u32[]{:S(2)}, u32[]{:S(2)}) collective-permute-start(f32[5,5,1,4,128]{4,2,3,1,0:T(1,128)S(1)} %get-tuple-element.494), channel_id=1, source_target_pairs={{0,1},{1,2},{2,3},{3,0},{4,5},{5,6},{6,7},{7,4},{8,9},{9,10},{10,1... | collective-permute-start | bytes 153608 | tf_op jit(solution)/shard_map/ppermute | solution.py:20
  190.7 2.6 %collective-permute-done.23 = f32[5,5,1,4,128]{4,2,3,1,0:T(1,128)S(1)} collective-permute-done((f32[5,5,1,4,128]{4,2,3,1,0:T(1,128)S(1)}, f32[5,5,1,4,128]{4,2,3,1,0:T(1,128)S(1)}, u32[]{:S(2)}, u32[]{:S(2)}) %collective-permute-start.23) | collective-permute-done | bytes 51232 | tf_op jit(solution)/shard_map/ppermute | solution.py:21
  193.3 1.3 collective-permute-done.22
  (925 shorter events, 111.7 us)
Async XLA Ops:
  4.1 8.2 %collective-permute-start.1 = (f32[1,1,2,10,128]{4,2,3,1,0:T(2,128)S(1)}, f32[1,1,2,10,128]{4,2,3,1,0:T(2,128)S(1)}, u32[]{:S(2)}, u32[]{:S(2)}) collective-permute-start(f32[1,1,2,10,128]{4,2,3,1,0:T(2,128)S(1)} %constant_dynamic-update-slice_fusion), channel_id=1, source_target_pairs={{8,0},{16,8},{24,16},{0,24},{9,1},{17,9},{25,17},{1,25},{10,2},{18... | collective-permute-start | bytes 30728 | tf_op jit(solution)/shard_map/ppermute | solution.py:21
  6.5 5.7 %collective-permute-start = (f32[1,1,2,10,128]{4,2,3,1,0:T(2,128)S(1)}, f32[1,1,2,10,128]{4,2,3,1,0:T(2,128)S(1)}, u32[]{:S(2)}, u32[]{:S(2)}) collective-permute-start(f32[1,1,2,10,128]{4,2,3,1,0:T(2,128)S(1)} %constant_dynamic-update-slice_fusion), channel_id=1, source_target_pairs={{0,8},{8,16},{16,24},{24,0},{1,9},{9,17},{17,25},{25,1},{2,10},{10... | collective-permute-start | bytes 30728 | tf_op jit(solution)/shard_map/ppermute | solution.py:20
  9.3 61.2 %copy-start.9 = (f32[2,128]{1,0:T(2,128)}, f32[2,128]{1,0:T(2,128)S(1)}, u32[]{:S(2)}) copy-start(f32[2,128]{1,0:T(2,128)S(1)} %get-tuple-element.585) | copy-start | bytes 3076
  9.3 62.9 %copy-start.11 = (f32[2,128]{1,0:T(2,128)}, f32[2,128]{1,0:T(2,128)S(1)}, u32[]{:S(2)}) copy-start(f32[2,128]{1,0:T(2,128)S(1)} %get-tuple-element.586) | copy-start | bytes 3076
  9.3 62.9 %copy-start.13 = (f32[2,128]{1,0:T(2,128)}, f32[2,128]{1,0:T(2,128)S(1)}, u32[]{:S(2)}) copy-start(f32[2,128]{1,0:T(2,128)S(1)} %get-tuple-element.584) | copy-start | bytes 3076
  10.7 35.4 %copy-start.114 = (s32[1024]{0:T(1024)}, s32[1024]{0:T(1024)S(1)}, u32[]{:S(2)}) copy-start(s32[1024]{0:T(1024)S(1)} %pad_clamp_fusion.1) | copy-start | bytes 12292
  10.7 32.9 %copy-start.115 = (s32[1024]{0:T(1024)}, s32[1024]{0:T(1024)S(1)}, u32[]{:S(2)}) copy-start(s32[1024]{0:T(1024)S(1)} %pad_clamp_fusion.2) | copy-start | bytes 12292
  10.9 37.6 %copy-start.117 = (s32[1024]{0:T(1024)}, s32[1024]{0:T(1024)S(1)}, u32[]{:S(2)}) copy-start(s32[1024]{0:T(1024)S(1)} %pad_clamp_fusion.12) | copy-start | bytes 12292
  12.1 69.0 %copy-start.93 = (f32[2]{0:T(128)}, f32[2]{0:T(128)S(1)}, u32[]{:S(2)}) copy-start(f32[2]{0:T(128)S(1)} %get-tuple-element.644) | copy-start | bytes 28
  12.1 69.2 %copy-start.90 = (f32[2]{0:T(128)}, f32[2]{0:T(128)S(1)}, u32[]{:S(2)}) copy-start(f32[2]{0:T(128)S(1)} %get-tuple-element.643) | copy-start | bytes 28
  12.2 69.4 %copy-start.87 = (f32[2]{0:T(128)}, f32[2]{0:T(128)S(1)}, u32[]{:S(2)}) copy-start(f32[2]{0:T(128)S(1)} %get-tuple-element.642) | copy-start | bytes 28
  12.2 69.6 %copy-start.84 = (f32[2]{0:T(128)}, f32[2]{0:T(128)S(1)}, u32[]{:S(2)}) copy-start(f32[2]{0:T(128)S(1)} %get-tuple-element.641) | copy-start | bytes 28
  12.2 69.9 %copy-start.80 = (f32[2]{0:T(128)}, f32[2]{0:T(128)S(1)}, u32[]{:S(2)}) copy-start(f32[2]{0:T(128)S(1)} %get-tuple-element.639) | copy-start | bytes 28
  12.2 69.9 %copy-start.82 = (f32[2]{0:T(128)}, f32[2]{0:T(128)S(1)}, u32[]{:S(2)}) copy-start(f32[2]{0:T(128)S(1)} %get-tuple-element.640) | copy-start | bytes 28
  12.3 4.0 %collective-permute-start.3 = (f32[3,1,2,10,128]{4,2,3,1,0:T(2,128)S(1)}, f32[3,1,2,10,128]{4,2,3,1,0:T(2,128)S(1)}, u32[]{:S(2)}, u32[]{:S(2)}) collective-permute-start(f32[3,1,2,10,128]{4,2,3,1,0:T(2,128)S(1)} %pad_maximum_fusion.22), channel_id=1, source_target_pairs={{4,0},{0,4},{5,1},{1,5},{6,2},{2,6},{7,3},{3,7},{12,8},{8,12},{13,... | collective-permute-start | bytes 92168 | tf_op jit(solution)/shard_map/ppermute | solution.py:21
  13.8 3.9 %collective-permute-start.2 = (f32[3,1,2,10,128]{4,2,3,1,0:T(2,128)S(1)}, f32[3,1,2,10,128]{4,2,3,1,0:T(2,128)S(1)}, u32[]{:S(2)}, u32[]{:S(2)}) collective-permute-start(f32[3,1,2,10,128]{4,2,3,1,0:T(2,128)S(1)} %pad_maximum_fusion.22), channel_id=1, source_target_pairs={{0,4},{4,0},{1,5},{5,1},{2,6},{6,2},{3,7},{7,3},{8,12},{12,8},{9,1... | collective-permute-start | bytes 92168 | tf_op jit(solution)/shard_map/ppermute | solution.py:20
  17.8 7.4 %collective-permute-start.5 = (f32[3,3,1,10,128]{4,2,3,1,0:T(1,128)S(1)}, f32[3,3,1,10,128]{4,2,3,1,0:T(1,128)S(1)}, u32[]{:S(2)}, u32[]{:S(2)}) collective-permute-start(f32[3,3,1,10,128]{4,2,3,1,0:T(1,128)S(1)} %get-tuple-element.499), channel_id=1, source_target_pairs={{1,0},{2,1},{3,2},{0,3},{5,4},{6,5},{7,6},{4,7},{9,8},{10,9},{11,1... | collective-permute-start | bytes 138248 | tf_op jit(solution)/shard_map/ppermute | solution.py:21
  21.5 5.9 %collective-permute-start.4 = (f32[3,3,1,10,128]{4,2,3,1,0:T(1,128)S(1)}, f32[3,3,1,10,128]{4,2,3,1,0:T(1,128)S(1)}, u32[]{:S(2)}, u32[]{:S(2)}) collective-permute-start(f32[3,3,1,10,128]{4,2,3,1,0:T(1,128)S(1)} %get-tuple-element.498), channel_id=1, source_target_pairs={{0,1},{1,2},{2,3},{3,0},{4,5},{5,6},{6,7},{7,4},{8,9},{9,10},{10,1... | collective-permute-start | bytes 138248 | tf_op jit(solution)/shard_map/ppermute | solution.py:20
  22.9 33.4 %copy-start.65 = (f32[2,3]{0,1:T(4,128)}, f32[2,3]{0,1:T(4,128)S(1)}, u32[]{:S(2)}) copy-start(f32[2,3]{0,1:T(4,128)S(1)} %copy.563) | copy-start | bytes 76
  23.1 33.2 %copy-start.59 = (f32[2,3]{0,1:T(4,128)}, f32[2,3]{0,1:T(4,128)S(1)}, u32[]{:S(2)}) copy-start(f32[2,3]{0,1:T(4,128)S(1)} %copy.559) | copy-start | bytes 76
  23.3 33.0 %copy-start.57 = (f32[2,3]{0,1:T(4,128)}, f32[2,3]{0,1:T(4,128)S(1)}, u32[]{:S(2)}) copy-start(f32[2,3]{0,1:T(4,128)S(1)} %copy.555) | copy-start | bytes 76
  23.5 32.8 %copy-start.53 = (f32[2,3]{0,1:T(4,128)}, f32[2,3]{0,1:T(4,128)S(1)}, u32[]{:S(2)}) copy-start(f32[2,3]{0,1:T(4,128)S(1)} %copy.551) | copy-start | bytes 76
  23.7 32.6 %copy-start.49 = (f32[2,3]{0,1:T(4,128)}, f32[2,3]{0,1:T(4,128)S(1)}, u32[]{:S(2)}) copy-start(f32[2,3]{0,1:T(4,128)S(1)} %copy.547) | copy-start | bytes 76
  23.9 32.4 %copy-start.45 = (f32[2,3]{0,1:T(4,128)}, f32[2,3]{0,1:T(4,128)S(1)}, u32[]{:S(2)}) copy-start(f32[2,3]{0,1:T(4,128)S(1)} %copy.543) | copy-start | bytes 76
  24.1 32.2 %copy-start.41 = (f32[2,3]{0,1:T(4,128)}, f32[2,3]{0,1:T(4,128)S(1)}, u32[]{:S(2)}) copy-start(f32[2,3]{0,1:T(4,128)S(1)} %copy.539) | copy-start | bytes 76
  24.3 32.0 %copy-start.43 = (f32[2,3]{0,1:T(4,128)}, f32[2,3]{0,1:T(4,128)S(1)}, u32[]{:S(2)}) copy-start(f32[2,3]{0,1:T(4,128)S(1)} %copy.535) | copy-start | bytes 76
  24.7 36.4 %copy-start.63 = (f32[2,3]{0,1:T(4,128)}, f32[2,3]{0,1:T(4,128)S(1)}, u32[]{:S(2)}) copy-start(f32[2,3]{0,1:T(4,128)S(1)} %copy.515) | copy-start | bytes 76
  24.9 36.2 %copy-start.51 = (f32[2,3]{0,1:T(4,128)}, f32[2,3]{0,1:T(4,128)S(1)}, u32[]{:S(2)}) copy-start(f32[2,3]{0,1:T(4,128)S(1)} %copy.527) | copy-start | bytes 76
  25.1 36.1 %copy-start.55 = (f32[2,3]{0,1:T(4,128)}, f32[2,3]{0,1:T(4,128)S(1)}, u32[]{:S(2)}) copy-start(f32[2,3]{0,1:T(4,128)S(1)} %copy.523) | copy-start | bytes 76
  25.3 35.9 %copy-start.61 = (f32[2,3]{0,1:T(4,128)}, f32[2,3]{0,1:T(4,128)S(1)}, u32[]{:S(2)}) copy-start(f32[2,3]{0,1:T(4,128)S(1)} %copy.519) | copy-start | bytes 76
  85.8 4.0 %collective-permute-start.6 = (f32[1,3,4,11,128]{4,2,3,1,0:T(4,128)}, f32[1,3,4,11,128]{4,2,3,1,0:T(4,128)}, u32[]{:S(2)}, u32[]{:S(2)}) collective-permute-start(f32[1,3,4,11,128]{4,2,3,1,0:T(4,128)} %copy.564), channel_id=1, source_target_pairs={{0,8},{8,16},{16,24},{24,0},{1,9},{9,17},{17,25},{25,1},{2,10},{10... | collective-permute-start | bytes 202760 | tf_op jit(solution)/shard_map/ppermute | solution.py:20
  86.8 4.0 %collective-permute-start.7 = (f32[1,3,4,11,128]{4,2,3,1,0:T(4,128)S(1)}, f32[1,3,4,11,128]{4,2,3,1,0:T(4,128)S(1)}, u32[]{:S(2)}, u32[]{:S(2)}) collective-permute-start(f32[1,3,4,11,128]{4,2,3,1,0:T(4,128)S(1)} %copy.565), channel_id=1, source_target_pairs={{8,0},{16,8},{24,16},{0,24},{9,1},{17,9},{25,17},{1,25},{10,2},{18... | collective-permute-start | bytes 202760 | tf_op jit(solution)/shard_map/ppermute | solution.py:21
  90.9 5.9 %collective-permute-start.9 = (f32[5,1,4,11,128]{4,2,3,1,0:T(4,128)S(1)}, f32[5,1,4,11,128]{4,2,3,1,0:T(4,128)S(1)}, u32[]{:S(2)}, u32[]{:S(2)}) collective-permute-start(f32[5,1,4,11,128]{4,2,3,1,0:T(4,128)S(1)} %get-tuple-element.491), channel_id=1, source_target_pairs={{4,0},{0,4},{5,1},{1,5},{6,2},{2,6},{7,3},{3,7},{12,8},{8,12},{13,... | collective-permute-start | bytes 337928 | tf_op jit(solution)/shard_map/ppermute | solution.py:21
  91.7 7.6 %collective-permute-start.8 = (f32[5,1,4,11,128]{4,2,3,1,0:T(4,128)S(1)}, f32[5,1,4,11,128]{4,2,3,1,0:T(4,128)S(1)}, u32[]{:S(2)}, u32[]{:S(2)}) collective-permute-start(f32[5,1,4,11,128]{4,2,3,1,0:T(4,128)S(1)} %get-tuple-element.490), channel_id=1, source_target_pairs={{0,4},{4,0},{1,5},{5,1},{2,6},{6,2},{3,7},{7,3},{8,12},{12,8},{9,1... | collective-permute-start | bytes 337928 | tf_op jit(solution)/shard_map/ppermute | solution.py:20
  99.5 6.0 %collective-permute-start.11 = (f32[5,5,1,11,128]{4,2,3,1,0:T(1,128)S(1)}, f32[5,5,1,11,128]{4,2,3,1,0:T(1,128)S(1)}, u32[]{:S(2)}, u32[]{:S(2)}) collective-permute-start(f32[5,5,1,11,128]{4,2,3,1,0:T(1,128)S(1)} %get-tuple-element.489), channel_id=1, source_target_pairs={{1,0},{2,1},{3,2},{0,3},{5,4},{6,5},{7,6},{4,7},{9,8},{10,9},{11,1... | collective-permute-start | bytes 422408 | tf_op jit(solution)/shard_map/ppermute | solution.py:21
  101.3 7.2 %collective-permute-start.10 = (f32[5,5,1,11,128]{4,2,3,1,0:T(1,128)S(1)}, f32[5,5,1,11,128]{4,2,3,1,0:T(1,128)S(1)}, u32[]{:S(2)}, u32[]{:S(2)}) collective-permute-start(f32[5,5,1,11,128]{4,2,3,1,0:T(1,128)S(1)} %get-tuple-element.488), channel_id=1, source_target_pairs={{0,1},{1,2},{2,3},{3,0},{4,5},{5,6},{6,7},{7,4},{8,9},{9,10},{10,1... | collective-permute-start | bytes 422408 | tf_op jit(solution)/shard_map/ppermute | solution.py:20
  108.8 8.8 %collective-permute-start.13 = (f32[1,1,2,5,128]{4,2,3,1,0:T(2,128)S(1)}, f32[1,1,2,5,128]{4,2,3,1,0:T(2,128)S(1)}, u32[]{:S(2)}, u32[]{:S(2)}) collective-permute-start(f32[1,1,2,5,128]{4,2,3,1,0:T(2,128)S(1)} %bitcast.2145), channel_id=1, source_target_pairs={{8,0},{16,8},{24,16},{0,24},{9,1},{17,9},{25,17},{1,25},{10,2},{18... | collective-permute-start | bytes 15368 | tf_op jit(solution)/shard_map/ppermute | solution.py:21
  108.9 8.7 %collective-permute-start.12 = (f32[1,1,2,5,128]{4,2,3,1,0:T(2,128)S(1)}, f32[1,1,2,5,128]{4,2,3,1,0:T(2,128)S(1)}, u32[]{:S(2)}, u32[]{:S(2)}) collective-permute-start(f32[1,1,2,5,128]{4,2,3,1,0:T(2,128)S(1)} %bitcast.2146), channel_id=1, source_target_pairs={{0,8},{8,16},{16,24},{24,0},{1,9},{9,17},{17,25},{25,1},{2,10},{10... | collective-permute-start | bytes 15368 | tf_op jit(solution)/shard_map/ppermute | solution.py:20
  117.6 3.8 %collective-permute-start.15 = (f32[3,1,2,5,128]{4,2,3,1,0:T(2,128)S(1)}, f32[3,1,2,5,128]{4,2,3,1,0:T(2,128)S(1)}, u32[]{:S(2)}, u32[]{:S(2)}) collective-permute-start(f32[3,1,2,5,128]{4,2,3,1,0:T(2,128)S(1)} %pad_maximum_fusion.35), channel_id=1, source_target_pairs={{4,0},{0,4},{5,1},{1,5},{6,2},{2,6},{7,3},{3,7},{12,8},{8,12},{13,... | collective-permute-start | bytes 46088 | tf_op jit(solution)/shard_map/ppermute | solution.py:21
  118.3 3.7 %collective-permute-start.14 = (f32[3,1,2,5,128]{4,2,3,1,0:T(2,128)S(1)}, f32[3,1,2,5,128]{4,2,3,1,0:T(2,128)S(1)}, u32[]{:S(2)}, u32[]{:S(2)}) collective-permute-start(f32[3,1,2,5,128]{4,2,3,1,0:T(2,128)S(1)} %pad_maximum_fusion.35), channel_id=1, source_target_pairs={{0,4},{4,0},{1,5},{5,1},{2,6},{6,2},{3,7},{7,3},{8,12},{12,8},{9,1... | collective-permute-start | bytes 46088 | tf_op jit(solution)/shard_map/ppermute | solution.py:20
  122.0 3.9 %collective-permute-start.17 = (f32[3,3,1,5,128]{4,2,3,1,0:T(1,128)S(1)}, f32[3,3,1,5,128]{4,2,3,1,0:T(1,128)S(1)}, u32[]{:S(2)}, u32[]{:S(2)}) collective-permute-start(f32[3,3,1,5,128]{4,2,3,1,0:T(1,128)S(1)} %get-tuple-element.503), channel_id=1, source_target_pairs={{1,0},{2,1},{3,2},{0,3},{5,4},{6,5},{7,6},{4,7},{9,8},{10,9},{11,1... | collective-permute-start | bytes 69128 | tf_op jit(solution)/shard_map/ppermute | solution.py:21
  123.7 5.6 %collective-permute-start.16 = (f32[3,3,1,5,128]{4,2,3,1,0:T(1,128)S(1)}, f32[3,3,1,5,128]{4,2,3,1,0:T(1,128)S(1)}, u32[]{:S(2)}, u32[]{:S(2)}) collective-permute-start(f32[3,3,1,5,128]{4,2,3,1,0:T(1,128)S(1)} %get-tuple-element.502), channel_id=1, source_target_pairs={{0,1},{1,2},{2,3},{3,0},{4,5},{5,6},{6,7},{7,4},{8,9},{9,10},{10,1... | collective-permute-start | bytes 69128 | tf_op jit(solution)/shard_map/ppermute | solution.py:20
  179.5 3.3 %collective-permute-start.18 = (f32[1,3,4,4,128]{4,2,3,1,0:T(4,128)S(1)}, f32[1,3,4,4,128]{4,2,3,1,0:T(4,128)S(1)}, u32[]{:S(2)}, u32[]{:S(2)}) collective-permute-start(f32[1,3,4,4,128]{4,2,3,1,0:T(4,128)S(1)} %copy.620), channel_id=1, source_target_pairs={{0,8},{8,16},{16,24},{24,0},{1,9},{9,17},{17,25},{25,1},{2,10},{10... | collective-permute-start | bytes 73736 | tf_op jit(solution)/shard_map/ppermute | solution.py:20
  179.7 3.3 %collective-permute-start.19 = (f32[1,3,4,4,128]{4,2,3,1,0:T(4,128)S(1)}, f32[1,3,4,4,128]{4,2,3,1,0:T(4,128)S(1)}, u32[]{:S(2)}, u32[]{:S(2)}) collective-permute-start(f32[1,3,4,4,128]{4,2,3,1,0:T(4,128)S(1)} %copy.621), channel_id=1, source_target_pairs={{8,0},{16,8},{24,16},{0,24},{9,1},{17,9},{25,17},{1,25},{10,2},{18... | collective-permute-start | bytes 73736 | tf_op jit(solution)/shard_map/ppermute | solution.py:21
  183.0 4.4 %collective-permute-start.21 = (f32[5,1,4,4,128]{4,2,3,1,0:T(4,128)S(1)}, f32[5,1,4,4,128]{4,2,3,1,0:T(4,128)S(1)}, u32[]{:S(2)}, u32[]{:S(2)}) collective-permute-start(f32[5,1,4,4,128]{4,2,3,1,0:T(4,128)S(1)} %get-tuple-element.497), channel_id=1, source_target_pairs={{4,0},{0,4},{5,1},{1,5},{6,2},{2,6},{7,3},{3,7},{12,8},{8,12},{13,... | collective-permute-start | bytes 122888 | tf_op jit(solution)/shard_map/ppermute | solution.py:21
  184.5 4.0 %collective-permute-start.20 = (f32[5,1,4,4,128]{4,2,3,1,0:T(4,128)S(1)}, f32[5,1,4,4,128]{4,2,3,1,0:T(4,128)S(1)}, u32[]{:S(2)}, u32[]{:S(2)}) collective-permute-start(f32[5,1,4,4,128]{4,2,3,1,0:T(4,128)S(1)} %get-tuple-element.496), channel_id=1, source_target_pairs={{0,4},{4,0},{1,5},{5,1},{2,6},{6,2},{3,7},{7,3},{8,12},{12,8},{9,1... | collective-permute-start | bytes 122888 | tf_op jit(solution)/shard_map/ppermute | solution.py:20
  188.6 4.7 %collective-permute-start.23 = (f32[5,5,1,4,128]{4,2,3,1,0:T(1,128)S(1)}, f32[5,5,1,4,128]{4,2,3,1,0:T(1,128)S(1)}, u32[]{:S(2)}, u32[]{:S(2)}) collective-permute-start(f32[5,5,1,4,128]{4,2,3,1,0:T(1,128)S(1)} %get-tuple-element.495), channel_id=1, source_target_pairs={{1,0},{2,1},{3,2},{0,3},{5,4},{6,5},{7,6},{4,7},{9,8},{10,9},{11,1... | collective-permute-start | bytes 153608 | tf_op jit(solution)/shard_map/ppermute | solution.py:21
  188.7 6.0 %collective-permute-start.22 = (f32[5,5,1,4,128]{4,2,3,1,0:T(1,128)S(1)}, f32[5,5,1,4,128]{4,2,3,1,0:T(1,128)S(1)}, u32[]{:S(2)}, u32[]{:S(2)}) collective-permute-start(f32[5,5,1,4,128]{4,2,3,1,0:T(1,128)S(1)} %get-tuple-element.494), channel_id=1, source_target_pairs={{0,1},{1,2},{2,3},{3,0},{4,5},{5,6},{6,7},{7,4},{8,9},{9,10},{10,1... | collective-permute-start | bytes 153608 | tf_op jit(solution)/shard_map/ppermute | solution.py:20
  (109 other events, 531.1 us)
where the time goes:
time: 198 us; the launch traced here: 197 us
  local copies, waits for them, and re-layouts  66.2 us (33%)
  other arithmetic  64.9 us (33%)
  waiting for transfers between devices  35.6 us (18%)
  starting transfers between devices  24.9 us (13%)
  between operations  3.99 us (2%)
    unnamed x506, local copies, waits for them, and re-layouts  28.8 us
    ppermute x12, waiting for transfers between devices, extended(): before = lax.ppermute(last, axis, up)  18 us
    ppermute x12, starting transfers between devices, extended(): after = lax.ppermute(leading, axis, down)  17.7 us
    ppermute x12, waiting for transfers between devices, extended(): after = lax.ppermute(leading, axis, down)  17.6 us
    reduce_sum x6, other arithmetic, density_terms(): jnp.sum(with_right * moment_term, axis=2)  11.1 us
    mul x26, other arithmetic, listed_sums(): right_parts.append(one_right * scale_part)  11 us
    gather x13, local copies, waits for them, and re-layouts, listed_sums(): right_extra = jnp.take(pad_extra, target[:, slot_index], axis=0)  8.72 us
    slice x27, local copies, waits for them, and re-layouts, force_pair(): relative = left_side[:, 3:6, :, None] - right_side[:, 3:6, None, :]  7.8 us
  transfers between devices with their start and end apart: 24, of which 18 were waited for; matrix products, arithmetic and copies ran while one was open for 6% of the time, Pallas kernels for 0%

commit v1 on v0

v1 whole, which is shorter than its diff:
```python
import functools
import math

import jax
import jax.numpy as jnp
from jax import lax
from jax.experimental import pallas as pl
from jax.experimental.pallas import tpu as pltpu
from jax.sharding import PartitionSpec as P

kernel_norm = 21.0 / (16.0 * math.pi)
pressure_factor = 2.0 / 3.0
ridge_factor = 0.1
pair_scale = -160.0 * kernel_norm

LIMIT = 16 * 1024 * 1024
AXES = ("gx", "gy", "gz")
X, Y, Z, H, V, M, FLAGS = range(7)
PR, CA, CX, CY, CZ, VX, VY, VZ = range(8)


def code_of(step):
    index = (step[0] + 1) * 9 + (step[1] + 1) * 3 + step[2] + 1
    return index if index < 13 else index - 1


def swap(array, axis, phase):
    count = lax.axis_size(axis)
    pairs = []
    for first in range(phase, count, 2):
        second = (first + 1) % count
        pairs += [(first, second), (second, first)]
    return lax.ppermute(array, axis, pairs)


def swaps(array, axis):
    count = lax.axis_size(axis)
    if count == 2:
        return [swap(array, axis, 0)]
    return [swap(array, axis, 1), swap(array, axis, 0)][::-1]


def beside(get, step, axis):
    if step == 0:
        return get(0)
    if lax.axis_size(axis) == 2:
        return get(1)
    even = lax.axis_index(axis) % 2 == 0
    first, second = (1, 2) if step == 1 else (2, 1)
    return jnp.where(even, get(first), get(second))


def spread(row, per_leaf):
    return jnp.broadcast_to(row, (8, per_leaf))


def block_list(stage, leaves):
    blocks = []
    for dx in (-1, 0, 1):
        for dy in (-1, 0, 1):
            for leaf in range(leaves):
                for dz in (-1, 0, 1):
                    level = leaf + dz
                    if level < 0 or level >= leaves:
                        kind = "z"
                    elif dx:
                        kind = "x"
                    elif dy:
                        kind = "y"
                    else:
                        kind = "own"
                    if kind == stage:
                        blocks.append((leaf, (dx, dy, dz)))
    return blocks


def tile_at(refs, stage, dx, dy, level, leaves):
    def along_x(kx):
        def along_y(ky):
            if stage == "own":
                return refs[0][level]
            if stage == "y":
                return refs[ky - 1][level]
            if stage == "x":
                return refs[kx - 1][ky, level]
            ny = 1 if lax.axis_size("gy") == 2 else 2
            column = kx * (1 + ny) + ky
            even = lax.axis_index("gz") % 2 == 0
            above = level >= leaves
            return jnp.where(
                even, refs[0 if above else 1][column], refs[1 if above else 0][column]
            )

        return beside(along_y, dy, "gy")

    return beside(along_x, dx, "gx")


def tile_key(dx, dy, level):
    if lax.axis_size("gx") == 2:
        dx = abs(dx)
    if lax.axis_size("gy") == 2:
        dy = abs(dy)
    return (dx, dy, level)


def plan(stage, leaves):
    groups = {}
    for number, (leaf, step) in enumerate(block_list(stage, leaves)):
        key = tile_key(step[0], step[1], leaf + step[2])
        groups.setdefault(key, []).append((number, leaf, step))
    return list(groups.items())


def moment_body(stage, leaves, per_leaf, count, *refs):
    own = refs[0]
    sources = refs[1 : 1 + count]
    rest = refs[1 + count :]
    if stage == "own":
        acc_in, rest = None, rest
    else:
        acc_in, rest = rest[0], rest[1:]
    acc_out, vw_out, vg_out, tall_out, row_ref, weight_ref = rest
    if stage == "own":
        sources = (own,)
    groups = plan(stage, leaves)
    for leaf in range(leaves):
        own_tile = own[leaf]
        for part in range(3):
            for shift in (-1, 0, 1):
                row_ref[leaf, 3 * part + shift + 1] = spread(
                    own_tile[part : part + 1] - float(shift), per_leaf
                )
        row_ref[leaf, 9] = spread(own_tile[H : H + 1], per_leaf)
    for place, ((dx, dy, level), blocks) in enumerate(groups):
        tile = tile_at(sources, stage, dx, dy, level, leaves)
        tall_out[place] = tile.T
        for number, leaf, step in blocks:
            if step != (0, 0, 0):
                code = code_of(step)
                weight = (
                    own[leaf][FLAGS : FLAGS + 1, code : code + 1]
                    + tile[FLAGS : FLAGS + 1, 25 - code : 26 - code]
                )
                weight_ref[number] = jnp.broadcast_to(weight, (8, per_leaf))

    def step_fn(strip, carry):
        rows = pl.ds(pl.multiple_of(strip * 8, 8), 8)
        carry = [list(part) for part in carry]
        for place, (_, blocks) in enumerate(groups):

            def column(feature):
                return jnp.broadcast_to(
                    tall_out[place, rows, feature : feature + 1], (8, per_leaf)
                )

            xj, yj, zj, hj, vj, mj = [column(feature) for feature in (X, Y, Z, H, V, M)]
            for number, leaf, step in blocks:
                dx = row_ref[leaf, step[0] + 1] - xj
                dy = row_ref[leaf, step[1] + 4] - yj
                dz = row_ref[leaf, step[2] + 7] - zj
                dist_sq = dx * dx + dy * dy + dz * dz
                inverse = 1.0 / (row_ref[leaf, 9] + hj)
                inverse_sq = inverse * inverse
                dist = dist_sq * lax.rsqrt(jnp.maximum(dist_sq, 1e-30))
                remain = jnp.maximum(1.0 - dist * inverse, 0.0)
                remain_sq = remain * remain
                edge = (inverse_sq * inverse) * (remain_sq * remain)
                if step != (0, 0, 0):
                    edge = edge * weight_ref[number]
                shape = remain * (0.2 * remain - 0.25)
                v_edge = vj * edge
                vw = v_edge * shape
                vg = v_edge * inverse_sq
                vw_out[number, rows, :] = vw
                vg_out[number, rows, :] = vg
                vx, vy, vz = vw * dx, vw * dy, vw * dz
                terms = [
                    (mj * edge) * shape,
                    vw,
                    vx,
                    vy,
                    vz,
                    vx * dx,
                    vx * dy,
                    vx * dz,
                    vy * dy,
                    vy * dz,
                    vz * dz,
                ]
                carry[leaf] = [total + term for total, term in zip(carry[leaf], terms)]
        return tuple(tuple(part) for part in carry)

    if acc_in is None:
        zero = jnp.zeros((8, per_leaf), jnp.float32)
        start = tuple((zero,) * 11 for _ in range(leaves))
    else:
        start = tuple(tuple(acc_in[leaf, k] for k in range(11)) for leaf in range(leaves))
    totals = lax.fori_loop(0, per_leaf // 8, step_fn, start)
    return own, acc_out, totals


def moment_kernel(stage, leaves, per_leaf, count, *refs):
    _, acc_out, totals = moment_body(stage, leaves, per_leaf, count, *refs)
    for leaf in range(leaves):
        for k in range(11):
            acc_out[leaf, k] = totals[leaf][k]


def corrections(moments, smooth, energy):
    density, zeroth, first_x, first_y, first_z, s_xx, s_xy, s_xz, s_yy, s_yz, s_zz = moments
    ridge_term = ridge_factor * smooth * smooth * zeroth
    s_xx = s_xx + ridge_term
    s_yy = s_yy + ridge_term
    s_zz = s_zz + ridge_term
    c_xx = s_yy * s_zz - s_yz * s_yz
    c_xy = s_yz * s_xz - s_xy * s_zz
    c_xz = s_xy * s_yz - s_yy * s_xz
    c_yy = s_xx * s_zz - s_xz * s_xz
    c_yz = s_xy * s_xz - s_xx * s_yz
    c_zz = s_xx * s_yy - s_xy * s_xy
    determinant = s_xx * c_xx + s_xy * c_xy + s_xz * c_xz
    solve_x = (c_xx * first_x + c_xy * first_y + c_xz * first_z) / determinant
    solve_y = (c_xy * first_x + c_yy * first_y + c_yz * first_z) / determinant
    solve_z = (c_xz * first_x + c_yz * first_y + c_zz * first_z) / determinant
    coef_a = 1.0 / (zeroth - (first_x * solve_x + first_y * solve_y + first_z * solve_z))
    pressure = pressure_factor * density * energy
    return [pressure, coef_a, -coef_a * solve_x, -coef_a * solve_y, -coef_a * solve_z]


def field_kernel(leaves, per_leaf, count, *refs):
    velocity, energies, fields_out = refs[-8:-5]
    own, _, totals = moment_body(
        "z", leaves, per_leaf, count, *refs[: 2 + count], None, *refs[-5:]
    )
    rows = []
    for k in range(11):
        parts = [jnp.sum(totals[leaf][k], axis=0, keepdims=True) for leaf in range(leaves)]
        rows.append(jnp.concatenate(parts, axis=0))
    smooth = jnp.concatenate([own[leaf][H : H + 1] for leaf in range(leaves)], axis=0)
    fields = corrections(rows, smooth, energies[0, 0])
    for k, value in enumerate(fields):
        for leaf in range(leaves):
            fields_out[leaf, k : k + 1, :] = value[leaf : leaf + 1]
    for leaf in range(leaves):
        fields_out[leaf, VX : VZ + 1, :] = velocity[0, 0, leaf]


def force_body(stage, leaves, per_leaf, count, *refs):
    own, own_fields = refs[0], refs[1]
    sources = refs[2 : 2 + count]
    rest = refs[2 + count :]
    if stage == "own":
        acc_in = None
        sources = (own_fields,)
    else:
        acc_in, rest = rest[0], rest[1:]
    vw_in, vg_in, tall_in = rest[:3]
    tall_ref, row_ref = rest[-2:]
    groups = plan(stage, leaves)
    for leaf in range(leaves):
        own_tile = own[leaf]
        own_field = own_fields[leaf]
        for part in range(3):
            for shift in (-1, 0, 1):
                row_ref[leaf, 3 * part + shift + 1] = spread(
                    own_tile[part : part + 1] - float(shift), per_leaf
                )
        for k in range(5):
            row_ref[leaf, 9 + k] = spread(own_field[k : k + 1], per_leaf)
    for place, ((dx, dy, level), blocks) in enumerate(groups):
        tall_ref[place] = tile_at(sources, stage, dx, dy, level, leaves).T

    def step_fn(strip, carry):
        rows = pl.ds(pl.multiple_of(strip * 8, 8), 8)
        carry = [list(part) for part in carry]
        for place, (_, blocks) in enumerate(groups):

            def column(ref, feature):
                return jnp.broadcast_to(ref[place, rows, feature : feature + 1], (8, per_leaf))

            xj, yj, zj = [column(tall_in, feature) for feature in (X, Y, Z)]
            pj, aj, cxj, cyj, czj, vxj, vyj, vzj = [column(tall_ref, k) for k in range(8)]
            for number, leaf, step in blocks:
                dx = row_ref[leaf, step[0] + 1] - xj
                dy = row_ref[leaf, step[1] + 4] - yj
                dz = row_ref[leaf, step[2] + 7] - zj
                tx = row_ref[leaf, 11] - cxj
                ty = row_ref[leaf, 12] - cyj
                tz = row_ref[leaf, 13] - czj
                strength = row_ref[leaf, 9] + pj
                along = tx * dx + ty * dy + tz * dz
                flat = strength * vw_in[number, rows, :]
                radial = (strength * vg_in[number, rows, :]) * ((row_ref[leaf, 10] + aj) + along)
                fx = flat * tx + radial * dx
                fy = flat * ty + radial * dy
                fz = flat * tz + radial * dz
                work = fx * vxj + fy * vyj + fz * vzj
                carry[leaf] = [
                    total + term for total, term in zip(carry[leaf], [fx, fy, fz, work])
                ]
        return tuple(tuple(part) for part in carry)

    if acc_in is None:
        zero = jnp.zeros((8, per_leaf), jnp.float32)
        start = tuple((zero,) * 4 for _ in range(leaves))
    else:
        start = tuple(tuple(acc_in[leaf, k] for k in range(4)) for leaf in range(leaves))
    return lax.fori_loop(0, per_leaf // 8, step_fn, start)


def force_kernel(stage, leaves, per_leaf, count, *refs):
    totals = force_body(stage, leaves, per_leaf, count, *refs)
    acc_out = refs[-3]
    for leaf in range(leaves):
        for k in range(4):
            acc_out[leaf, k] = totals[leaf][k]


def finish_kernel(leaves, per_leaf, count, *refs):
    totals = force_body("z", leaves, per_leaf, count, *refs)
    own, own_fields = refs[0], refs[1]
    acceleration, heating = refs[-4], refs[-3]
    for leaf in range(leaves):
        tile, field = own[leaf], own_fields[leaf]
        ratio = tile[V : V + 1] / tile[M : M + 1]
        force = [jnp.sum(totals[leaf][k], axis=0, keepdims=True) for k in range(4)]
        work = -force[3]
        for k in range(3):
            acceleration[0, 0, leaf, k : k + 1, :] = (-0.5 * ratio) * force[k]
            work = work + field[VX + k : VX + k + 1] * force[k]
        heating[0, 0, leaf : leaf + 1, :] = (0.25 * ratio) * work


def pack_kernel(leaves, per_leaf, offsets, volumes, masses, smoothing, neighbours, counts, out):
    lane = lax.broadcasted_iota(jnp.int32, (1, per_leaf), 1)
    for leaf in range(leaves):
        flags = jnp.zeros((1, per_leaf), jnp.float32)
        for slot in range(neighbours.shape[3]):
            code = jnp.where(slot < counts[0, 0, leaf], neighbours[0, 0, leaf, slot], -1)
            flags = flags + jnp.where(lane == code, 1.0, 0.0)
        out[leaf, X : Z + 1, :] = offsets[0, 0, leaf]
        out[leaf, H : H + 1, :] = smoothing[0, 0, leaf : leaf + 1]
        out[leaf, V : V + 1, :] = pair_scale * volumes[0, 0, leaf : leaf + 1]
        out[leaf, M : M + 1, :] = pair_scale * masses[0, 0, leaf : leaf + 1]
        out[leaf, FLAGS : FLAGS + 1, :] = flags
        out[leaf, FLAGS + 1 : FLAGS + 2, :] = jnp.zeros((1, per_leaf), jnp.float32)


def per_device(offsets, velocity, masses, volumes, energies, smoothing, neighbours, counts):
    leaves, per_leaf = masses.shape[2], masses.shape[3]
    f32 = jnp.float32
    vmem = pl.BlockSpec(memory_space=pltpu.VMEM)
    smem = pl.BlockSpec(memory_space=pltpu.SMEM)
    params = pltpu.CompilerParams(vmem_limit_bytes=LIMIT)
    parity = lax.axis_index("gz") % 2 == 0

    def cost(blocks, ops):
        return pl.CostEstimate(
            flops=blocks * per_leaf * per_leaf * ops, bytes_accessed=blocks * 4096, transcendentals=0
        )

    own = pl.pallas_call(
        functools.partial(pack_kernel, leaves, per_leaf),
        out_shape=jax.ShapeDtypeStruct((leaves, 8, per_leaf), f32),
        in_specs=[vmem] * 4 + [smem] * 2,
        out_specs=vmem,
        compiler_params=params,
        name="pack",
    )(offsets, volumes, masses, smoothing, neighbours, counts)

    def exchange_y(tile):
        return swaps(tile, "gy")

    def exchange_x(tile, from_y):
        return swaps(jnp.stack([tile] + from_y, axis=0), "gx")

    def exchange_z(tile, from_y, from_x):
        column = jnp.concatenate([jnp.stack([tile] + from_y, axis=0)] + from_x, axis=0)
        bottom, top = column[:, 0], column[:, leaves - 1]
        far = swap(jnp.where(parity, bottom, top), "gz", 1)
        near = swap(jnp.where(parity, top, bottom), "gz", 0)
        return [near, far]

    stages = ("own", "y", "x", "z")
    sizes = {stage: len(block_list(stage, leaves)) for stage in stages}
    tiles = {stage: len(plan(stage, leaves)) for stage in stages}

    def moment_call(stage, sources, acc):
        size = sizes[stage]
        kept = [
            jax.ShapeDtypeStruct((size, per_leaf, per_leaf), f32),
            jax.ShapeDtypeStruct((size, per_leaf, per_leaf), f32),
            jax.ShapeDtypeStruct((tiles[stage], per_leaf, 8), f32),
        ]
        operands = [own] + list(sources) + ([] if acc is None else [acc])
        if stage == "z":
            body = functools.partial(field_kernel, leaves, per_leaf, len(sources))
            operands += [velocity, energies]
            first = jax.ShapeDtypeStruct((leaves, 8, per_leaf), f32)
        else:
            body = functools.partial(moment_kernel, stage, leaves, per_leaf, len(sources))
            first = jax.ShapeDtypeStruct((leaves, 11, 8, per_leaf), f32)
        scratch = [
            pltpu.VMEM((leaves, 10, 8, per_leaf), f32),
            pltpu.VMEM((size, 8, per_leaf), f32),
        ]
        return pl.pallas_call(
            body,
            out_shape=[first] + kept,
            in_specs=[vmem] * len(operands),
            out_specs=[vmem] * 4,
            scratch_shapes=scratch,
            compiler_params=params,
            cost_estimate=cost(size, 55),
            name="moments_" + stage,
        )(*operands)

    def force_call(stage, sources, acc, kept, fields):
        size = sizes[stage]
        operands = [own, fields] + list(sources) + ([] if acc is None else [acc]) + list(kept)
        if stage == "z":
            body = functools.partial(finish_kernel, leaves, per_leaf, len(sources))
            out = [
                jax.ShapeDtypeStruct((1, 1, leaves, 3, per_leaf), f32),
                jax.ShapeDtypeStruct((1, 1, leaves, per_leaf), f32),
            ]
        else:
            body = functools.partial(force_kernel, stage, leaves, per_leaf, len(sources))
            out = [jax.ShapeDtypeStruct((leaves, 4, 8, per_leaf), f32)]
        scratch = [
            pltpu.VMEM((tiles[stage], per_leaf, 8), f32),
            pltpu.VMEM((leaves, 14, 8, per_leaf), f32),
        ]
        return pl.pallas_call(
            body,
            out_shape=out,
            in_specs=[vmem] * len(operands),
            out_specs=[vmem] * len(out),
            scratch_shapes=scratch,
            compiler_params=params,
            cost_estimate=cost(size, 36),
            name="force_" + stage,
        )(*operands)

    from_y = exchange_y(own)
    acc, *kept_own = moment_call("own", [], None)
    from_x = exchange_x(own, from_y)
    acc, *kept_y = moment_call("y", from_y, acc)
    from_z = exchange_z(own, from_y, from_x)
    acc, *kept_x = moment_call("x", from_x, acc)
    fields, *kept_z = moment_call("z", from_z, acc)

    field_y = exchange_y(fields)
    (acc,) = force_call("own", [], None, kept_own, fields)
    field_x = exchange_x(fields, field_y)
    (acc,) = force_call("y", field_y, acc, kept_y, fields)
    field_z = exchange_z(fields, field_y, field_x)
    (acc,) = force_call("x", field_x, acc, kept_x, fields)
    acceleration, heating = force_call("z", field_z, acc, kept_z, fields)
    return (acceleration, heating)


def solution(mesh):
    in_specs = (
        P("gx", "gy", "gz", None, None),
        P("gx", "gy", "gz", None, None),
        P("gx", "gy", "gz", None),
        P("gx", "gy", "gz", None),
        P("gx", "gy", "gz", None),
        P("gx", "gy", "gz", None),
        P("gx", "gy", "gz", None),
        P("gx", "gy", "gz"),
    )
    out_specs = (P("gx", "gy", "gz", None, None), P("gx", "gy", "gz", None))
    return jax.shard_map(
        per_device, mesh=mesh, in_specs=in_specs, out_specs=out_specs, check_vma=False
    )
```

time: 198 us -> 55.7 us (0.28)
  other arithmetic: 64.9 us -> 0.03 us
  local copies, waits for them, and re-layouts: 66.2 us -> 6.01 us
  waiting for transfers between devices: 35.6 us -> 6.58 us
  Pallas kernels: 0 us -> 27.2 us
  starting transfers between devices: 24.9 us -> 14.8 us
  between operations: 3.99 us -> 0.79 us
    ppermute x24 -> x10, waiting for transfers between devices: 35.6 us -> 6.58 us  [swap(): return lax.ppermute(array, axis, pairs)]
    pallas_call x0 -> x9, Pallas kernels: none -> 27.2 us  [the longest x4 13.4 us: moment_call(): pl.pallas_call(body, out_shape=[first] + kept, in_specs=[vmem] * len(oper...]
    unnamed x506 -> x14, local copies, waits for them, and re-layouts: 28.8 us -> 5.42 us
    reduce_sum x36 -> x0, other arithmetic: 23.2 us -> none  [the longest x6 11.1 us: density_terms(): jnp.sum(with_right * moment_term, axis=2)]
    mul x49 -> x0, other arithmetic: 18.3 us -> none  [the longest x26 11 us: listed_sums(): right_parts.append(one_right * scale_part)]
    slice x108 -> x0, local copies, waits for them, and re-layouts: 18.1 us -> none  [the longest x27 7.8 us: force_pair(): relative = left_side[:, 3:6, :, None] - right_side[:, 3:6, None, :]]
    gather x26 -> x0, local copies, waits for them, and re-layouts: 16.1 us -> none  [the longest x13 8.72 us: listed_sums(): right_extra = jnp.take(pad_extra, target[:, slot_index], axis=0)]
    select_n x33 -> x2, other arithmetic: 14.6 us -> 0.02 us  [exchange_z(): far = swap(jnp.where(parity, bottom, top), 'gz', 1)]
  transfers between devices with their start and end apart: 24 -> 10, of which waited for: 18 -> 4; matrix products, arithmetic and copies ran while one was open for 6% -> 1% of each run, Pallas kernels for 0% -> 30%
where the time goes in v1:
time: 55.7 us; the launch traced here: 55.4 us
  Pallas kernels  27.2 us (49%)
  starting transfers between devices  14.8 us (27%)
  waiting for transfers between devices  6.58 us (12%)
  local copies, waits for them, and re-layouts  6.01 us (11%)
  between operations  0.79 us (1%)
    ppermute x10, starting transfers between devices, swap(): return lax.ppermute(array, axis, pairs)  14.8 us
    pallas_call x4, Pallas kernels, moment_call(): pl.pallas_call(body, out_shape=[first] + kept, in_specs=[vmem] * len(oper...  13.4 us
    pallas_call x4, Pallas kernels, force_call(): pl.pallas_call(body, out_shape=out, in_specs=[vmem] * len(operands), out_...  13.2 us
    ppermute x10, waiting for transfers between devices, swap(): return lax.ppermute(array, axis, pairs)  6.58 us
    unnamed x14, local copies, waits for them, and re-layouts  5.42 us
  transfers between devices with their start and end apart: 10, of which 4 were waited for; matrix products, arithmetic and copies ran while one was open for 1% of the time, Pallas kernels for 30%

profile of v1, /device:TPU:0, one launch (start us, length us, event | category | flops | bytes accessed | tf_op | source)
XLA Modules:
  0.0 55.4 jit_solution(2970057900950722170)
XLA Ops:
  0.6 0.7 %copy.10.offsets = f32[1,1,2,3,128]{4,3,2,1,0:T(4,128)S(1)} copy(f32[1,1,2,3,128]{4,2,3,1,0:T(2,128)} %param.8) | data formatting | bytes 6144 | tf_op args[0]
  1.3 0.0 copy-start.1
  1.3 0.7 %copy-done.1 = f32[1,1,2,128]{3,2,1,0:T(2,128)S(1)} copy-done((f32[1,1,2,128]{3,2,1,0:T(2,128)S(1)}, f32[1,1,2,128]{3,2,1,0:T(2,128)}, u32[]{:S(2)}) %copy-start.1) | copy-done | bytes 1048
  2.0 0.0 copy-start.2
  2.0 0.7 %copy-done.2 = f32[1,1,2,128]{3,2,1,0:T(2,128)S(1)} copy-done((f32[1,1,2,128]{3,2,1,0:T(2,128)S(1)}, f32[1,1,2,128]{3,2,1,0:T(2,128)}, u32[]{:S(2)}) %copy-start.2) | copy-done | bytes 1048
  2.7 0.0 copy-start.3
  2.7 0.7 %copy-done.3 = f32[1,1,2,128]{3,2,1,0:T(2,128)S(1)} copy-done((f32[1,1,2,128]{3,2,1,0:T(2,128)S(1)}, f32[1,1,2,128]{3,2,1,0:T(2,128)}, u32[]{:S(2)}) %copy-start.3) | copy-done | bytes 1048
  3.4 0.0 copy-start.4
  3.4 0.7 %copy-done.4 = s32[1,1,2,13]{3,2,1,0:T(2,128)S(1)} copy-done((s32[1,1,2,13]{3,2,1,0:T(2,128)S(1)}, s32[1,1,2,13]{3,2,1,0:T(2,128)}, u32[]{:S(2)}) %copy-start.4) | copy-done | bytes 128
  4.0 0.0 copy-start.5
  4.0 0.7 %copy-done.5 = s32[1,1,2]{2,1,0:T(1,128)S(1)} copy-done((s32[1,1,2]{2,1,0:T(1,128)S(1)}, s32[1,1,2]{2,1,0:T(1,128)}, u32[]{:S(2)}) %copy-start.5) | copy-done | bytes 32
  4.7 0.6 %pack.1.refs_0_ = f32[2,8,128]{2,1,0:T(8,128)S(1)} custom-call(f32[1,1,2,3,128]{4,3,2,1,0:T(4,128)S(1)} %copy.10.offsets, f32[1,1,2,128]{3,2,1,0:T(2,128)S(1)} %copy-done.1, f32[1,1,2,128]{3,2,1,0:T(2,128)S(1)} %copy-done.2, f32[1,1,2,128]{3,2,1,0:T(2,128)S(1)} %copy-done.3, s32[1,1,2,13]{3,2,1,0:T(2,128)S(1)} %copy-done.4, s32[1,1,2]{2,1,0:T(1,128)S(1)} %copy-done.5), custom_call_target="tpu_custom_call" | custom-call | tf_op jit(solution)/shard_map/pack/pallas_call | solution.py:363
  5.3 3.0 %collective-permute-start = (f32[2,8,128]{2,1,0:T(8,128)S(1)}, f32[2,8,128]{2,1,0:T(8,128)S(1)}, u32[]{:S(2)}, u32[]{:S(2)}) collective-permute-start(f32[2,8,128]{2,1,0:T(8,128)S(1)} %pack.1.refs_0_), channel_id=1, source_target_pairs={{0,4},{4,0},{1,5},{5,1},{2,6},{6,2},{3,7},{7,3},{8,12},{12,8},{9,1... | collective-permute-start | bytes 24584 | tf_op jit(solution)/shard_map/ppermute | solution.py:33
  8.3 1.6 %collective-permute-done.refs_1_ = f32[2,8,128]{2,1,0:T(8,128)S(1)} collective-permute-done((f32[2,8,128]{2,1,0:T(8,128)S(1)}, f32[2,8,128]{2,1,0:T(8,128)S(1)}, u32[]{:S(2)}, u32[]{:S(2)}) %collective-permute-start) | collective-permute-done | bytes 8224 | tf_op jit(solution)/shard_map/ppermute | solution.py:33
  9.9 0.3 collective-permute-start.2
  10.3 1.8 %collective-permute-start.1 = (f32[2,2,8,128]{3,2,0,1:T(8,128)S(1)}, f32[2,2,8,128]{3,2,0,1:T(8,128)S(1)}, u32[]{:S(2)}, u32[]{:S(2)}) collective-permute-start(f32[2,2,8,128]{3,2,0,1:T(8,128)S(1)} %pad_maximum_fusion.2), channel_id=1, source_target_pairs={{0,8},{8,0},{16,24},{24,16},{1,9},{9,1},{17,25},{25,17},{2,10},{10... | collective-permute-start | bytes 49160 | tf_op jit(solution)/shard_map/ppermute | solution.py:33
  12.1 1.0 %collective-permute-done.2 = f32[2,2,8,128]{3,2,0,1:T(8,128)S(1)} collective-permute-done((f32[2,2,8,128]{3,2,0,1:T(8,128)S(1)}, f32[2,2,8,128]{3,2,0,1:T(8,128)S(1)}, u32[]{:S(2)}, u32[]{:S(2)}) %collective-permute-start.2) | collective-permute-done | bytes 16416 | tf_op jit(solution)/shard_map/ppermute | solution.py:33
  13.1 0.0 collective-permute-done.1
  13.1 4.3 %collective-permute-start.4 = (f32[6,8,128]{2,1,0:T(8,128)S(1)}, f32[6,8,128]{2,1,0:T(8,128)S(1)}, u32[]{:S(2)}, u32[]{:S(2)}) collective-permute-start(f32[6,8,128]{2,1,0:T(8,128)S(1)} %get-tuple-element.38), channel_id=1, source_target_pairs={{1,2},{2,1},{3,0},{0,3},{5,6},{6,5},{7,4},{4,7},{9,10},{10,9},{11,... | collective-permute-start | bytes 73736 | tf_op jit(solution)/shard_map/ppermute | solution.py:33
  17.4 0.0 collective-permute-start.3
  17.4 0.7 %copy.13.refs_4_ = f32[1,1,2,3,128]{4,3,2,1,0:T(4,128)S(1)} copy(f32[1,1,2,3,128]{4,2,3,1,0:T(2,128)} %param.9) | data formatting | bytes 6144 | tf_op args[1]
  18.1 2.0 %moments_own.1 = (f32[2,11,8,128]{3,2,1,0:T(8,128)S(1)}, f32[4,128,128]{2,1,0:T(8,128)S(1)}, f32[4,128,128]{2,1,0:T(8,128)S(1)}, f32[2,128,8]{2,1,0:T(8,128)S(1)}) custom-call(f32[2,8,128]{2,1,0:T(8,128)S(1)} %pack.1.refs_0_), custom_call_target="tpu_custom_call" | custom-call | flops 3604480 | bytes 16384 | tf_op jit(solution)/shard_map/moments_own/pallas_call | solution.py:408
  20.1 2.2 %moments_y.1 = (f32[2,11,8,128]{3,2,1,0:T(8,128)S(1)}, f32[8,128,128]{2,1,0:T(8,128)S(1)}, f32[8,128,128]{2,1,0:T(8,128)S(1)}, f32[2,128,8]{2,1,0:T(8,128)S(1)}) custom-call(f32[2,8,128]{2,1,0:T(8,128)S(1)} %pack.1.refs_0_, f32[2,8,128]{2,1,0:T(8,128)S(1)} %collective-permute-done.refs_1_, f32[2,11,8,128]{3,2,1,0:T(8,128)S(1)} %get-tuple-element.18.refs_2_), custom_call_target="tpu_custom_call" | custom-call | flops 7208960 | bytes 32768 | tf_op jit(solution)/shard_map/moments_y/pallas_call | solution.py:408
  22.4 5.0 %moments_x.1 = (f32[2,11,8,128]{3,2,1,0:T(8,128)S(1)}, f32[24,128,128]{2,1,0:T(8,128)S(1)}, f32[24,128,128]{2,1,0:T(8,128)S(1)}, f32[8,128,8]{2,1,0:T(8,128)S(1)}) custom-call(f32[2,8,128]{2,1,0:T(8,128)S(1)} %pack.1.refs_0_, f32[2,2,8,128]{3,2,1,0:T(8,128)S(1)} %copy.11.refs_1_, f32[2,2,8,128]{3,2,1,0:T(8,128)S(1)} %copy.12.refs_2_, ...), custom_call_target="tpu_custom_call" | custom-call | flops 21626880 | bytes 98304 | tf_op jit(solution)/shard_map/moments_x/pallas_call | solution.py:408
  27.4 0.0 collective-permute-done.4.refs_2_
  27.4 0.0 collective-permute-done.3.refs_1_
  27.4 0.0 copy-start
  27.4 0.7 %copy-done = f32[1,1,2,128]{3,2,1,0:T(2,128)S(1)} copy-done((f32[1,1,2,128]{3,2,1,0:T(2,128)S(1)}, f32[1,1,2,128]{3,2,1,0:T(2,128)}, u32[]{:S(2)}) %copy-start) | copy-done | bytes 1048
  28.1 4.2 %moments_z.1 = (f32[2,8,128]{2,1,0:T(8,128)S(1)}, f32[18,128,128]{2,1,0:T(8,128)S(1)}, f32[18,128,128]{2,1,0:T(8,128)S(1)}, f32[12,128,8]{2,1,0:T(8,128)S(1)}) custom-call(f32[2,8,128]{2,1,0:T(8,128)S(1)} %pack.1.refs_0_, f32[6,8,128]{2,1,0:T(8,128)S(1)} %collective-permute-done.3.refs_1_, f32[6,8,128]{2,1,0:T(8,128)S(1)} %collective-permute-done.4.refs_2_, ...), custom_call_target="tpu_custom_call" | custom-call | flops 16220160 | bytes 73728 | tf_op jit(solution)/shard_map/moments_z/pallas_call | solution.py:408
  32.3 1.6 %collective-permute-start.5 = (f32[2,8,128]{2,1,0:T(8,128)S(1)}, f32[2,8,128]{2,1,0:T(8,128)S(1)}, u32[]{:S(2)}, u32[]{:S(2)}) collective-permute-start(f32[2,8,128]{2,1,0:T(8,128)S(1)} %get-tuple-element.21.refs_1_), channel_id=1, source_target_pairs={{0,4},{4,0},{1,5},{5,1},{2,6},{6,2},{3,7},{7,3},{8,12},{12,8},{9,1... | collective-permute-start | bytes 24584 | tf_op jit(solution)/shard_map/ppermute | solution.py:33
  33.9 2.2 %collective-permute-done.5.refs_2_ = f32[2,8,128]{2,1,0:T(8,128)S(1)} collective-permute-done((f32[2,8,128]{2,1,0:T(8,128)S(1)}, f32[2,8,128]{2,1,0:T(8,128)S(1)}, u32[]{:S(2)}, u32[]{:S(2)}) %collective-permute-start.5) | collective-permute-done | bytes 8224 | tf_op jit(solution)/shard_map/ppermute | solution.py:33
  36.0 0.0 collective-permute-start.7
  36.0 1.5 %collective-permute-start.6 = (f32[2,2,8,128]{3,2,0,1:T(8,128)S(1)}, f32[2,2,8,128]{3,2,0,1:T(8,128)S(1)}, u32[]{:S(2)}, u32[]{:S(2)}) collective-permute-start(f32[2,2,8,128]{3,2,0,1:T(8,128)S(1)} %pad_maximum_fusion.3), channel_id=1, source_target_pairs={{0,8},{8,0},{16,24},{24,16},{1,9},{9,1},{17,25},{25,17},{2,10},{10... | collective-permute-start | bytes 49160 | tf_op jit(solution)/shard_map/ppermute | solution.py:33
  37.6 1.8 %collective-permute-done.7 = f32[2,2,8,128]{3,2,0,1:T(8,128)S(1)} collective-permute-done((f32[2,2,8,128]{3,2,0,1:T(8,128)S(1)}, f32[2,2,8,128]{3,2,0,1:T(8,128)S(1)}, u32[]{:S(2)}, u32[]{:S(2)}) %collective-permute-start.7) | collective-permute-done | bytes 16416 | tf_op jit(solution)/shard_map/ppermute | solution.py:33
  39.3 0.0 collective-permute-done.6
  39.4 1.0 %collective-permute-start.9 = (f32[6,8,128]{2,1,0:T(8,128)S(1)}, f32[6,8,128]{2,1,0:T(8,128)S(1)}, u32[]{:S(2)}, u32[]{:S(2)}) collective-permute-start(f32[6,8,128]{2,1,0:T(8,128)S(1)} %get-tuple-element.36), channel_id=1, source_target_pairs={{1,2},{2,1},{3,0},{0,3},{5,6},{6,5},{7,4},{4,7},{9,10},{10,9},{11,... | collective-permute-start | bytes 73736 | tf_op jit(solution)/shard_map/ppermute | solution.py:33
  40.3 1.2 %collective-permute-start.8 = (f32[6,8,128]{2,1,0:T(8,128)S(1)}, f32[6,8,128]{2,1,0:T(8,128)S(1)}, u32[]{:S(2)}, u32[]{:S(2)}) collective-permute-start(f32[6,8,128]{2,1,0:T(8,128)S(1)} %get-tuple-element.37), channel_id=1, source_target_pairs={{0,1},{1,0},{2,3},{3,2},{4,5},{5,4},{6,7},{7,6},{8,9},{9,8},{10,11... | collective-permute-start | bytes 73736 | tf_op jit(solution)/shard_map/ppermute | solution.py:33
  41.5 1.9 %force_own.1.refs_3_ = f32[2,4,8,128]{3,2,1,0:T(8,128)S(1)} custom-call(f32[2,8,128]{2,1,0:T(8,128)S(1)} %pack.1.refs_0_, f32[2,8,128]{2,1,0:T(8,128)S(1)} %get-tuple-element.21.refs_1_, f32[4,128,128]{2,1,0:T(8,128)S(1)} %get-tuple-element.22.refs_2_, f32[4,128,128]{2,1,0:T(8,128)S(1)} %get-tuple-element.23.refs_3_, f32[2,128,8]{2,1,0:T(8,128)S(1)} %get-tuple-element.24.refs_4_), custom_call_target="tpu_custom_call" | custom-call | flops 2359296 | bytes 16384 | tf_op jit(solution)/shard_map/force_own/pallas_call | solution.py:435
  43.4 2.0 %force_y.1.refs_4_ = f32[2,4,8,128]{3,2,1,0:T(8,128)S(1)} custom-call(f32[2,8,128]{2,1,0:T(8,128)S(1)} %pack.1.refs_0_, f32[2,8,128]{2,1,0:T(8,128)S(1)} %get-tuple-element.21.refs_1_, f32[2,8,128]{2,1,0:T(8,128)S(1)} %collective-permute-done.5.refs_2_, f32[2,4,8,128]{3,2,1,0:T(8,128)S(1)} %force_own.1.refs_3_, ...), custom_call_target="tpu_custom_call" | custom-call | flops 4718592 | bytes 32768 | tf_op jit(solution)/shard_map/force_y/pallas_call | solution.py:435
  45.4 3.8 %force_x.1.refs_4_ = f32[2,4,8,128]{3,2,1,0:T(8,128)S(1)} custom-call(f32[2,8,128]{2,1,0:T(8,128)S(1)} %pack.1.refs_0_, f32[2,8,128]{2,1,0:T(8,128)S(1)} %get-tuple-element.21.refs_1_, f32[2,2,8,128]{3,2,1,0:T(8,128)S(1)} %copy.14.refs_2_, f32[2,2,8,128]{3,2,1,0:T(8,128)S(1)} %copy.15.refs_3_, f32[2,4,8,128]{3,2,1,0:T(8,128)S(1)} %force_y.1.refs_4_, ...), custom_call_target="tpu_custom_call" | custom-call | flops 14155776 | bytes 98304 | tf_op jit(solution)/shard_map/force_x/pallas_call | solution.py:435
  49.2 0.0 collective-permute-done.9.refs_3_
  49.2 0.0 collective-permute-done.8.refs_2_
  49.2 5.6 %force_z.1 = (f32[1,1,2,3,128]{4,3,2,1,0:T(4,128)S(1)}, f32[1,1,2,128]{3,2,1,0:T(2,128)}) custom-call(f32[2,8,128]{2,1,0:T(8,128)S(1)} %pack.1.refs_0_, f32[2,8,128]{2,1,0:T(8,128)S(1)} %get-tuple-element.21.refs_1_, f32[6,8,128]{2,1,0:T(8,128)S(1)} %collective-permute-done.8.refs_2_, f32[6,8,128]{2,1,0:T(8,128)S(1)} %collective-permute-done.9.refs_3_, ...), custom_call_target="tpu_custom_call" | custom-call | flops 10616832 | bytes 73728 | tf_op jit(solution)/shard_map/force_z/pallas_call | solution.py:435
  54.8 0.6 %copy.16 = f32[1,1,2,3,128]{4,2,3,1,0:T(2,128)} copy(f32[1,1,2,3,128]{4,3,2,1,0:T(4,128)S(1)} %get-tuple-element.34) | data formatting | bytes 6144 | tf_op jit(solution)/shard_map/force_z/pallas_call | solution.py:435
  (10 shorter events, 0.0 us)
Async XLA Ops:
  1.3 0.7 %copy-start.1 = (f32[1,1,2,128]{3,2,1,0:T(2,128)S(1)}, f32[1,1,2,128]{3,2,1,0:T(2,128)}, u32[]{:S(2)}) copy-start(f32[1,1,2,128]{3,2,1,0:T(2,128)} %volumes.1) | copy-start | bytes 3076
  2.0 0.7 %copy-start.2 = (f32[1,1,2,128]{3,2,1,0:T(2,128)S(1)}, f32[1,1,2,128]{3,2,1,0:T(2,128)}, u32[]{:S(2)}) copy-start(f32[1,1,2,128]{3,2,1,0:T(2,128)} %masses.1) | copy-start | bytes 3076
  2.7 0.7 %copy-start.3 = (f32[1,1,2,128]{3,2,1,0:T(2,128)S(1)}, f32[1,1,2,128]{3,2,1,0:T(2,128)}, u32[]{:S(2)}) copy-start(f32[1,1,2,128]{3,2,1,0:T(2,128)} %smoothing.1) | copy-start | bytes 3076
  3.4 0.7 %copy-start.4 = (s32[1,1,2,13]{3,2,1,0:T(2,128)S(1)}, s32[1,1,2,13]{3,2,1,0:T(2,128)}, u32[]{:S(2)}) copy-start(s32[1,1,2,13]{3,2,1,0:T(2,128)} %neighbours.1) | copy-start | bytes 316
  4.0 0.7 %copy-start.5 = (s32[1,1,2]{2,1,0:T(1,128)S(1)}, s32[1,1,2]{2,1,0:T(1,128)}, u32[]{:S(2)}) copy-start(s32[1,1,2]{2,1,0:T(1,128)} %counts.1) | copy-start | bytes 28
  5.3 4.7 %collective-permute-start = (f32[2,8,128]{2,1,0:T(8,128)S(1)}, f32[2,8,128]{2,1,0:T(8,128)S(1)}, u32[]{:S(2)}, u32[]{:S(2)}) collective-permute-start(f32[2,8,128]{2,1,0:T(8,128)S(1)} %pack.1.refs_0_), channel_id=1, source_target_pairs={{0,4},{4,0},{1,5},{5,1},{2,6},{6,2},{3,7},{7,3},{8,12},{12,8},{9,1... | collective-permute-start | bytes 24584 | tf_op jit(solution)/shard_map/ppermute | solution.py:33
  9.9 3.2 %collective-permute-start.2 = (f32[2,2,8,128]{3,2,0,1:T(8,128)S(1)}, f32[2,2,8,128]{3,2,0,1:T(8,128)S(1)}, u32[]{:S(2)}, u32[]{:S(2)}) collective-permute-start(f32[2,2,8,128]{3,2,0,1:T(8,128)S(1)} %pad_maximum_fusion.2), channel_id=1, source_target_pairs={{8,16},{16,8},{24,0},{0,24},{9,17},{17,9},{25,1},{1,25},{10,18},{1... | collective-permute-start | bytes 49160 | tf_op jit(solution)/shard_map/ppermute | solution.py:33
  10.3 2.8 %collective-permute-start.1 = (f32[2,2,8,128]{3,2,0,1:T(8,128)S(1)}, f32[2,2,8,128]{3,2,0,1:T(8,128)S(1)}, u32[]{:S(2)}, u32[]{:S(2)}) collective-permute-start(f32[2,2,8,128]{3,2,0,1:T(8,128)S(1)} %pad_maximum_fusion.2), channel_id=1, source_target_pairs={{0,8},{8,0},{16,24},{24,16},{1,9},{9,1},{17,25},{25,17},{2,10},{10... | collective-permute-start | bytes 49160 | tf_op jit(solution)/shard_map/ppermute | solution.py:33
  13.1 14.3 %collective-permute-start.4 = (f32[6,8,128]{2,1,0:T(8,128)S(1)}, f32[6,8,128]{2,1,0:T(8,128)S(1)}, u32[]{:S(2)}, u32[]{:S(2)}) collective-permute-start(f32[6,8,128]{2,1,0:T(8,128)S(1)} %get-tuple-element.38), channel_id=1, source_target_pairs={{1,2},{2,1},{3,0},{0,3},{5,6},{6,5},{7,4},{4,7},{9,10},{10,9},{11,... | collective-permute-start | bytes 73736 | tf_op jit(solution)/shard_map/ppermute | solution.py:33
  17.4 10.0 %collective-permute-start.3 = (f32[6,8,128]{2,1,0:T(8,128)S(1)}, f32[6,8,128]{2,1,0:T(8,128)S(1)}, u32[]{:S(2)}, u32[]{:S(2)}) collective-permute-start(f32[6,8,128]{2,1,0:T(8,128)S(1)} %get-tuple-element.39), channel_id=1, source_target_pairs={{0,1},{1,0},{2,3},{3,2},{4,5},{5,4},{6,7},{7,6},{8,9},{9,8},{10,11... | collective-permute-start | bytes 73736 | tf_op jit(solution)/shard_map/ppermute | solution.py:33
  27.4 0.7 %copy-start = (f32[1,1,2,128]{3,2,1,0:T(2,128)S(1)}, f32[1,1,2,128]{3,2,1,0:T(2,128)}, u32[]{:S(2)}) copy-start(f32[1,1,2,128]{3,2,1,0:T(2,128)} %refs_5_.1) | copy-start | bytes 3076
  32.3 3.7 %collective-permute-start.5 = (f32[2,8,128]{2,1,0:T(8,128)S(1)}, f32[2,8,128]{2,1,0:T(8,128)S(1)}, u32[]{:S(2)}, u32[]{:S(2)}) collective-permute-start(f32[2,8,128]{2,1,0:T(8,128)S(1)} %get-tuple-element.21.refs_1_), channel_id=1, source_target_pairs={{0,4},{4,0},{1,5},{5,1},{2,6},{6,2},{3,7},{7,3},{8,12},{12,8},{9,1... | collective-permute-start | bytes 24584 | tf_op jit(solution)/shard_map/ppermute | solution.py:33
  36.0 3.3 %collective-permute-start.7 = (f32[2,2,8,128]{3,2,0,1:T(8,128)S(1)}, f32[2,2,8,128]{3,2,0,1:T(8,128)S(1)}, u32[]{:S(2)}, u32[]{:S(2)}) collective-permute-start(f32[2,2,8,128]{3,2,0,1:T(8,128)S(1)} %pad_maximum_fusion.3), channel_id=1, source_target_pairs={{8,16},{16,8},{24,0},{0,24},{9,17},{17,9},{25,1},{1,25},{10,18},{1... | collective-permute-start | bytes 49160 | tf_op jit(solution)/shard_map/ppermute | solution.py:33
  36.0 3.3 %collective-permute-start.6 = (f32[2,2,8,128]{3,2,0,1:T(8,128)S(1)}, f32[2,2,8,128]{3,2,0,1:T(8,128)S(1)}, u32[]{:S(2)}, u32[]{:S(2)}) collective-permute-start(f32[2,2,8,128]{3,2,0,1:T(8,128)S(1)} %pad_maximum_fusion.3), channel_id=1, source_target_pairs={{0,8},{8,0},{16,24},{24,16},{1,9},{9,1},{17,25},{25,17},{2,10},{10... | collective-permute-start | bytes 49160 | tf_op jit(solution)/shard_map/ppermute | solution.py:33
  39.4 9.9 %collective-permute-start.9 = (f32[6,8,128]{2,1,0:T(8,128)S(1)}, f32[6,8,128]{2,1,0:T(8,128)S(1)}, u32[]{:S(2)}, u32[]{:S(2)}) collective-permute-start(f32[6,8,128]{2,1,0:T(8,128)S(1)} %get-tuple-element.36), channel_id=1, source_target_pairs={{1,2},{2,1},{3,0},{0,3},{5,6},{6,5},{7,4},{4,7},{9,10},{10,9},{11,... | collective-permute-start | bytes 73736 | tf_op jit(solution)/shard_map/ppermute | solution.py:33
  40.3 8.9 %collective-permute-start.8 = (f32[6,8,128]{2,1,0:T(8,128)S(1)}, f32[6,8,128]{2,1,0:T(8,128)S(1)}, u32[]{:S(2)}, u32[]{:S(2)}) collective-permute-start(f32[6,8,128]{2,1,0:T(8,128)S(1)} %get-tuple-element.37), channel_id=1, source_target_pairs={{0,1},{1,0},{2,3},{3,2},{4,5},{5,4},{6,7},{7,6},{8,9},{9,8},{10,11... | collective-permute-start | bytes 73736 | tf_op jit(solution)/shard_map/ppermute | solution.py:33

commit v2 on v1

v2 whole, which is shorter than its diff:
```python
import functools
import math

import jax
import jax.numpy as jnp
from jax import lax
from jax.experimental import pallas as pl
from jax.experimental.pallas import tpu as pltpu
from jax.sharding import PartitionSpec as P

kernel_norm = 21.0 / (16.0 * math.pi)
pressure_factor = 2.0 / 3.0
ridge_factor = 0.1
pair_scale = -160.0 * kernel_norm

LIMIT = 16 * 1024 * 1024
AXES = ("gx", "gy", "gz")
X, Y, Z, H, V, M, FLAGS = range(7)
PR, CA, CX, CY, CZ, VX, VY, VZ = range(8)


def code_of(step):
    index = (step[0] + 1) * 9 + (step[1] + 1) * 3 + step[2] + 1
    return index if index < 13 else index - 1


def swap(array, axis, phase):
    count = lax.axis_size(axis)
    pairs = []
    for first in range(phase, count, 2):
        second = (first + 1) % count
        pairs += [(first, second), (second, first)]
    return lax.ppermute(array, axis, pairs)


def swaps(array, axis):
    count = lax.axis_size(axis)
    if count == 2:
        return [swap(array, axis, 0)]
    return [swap(array, axis, 1), swap(array, axis, 0)][::-1]


def beside(get, step, axis):
    if step == 0:
        return get(0)
    if lax.axis_size(axis) == 2:
        return get(1)
    even = lax.axis_index(axis) % 2 == 0
    first, second = (1, 2) if step == 1 else (2, 1)
    return jnp.where(even, get(first), get(second))


def split(values, parts):
    pieces = []
    for _ in range(parts - 1):
        piece = values.astype(jnp.bfloat16).astype(jnp.float32)
        pieces.append(piece)
        values = values - piece
    return pieces + [values]


def stacked(parts):
    return jnp.concatenate(parts, axis=0).astype(jnp.bfloat16)


def left_form(features):
    high, middle, low = split(features, 3)
    return stacked([high, high, middle, high, low, middle]).T


def right_form(features):
    high, middle, low = split(features, 3)
    return stacked([high, middle, high, low, high, middle])


def pair_matrix(features):
    return jnp.concatenate(split(features, 2), axis=0).astype(jnp.bfloat16)


def feature_rows(features):
    rows = stacked(split(features, 3))
    return jnp.concatenate([rows, rows], axis=1)


def dot(left, right):
    return jnp.dot(left, right, preferred_element_type=jnp.float32)


def rows_of(tile, first, count=1):
    return [tile[k : k + 1] for k in range(first, first + count)]


def block_list(stage, leaves):
    blocks = []
    for dx in (-1, 0, 1):
        for dy in (-1, 0, 1):
            for leaf in range(leaves):
                for dz in (-1, 0, 1):
                    level = leaf + dz
                    if level < 0 or level >= leaves:
                        kind = "z"
                    elif dx:
                        kind = "x"
                    elif dy:
                        kind = "y"
                    else:
                        kind = "own"
                    if kind == stage:
                        blocks.append((leaf, (dx, dy, dz)))
    return blocks


def tile_at(refs, stage, dx, dy, level, leaves):
    def along_x(kx):
        def along_y(ky):
            if stage == "own":
                return refs[0][level]
            if stage == "y":
                return refs[ky - 1][level]
            if stage == "x":
                return refs[kx - 1][ky, level]
            ny = 1 if lax.axis_size("gy") == 2 else 2
            column = kx * (1 + ny) + ky
            even = lax.axis_index("gz") % 2 == 0
            above = level >= leaves
            return jnp.where(
                even, refs[0 if above else 1][column], refs[1 if above else 0][column]
            )

        return beside(along_y, dy, "gy")

    return beside(along_x, dx, "gx")


def tile_key(dx, dy, level):
    if lax.axis_size("gx") == 2:
        dx = abs(dx)
    if lax.axis_size("gy") == 2:
        dy = abs(dy)
    return (dx, dy, level)


def plan(stage, leaves):
    groups = {}
    for number, (leaf, step) in enumerate(block_list(stage, leaves)):
        key = tile_key(step[0], step[1], leaf + step[2])
        groups.setdefault(key, []).append((number, leaf, step))
    return list(groups.items())


def level_centre(level, leaves):
    return float(level) - 0.5 * (leaves - 1)


def pair_weight(own_tile, tile, step):
    if step == (0, 0, 0):
        return None
    code = code_of(step)
    weight = own_tile[FLAGS : FLAGS + 1, code : code + 1] + tile[FLAGS : FLAGS + 1, 25 - code : 26 - code]
    return jnp.broadcast_to(weight, (48, tile.shape[1]))


def add_weighted(acc, leaf, sums, weight):
    acc[leaf] = acc[leaf] + (sums if weight is None else sums * weight)


def place_rows(tile, dx, dy, level, leaves):
    centre = (float(dx), float(dy), level_centre(level, leaves))
    return [row + (part - 0.5) for row, part in zip(rows_of(tile, X, 3), centre)]


def moment_features(tile, dx, dy, level, leaves):
    x, y, z = place_rows(tile, dx, dy, level, leaves)
    (v, m) = rows_of(tile, V, 2)
    vx, vy, vz = v * x, v * y, v * z
    rows = [v, vx, vy, vz, vx * x, vx * y, vx * z, vy * y, vy * z, vz * z, m]
    return feature_rows(jnp.concatenate(rows + [jnp.zeros_like(v)] * 5, axis=0))


def moment_body(stage, leaves, per_leaf, own, sources, acc, w_out, g_out):
    one = jnp.ones((1, per_leaf), jnp.float32)
    zero = jnp.zeros((1, per_leaf), jnp.float32)
    number = 0
    widths = {}
    for leaf in range(leaves):
        smooth = rows_of(own[leaf], H)[0]
        widths[leaf] = right_form(
            jnp.concatenate([zero, smooth, zero, zero, zero, one, zero, zero], axis=0)
        )
    for (dx, dy, level), blocks in plan(stage, leaves):
        tile = tile_at(sources, stage, dx, dy, level, leaves)
        xj, yj, zj = [row - 0.5 for row in rows_of(tile, X, 3)]
        near = xj * xj + yj * yj + zj * zj
        left = left_form(
            jnp.concatenate([near, one, xj, yj, zj, tile[H : H + 1], zero, zero], axis=0)
        )
        inverses = {}
        features = {}
        for number, leaf, step in blocks:
            if leaf not in inverses:
                inverses[leaf] = 1.0 / dot(left, widths[leaf])
            if step[:2] not in features:
                features[step[:2]] = moment_features(tile, step[0], step[1], level, leaves)
            xi, yi, zi = [
                row - (0.5 + shift) for row, shift in zip(rows_of(own[leaf], X, 3), step)
            ]
            far = xi * xi + yi * yi + zi * zi
            right = right_form(
                jnp.concatenate(
                    [one, far, -2.0 * xi, -2.0 * yi, -2.0 * zi, zero, zero, zero], axis=0
                )
            )
            inverse = inverses[leaf]
            inverse_sq = inverse * inverse
            dist_sq = jnp.maximum(dot(left, right), 1e-30)
            dist = dist_sq * lax.rsqrt(dist_sq)
            remain = jnp.maximum(1.0 - dist * inverse, 0.0)
            edge = (inverse_sq * inverse) * (remain * remain * remain)
            pair_w = pair_matrix(edge * (remain * (0.2 * remain - 0.25)))
            w_out[number] = pair_w
            g_out[number] = edge * inverse_sq
            weight = pair_weight(own[leaf], tile, step)
            add_weighted(acc, leaf, dot(features[step[:2]], pair_w), weight)


def moment_kernel(stage, leaves, per_leaf, count, *refs):
    own = refs[0]
    sources = refs[1 : 1 + count] if count else (own,)
    rest = refs[1 + count :]
    if stage == "own":
        acc, w_out, g_out = rest
        acc[...] = jnp.zeros_like(acc)
    else:
        acc_in, acc, w_out, g_out = rest
        acc[...] = acc_in[...]
    moment_body(stage, leaves, per_leaf, own, sources, acc, w_out, g_out)


def corrections(moments, smooth, energy):
    density, zeroth, first_x, first_y, first_z, s_xx, s_xy, s_xz, s_yy, s_yz, s_zz = moments
    ridge_term = ridge_factor * smooth * smooth * zeroth
    s_xx = s_xx + ridge_term
    s_yy = s_yy + ridge_term
    s_zz = s_zz + ridge_term
    c_xx = s_yy * s_zz - s_yz * s_yz
    c_xy = s_yz * s_xz - s_xy * s_zz
    c_xz = s_xy * s_yz - s_yy * s_xz
    c_yy = s_xx * s_zz - s_xz * s_xz
    c_yz = s_xy * s_xz - s_xx * s_yz
    c_zz = s_xx * s_yy - s_xy * s_xy
    determinant = s_xx * c_xx + s_xy * c_xy + s_xz * c_xz
    solve_x = (c_xx * first_x + c_xy * first_y + c_xz * first_z) / determinant
    solve_y = (c_xy * first_x + c_yy * first_y + c_yz * first_z) / determinant
    solve_z = (c_xz * first_x + c_yz * first_y + c_zz * first_z) / determinant
    coef_a = 1.0 / (zeroth - (first_x * solve_x + first_y * solve_y + first_z * solve_z))
    pressure = pressure_factor * density * energy
    return [pressure, coef_a, -coef_a * solve_x, -coef_a * solve_y, -coef_a * solve_z]

def gathered(acc, leaf):
    sums = acc[leaf]
    return sums[0:16] + (sums[16:32] + sums[32:48])


def field_kernel(leaves, per_leaf, count, *refs):
    own = refs[0]
    sources = refs[1 : 1 + count]
    acc_in, extra, fields_out, w_out, g_out, acc = refs[1 + count :]
    acc[...] = acc_in[...]
    moment_body("z", leaves, per_leaf, own, sources, acc, w_out, g_out)
    columns = []
    for leaf in range(leaves):
        sums = gathered(acc, leaf)
        zeroth, fx, fy, fz, sxx, sxy, sxz, syy, syz, szz, density = rows_of(sums, 0, 11)
        x, y, z = place_rows(own[leaf], 0, 0, leaf, leaves)
        mx, my, mz = x * zeroth - fx, y * zeroth - fy, z * zeroth - fz
        columns.append(
            [
                density,
                zeroth,
                mx,
                my,
                mz,
                x * mx - x * fx + sxx,
                x * my - y * fx + sxy,
                x * mz - z * fx + sxz,
                y * my - y * fy + syy,
                y * mz - z * fy + syz,
                z * mz - z * fz + szz,
                own[leaf][H : H + 1],
                extra[leaf][3:4],
            ]
        )
    rows = [jnp.concatenate(parts, axis=0) for parts in zip(*columns)]
    fields = corrections(rows[:11], rows[11], rows[12])
    for leaf in range(leaves):
        for k, value in enumerate(fields):
            fields_out[leaf, k : k + 1, :] = value[leaf : leaf + 1]
        fields_out[leaf, VX : VZ + 1, :] = extra[leaf][0:3]


def force_body(stage, leaves, per_leaf, own, fields, sources, places, accs, w_in, g_in):
    one = jnp.ones((1, per_leaf), jnp.float32)
    acc_w, acc_g = accs
    for (dx, dy, level), blocks in plan(stage, leaves):
        tile = tile_at(places, stage, dx, dy, level, leaves)
        field = tile_at(sources, stage, dx, dy, level, leaves)
        xj, yj, zj = [row - 0.5 for row in rows_of(tile, X, 3)]
        pressure, coef, cx, cy, cz, vx, vy, vz = rows_of(field, 0, 8)
        volume = tile[V : V + 1]
        left = left_form(
            jnp.concatenate(
                [one, coef + (cx * xj + cy * yj + cz * zj), xj, yj, zj, cx, cy, cz], axis=0
            )
        )

        def weighted(a, b, c):
            first = volume * jnp.concatenate(
                [one, a, b, c, vx, vy, vz, a * vx + b * vy + c * vz], axis=0
            )
            return feature_rows(jnp.concatenate([first, pressure * first], axis=0))

        with_w = weighted(cx, cy, cz)
        with_g = {}
        for number, leaf, step in blocks:
            if step[:2] not in with_g:
                with_g[step[:2]] = weighted(*place_rows(tile, step[0], step[1], level, leaves))
            xi, yi, zi = [
                row - (0.5 + shift) for row, shift in zip(rows_of(own[leaf], X, 3), step)
            ]
            _, coef_i, cxi, cyi, czi = rows_of(fields[leaf], 0, 5)
            right = right_form(
                jnp.concatenate(
                    [coef_i + (cxi * xi + cyi * yi + czi * zi), one]
                    + [-cxi, -cyi, -czi, -xi, -yi, -zi],
                    axis=0,
                )
            )
            radial = pair_matrix(g_in[number] * dot(left, right))
            weight = pair_weight(own[leaf], tile, step)
            add_weighted(acc_w, leaf, dot(with_w, w_in[number]), weight)
            add_weighted(acc_g, leaf, dot(with_g[step[:2]], radial), weight)


def force_setup(stage, count, refs):
    own, fields = refs[0], refs[1]
    sources = refs[2 : 2 + count] if count else (fields,)
    places = refs[2 + count : 2 + 2 * count] if count else (own,)
    return own, fields, sources, places, refs[2 + 2 * count :]


def force_kernel(stage, leaves, per_leaf, count, *refs):
    own, fields, sources, places, rest = force_setup(stage, count, refs)
    if stage == "own":
        w_in, g_in, acc_w, acc_g = rest
        acc_w[...] = jnp.zeros_like(acc_w)
        acc_g[...] = jnp.zeros_like(acc_g)
    else:
        w_before, g_before, w_in, g_in, acc_w, acc_g = rest
        acc_w[...] = w_before[...]
        acc_g[...] = g_before[...]
    force_body(
        stage, leaves, per_leaf, own, fields, sources, places, (acc_w, acc_g), w_in, g_in
    )


def finish_kernel(leaves, per_leaf, count, *refs):
    own, fields, sources, places, rest = force_setup("z", count, refs)
    w_before, g_before, w_in, g_in, acceleration, heating, acc_w, acc_g = rest
    acc_w[...] = w_before[...]
    acc_g[...] = g_before[...]
    force_body(
        "z", leaves, per_leaf, own, fields, sources, places, (acc_w, acc_g), w_in, g_in
    )
    for leaf in range(leaves):
        tile = own[leaf]
        pressure, _, cx, cy, cz, vx, vy, vz = rows_of(fields[leaf], 0, 8)
        sums_w, sums_g = gathered(acc_w, leaf), gathered(acc_g, leaf)
        both_w = pressure * sums_w[0:8] + sums_w[8:16]
        both_g = pressure * sums_g[0:8] + sums_g[8:16]
        w_rows, g_rows = rows_of(both_w, 0, 8), rows_of(both_g, 0, 8)
        coefs = (cx, cy, cz)
        spots = place_rows(tile, 0, 0, leaf, leaves)
        ratio = tile[V : V + 1] / tile[M : M + 1]
        work = w_rows[7] + g_rows[7]
        for k, (coef, spot, speed) in enumerate(zip(coefs, spots, (vx, vy, vz))):
            force = (coef * w_rows[0] - w_rows[1 + k]) + (spot * g_rows[0] - g_rows[1 + k])
            work = work + speed * force - coef * w_rows[4 + k] - spot * g_rows[4 + k]
            acceleration[0, 0, k, leaf : leaf + 1, :] = (-0.5 * ratio) * force
        heating[0, 0, leaf : leaf + 1, :] = (0.25 * ratio) * work


def pack_kernel(leaves, per_leaf, *refs):
    inputs = refs[:6]
    neighbours, counts = refs[6:8]
    out, extra = refs[8:10]
    held = refs[10:16]
    sems = refs[16]
    copies = [
        pltpu.make_async_copy(source, target, sems.at[k])
        for k, (source, target) in enumerate(zip(inputs, held))
    ]
    for copy in copies:
        copy.start()
    lane = lax.broadcasted_iota(jnp.int32, (1, per_leaf), 1)
    for leaf in range(leaves):
        flags = jnp.zeros((1, per_leaf), jnp.float32)
        for slot in range(neighbours.shape[3]):
            code = jnp.where(slot < counts[0, 0, leaf], neighbours[0, 0, leaf, slot], -1)
            flags = flags + jnp.where(lane == code, 1.0, 0.0)
        out[leaf, FLAGS : FLAGS + 1, :] = flags
        out[leaf, FLAGS + 1 : FLAGS + 2, :] = jnp.zeros((1, per_leaf), jnp.float32)
        extra[leaf, 4:8, :] = jnp.zeros((4, per_leaf), jnp.float32)
    for copy in copies:
        copy.wait()
    offsets, velocity, masses, volumes, energies, smoothing = held
    for leaf in range(leaves):
        one = slice(leaf, leaf + 1)
        for part in range(3):
            out[leaf, part : part + 1, :] = offsets[0, 0, part, one]
            extra[leaf, part : part + 1, :] = velocity[0, 0, part, one]
        out[leaf, H : H + 1, :] = smoothing[0, 0, one]
        out[leaf, V : V + 1, :] = pair_scale * volumes[0, 0, one]
        out[leaf, M : M + 1, :] = pair_scale * masses[0, 0, one]
        extra[leaf, 3:4, :] = energies[0, 0, one]


def per_device(offsets, velocity, masses, volumes, energies, smoothing, neighbours, counts):
    leaves, per_leaf = masses.shape[2], masses.shape[3]
    f32, bf16 = jnp.float32, jnp.bfloat16
    vmem = pl.BlockSpec(memory_space=pltpu.VMEM)
    smem = pl.BlockSpec(memory_space=pltpu.SMEM)
    anywhere = pl.BlockSpec(memory_space=pl.ANY)
    params = pltpu.CompilerParams(vmem_limit_bytes=LIMIT)
    parity = lax.axis_index("gz") % 2 == 0
    offsets = jnp.swapaxes(offsets, 2, 3)
    velocity = jnp.swapaxes(velocity, 2, 3)

    def cost(blocks, ops):
        return pl.CostEstimate(
            flops=blocks * per_leaf * per_leaf * ops, bytes_accessed=blocks * 4096, transcendentals=0
        )

    inputs = (offsets, velocity, masses, volumes, energies, smoothing)
    own, extra = pl.pallas_call(
        functools.partial(pack_kernel, leaves, per_leaf),
        out_shape=[jax.ShapeDtypeStruct((leaves, 8, per_leaf), f32)] * 2,
        in_specs=[anywhere] * 6 + [smem] * 2,
        out_specs=[vmem] * 2,
        scratch_shapes=[pltpu.VMEM(array.shape, f32) for array in inputs]
        + [pltpu.SemaphoreType.DMA((6,))],
        compiler_params=params,
        name="pack",
    )(*inputs, neighbours, counts)

    def exchange_y(tile):
        return swaps(tile, "gy")

    def exchange_x(tile, from_y):
        return swaps(jnp.stack([tile] + from_y, axis=0), "gx")

    def exchange_z(tile, from_y, from_x):
        column = jnp.concatenate([jnp.stack([tile] + from_y, axis=0)] + from_x, axis=0)
        bottom, top = column[:, 0], column[:, leaves - 1]
        far = swap(jnp.where(parity, bottom, top), "gz", 1)
        near = swap(jnp.where(parity, top, bottom), "gz", 0)
        return [near, far]

    stages = ("own", "y", "x", "z")
    sizes = {stage: len(block_list(stage, leaves)) for stage in stages}
    acc_shape = jax.ShapeDtypeStruct((leaves, 48, per_leaf), f32)
    acc_scratch = pltpu.VMEM((leaves, 48, per_leaf), f32)

    def moment_call(stage, sources, acc):
        size = sizes[stage]
        kept = [
            jax.ShapeDtypeStruct((size, 2 * per_leaf, per_leaf), bf16),
            jax.ShapeDtypeStruct((size, per_leaf, per_leaf), f32),
        ]
        operands = [own] + list(sources) + ([] if acc is None else [acc])
        scratch = []
        if stage == "z":
            body = functools.partial(field_kernel, leaves, per_leaf, len(sources))
            operands += [extra]
            first = jax.ShapeDtypeStruct((leaves, 8, per_leaf), f32)
            scratch = [acc_scratch]
        else:
            body = functools.partial(moment_kernel, stage, leaves, per_leaf, len(sources))
            first = acc_shape
        return pl.pallas_call(
            body,
            out_shape=[first] + kept,
            in_specs=[vmem] * len(operands),
            out_specs=[vmem] * 3,
            scratch_shapes=scratch,
            compiler_params=params,
            cost_estimate=cost(size, 55),
            name="moments_" + stage,
        )(*operands)

    def force_call(stage, sources, places, accs, kept, fields):
        size = sizes[stage]
        operands = [own, fields] + list(sources) + list(places) + list(accs) + list(kept)
        scratch = []
        if stage == "z":
            body = functools.partial(finish_kernel, leaves, per_leaf, len(sources))
            out = [
                jax.ShapeDtypeStruct((1, 1, 3, leaves, per_leaf), f32),
                jax.ShapeDtypeStruct((1, 1, leaves, per_leaf), f32),
            ]
            scratch = [acc_scratch] * 2
        else:
            body = functools.partial(force_kernel, stage, leaves, per_leaf, len(sources))
            out = [acc_shape] * 2
        return pl.pallas_call(
            body,
            out_shape=out,
            in_specs=[vmem] * len(operands),
            out_specs=[vmem] * len(out),
            scratch_shapes=scratch,
            compiler_params=params,
            cost_estimate=cost(size, 36),
            name="force_" + stage,
        )(*operands)

    from_y = exchange_y(own)
    acc, *kept_own = moment_call("own", [], None)
    from_x = exchange_x(own, from_y)
    acc, *kept_y = moment_call("y", from_y, acc)
    from_z = exchange_z(own, from_y, from_x)
    acc, *kept_x = moment_call("x", from_x, acc)
    fields, *kept_z = moment_call("z", from_z, acc)

    field_y = exchange_y(fields)
    accs = force_call("own", [], [], [], kept_own, fields)
    field_x = exchange_x(fields, field_y)
    accs = force_call("y", field_y, from_y, accs, kept_y, fields)
    field_z = exchange_z(fields, field_y, field_x)
    accs = force_call("x", field_x, from_x, accs, kept_x, fields)
    acceleration, heating = force_call("z", field_z, from_z, accs, kept_z, fields)
    return (jnp.swapaxes(acceleration, 2, 3), heating)


def solution(mesh):
    in_specs = (
        P("gx", "gy", "gz", None, None),
        P("gx", "gy", "gz", None, None),
        P("gx", "gy", "gz", None),
        P("gx", "gy", "gz", None),
        P("gx", "gy", "gz", None),
        P("gx", "gy", "gz", None),
        P("gx", "gy", "gz", None),
        P("gx", "gy", "gz"),
    )
    out_specs = (P("gx", "gy", "gz", None, None), P("gx", "gy", "gz", None))
    return jax.shard_map(
        per_device, mesh=mesh, in_specs=in_specs, out_specs=out_specs, check_vma=False
    )
```

time: 55.7 us -> 43.1 us (0.77)
  Pallas kernels: 27.2 us -> 15.2 us
  local copies, waits for them, and re-layouts: 6.01 us -> 5.42 us
    pallas_call x4, Pallas kernels: 13.2 us -> 6.47 us  [force_call(): pl.pallas_call(body, out_shape=out, in_specs=[vmem] * len(operands), out_...]
    pallas_call x4, Pallas kernels: 13.4 us -> 8.12 us  [moment_call(): pl.pallas_call(body, out_shape=[first] + kept, in_specs=[vmem] * len(oper...]
    pallas_call x1 -> x0, local copies, waits for them, and re-layouts: 0.58 us -> none  [force_call(): pl.pallas_call(body, out_shape=out, in_specs=[vmem] * len(operands), out_...]
    unnamed x14 -> x16, local copies, waits for them, and re-layouts: 5.42 us -> 5.41 us
  transfers between devices with their start and end apart: 10 -> 10, of which waited for: 4 -> 4; matrix products, arithmetic and copies ran while one was open for 1% -> 0% of each run, Pallas kernels for 30% -> 22%
where the time goes in v2:
time: 43.1 us; the launch traced here: 42.8 us
  Pallas kernels  15.2 us (35%)
  starting transfers between devices  14.7 us (34%)
  waiting for transfers between devices  6.58 us (15%)
  local copies, waits for them, and re-layouts  5.42 us (13%)
  between operations  0.79 us (2%)
    ppermute x10, starting transfers between devices, swap(): return lax.ppermute(array, axis, pairs)  14.7 us
    pallas_call x4, Pallas kernels, moment_call(): pl.pallas_call(body, out_shape=[first] + kept, in_specs=[vmem] * len(oper...  8.12 us
    ppermute x10, waiting for transfers between devices, swap(): return lax.ppermute(array, axis, pairs)  6.58 us
    pallas_call x4, Pallas kernels, force_call(): pl.pallas_call(body, out_shape=out, in_specs=[vmem] * len(operands), out_...  6.47 us
    unnamed x16, local copies, waits for them, and re-layouts  5.41 us
  transfers between devices with their start and end apart: 10, of which 4 were waited for; matrix products, arithmetic and copies ran while one was open for 0% of the time, Pallas kernels for 22%

profile of v2, /device:TPU:0, one launch (start us, length us, event | category | flops | bytes accessed | tf_op | source)
XLA Modules:
  0.0 42.8 jit_solution(9316744099995887900)
XLA Ops:
  0.6 0.0 copy-start
  0.6 0.7 %copy-done = f32[1,1,2,3,128]{4,2,3,1,0:T(2,128)S(1)} copy-done((f32[1,1,2,3,128]{4,2,3,1,0:T(2,128)S(1)}, f32[1,1,2,3,128]{4,2,3,1,0:T(2,128)}, u32[]{:S(2)}) %copy-start) | copy-done | bytes 3096
  1.3 0.0 copy-start.1
  1.3 0.7 %copy-done.1 = f32[1,1,2,3,128]{4,2,3,1,0:T(2,128)S(1)} copy-done((f32[1,1,2,3,128]{4,2,3,1,0:T(2,128)S(1)}, f32[1,1,2,3,128]{4,2,3,1,0:T(2,128)}, u32[]{:S(2)}) %copy-start.1) | copy-done | bytes 3096
  2.0 0.0 copy-start.2
  2.0 0.7 %copy-done.2 = f32[1,1,2,128]{3,2,1,0:T(2,128)S(1)} copy-done((f32[1,1,2,128]{3,2,1,0:T(2,128)S(1)}, f32[1,1,2,128]{3,2,1,0:T(2,128)}, u32[]{:S(2)}) %copy-start.2) | copy-done | bytes 1048
  2.7 0.0 copy-start.3
  2.7 0.7 %copy-done.3 = f32[1,1,2,128]{3,2,1,0:T(2,128)S(1)} copy-done((f32[1,1,2,128]{3,2,1,0:T(2,128)S(1)}, f32[1,1,2,128]{3,2,1,0:T(2,128)}, u32[]{:S(2)}) %copy-start.3) | copy-done | bytes 1048
  3.4 0.0 copy-start.4
  3.4 0.7 %copy-done.4 = f32[1,1,2,128]{3,2,1,0:T(2,128)S(1)} copy-done((f32[1,1,2,128]{3,2,1,0:T(2,128)S(1)}, f32[1,1,2,128]{3,2,1,0:T(2,128)}, u32[]{:S(2)}) %copy-start.4) | copy-done | bytes 1048
  4.0 0.0 copy-start.5
  4.0 0.7 %copy-done.5 = f32[1,1,2,128]{3,2,1,0:T(2,128)S(1)} copy-done((f32[1,1,2,128]{3,2,1,0:T(2,128)S(1)}, f32[1,1,2,128]{3,2,1,0:T(2,128)}, u32[]{:S(2)}) %copy-start.5) | copy-done | bytes 1048
  4.7 0.0 copy-start.6
  4.7 0.7 %copy-done.6 = s32[1,1,2,13]{3,2,1,0:T(2,128)S(1)} copy-done((s32[1,1,2,13]{3,2,1,0:T(2,128)S(1)}, s32[1,1,2,13]{3,2,1,0:T(2,128)}, u32[]{:S(2)}) %copy-start.6) | copy-done | bytes 128
  5.4 0.0 copy-start.7
  5.4 0.7 %copy-done.7 = s32[1,1,2]{2,1,0:T(1,128)S(1)} copy-done((s32[1,1,2]{2,1,0:T(1,128)S(1)}, s32[1,1,2]{2,1,0:T(1,128)}, u32[]{:S(2)}) %copy-start.7) | copy-done | bytes 32
  6.1 0.7 %pack.1 = (f32[2,8,128]{2,1,0:T(8,128)S(1)}, f32[2,8,128]{2,1,0:T(8,128)S(1)}) custom-call(f32[1,1,3,2,128]{4,3,2,1,0:T(2,128)S(1)} %bitcast.23, f32[1,1,3,2,128]{4,3,2,1,0:T(2,128)S(1)} %bitcast.24, f32[1,1,2,128]{3,2,1,0:T(2,128)S(1)} %copy-done.2, f32[1,1,2,128]{3,2,1,0:T(2,128)S(1)} %copy-done.3, f32[1,1,2,128]{3,2,1,0:T(2,128)S(1)} %copy-done.4, ...), custom_call_target="tpu_custom_call" | custom-call | tf_op jit(solution)/shard_map/pack/pallas_call | solution.py:444
  6.7 3.0 %collective-permute-start = (f32[2,8,128]{2,1,0:T(8,128)S(1)}, f32[2,8,128]{2,1,0:T(8,128)S(1)}, u32[]{:S(2)}, u32[]{:S(2)}) collective-permute-start(f32[2,8,128]{2,1,0:T(8,128)S(1)} %get-tuple-element.24.refs_0_), channel_id=1, source_target_pairs={{0,4},{4,0},{1,5},{5,1},{2,6},{6,2},{3,7},{7,3},{8,12},{12,8},{9,1... | collective-permute-start | bytes 24584 | tf_op jit(solution)/shard_map/ppermute | solution.py:33
  9.8 1.6 %collective-permute-done.refs_1_.refs_3_ = f32[2,8,128]{2,1,0:T(8,128)S(1)} collective-permute-done((f32[2,8,128]{2,1,0:T(8,128)S(1)}, f32[2,8,128]{2,1,0:T(8,128)S(1)}, u32[]{:S(2)}, u32[]{:S(2)}) %collective-permute-start) | collective-permute-done | bytes 8224 | tf_op jit(solution)/shard_map/ppermute | solution.py:33
  11.4 0.3 collective-permute-start.2
  11.7 1.8 %collective-permute-start.1 = (f32[2,2,8,128]{3,2,0,1:T(8,128)S(1)}, f32[2,2,8,128]{3,2,0,1:T(8,128)S(1)}, u32[]{:S(2)}, u32[]{:S(2)}) collective-permute-start(f32[2,2,8,128]{3,2,0,1:T(8,128)S(1)} %pad_maximum_fusion.2), channel_id=1, source_target_pairs={{0,8},{8,0},{16,24},{24,16},{1,9},{9,1},{17,25},{25,17},{2,10},{10... | collective-permute-start | bytes 49160 | tf_op jit(solution)/shard_map/ppermute | solution.py:33
  13.6 1.0 %collective-permute-done.2 = f32[2,2,8,128]{3,2,0,1:T(8,128)S(1)} collective-permute-done((f32[2,2,8,128]{3,2,0,1:T(8,128)S(1)}, f32[2,2,8,128]{3,2,0,1:T(8,128)S(1)}, u32[]{:S(2)}, u32[]{:S(2)}) %collective-permute-start.2) | collective-permute-done | bytes 16416 | tf_op jit(solution)/shard_map/ppermute | solution.py:33
  14.6 0.0 collective-permute-done.1
  14.6 4.3 %collective-permute-start.4 = (f32[6,8,128]{2,1,0:T(8,128)S(1)}, f32[6,8,128]{2,1,0:T(8,128)S(1)}, u32[]{:S(2)}, u32[]{:S(2)}) collective-permute-start(f32[6,8,128]{2,1,0:T(8,128)S(1)} %get-tuple-element.48), channel_id=1, source_target_pairs={{1,2},{2,1},{3,0},{0,3},{5,6},{6,5},{7,4},{4,7},{9,10},{10,9},{11,... | collective-permute-start | bytes 73736 | tf_op jit(solution)/shard_map/ppermute | solution.py:33
  18.9 0.0 collective-permute-start.3
  18.9 0.9 %moments_own.1 = (f32[2,48,128]{2,1,0:T(8,128)S(1)}, bf16[4,256,128]{2,1,0:T(8,128)(2,1)S(1)}, f32[4,128,128]{2,1,0:T(8,128)S(1)}) custom-call(f32[2,8,128]{2,1,0:T(8,128)S(1)} %get-tuple-element.24.refs_0_), custom_call_target="tpu_custom_call" | custom-call | flops 3604480 | bytes 16384 | tf_op jit(solution)/shard_map/moments_own/pallas_call | solution.py:489
  19.8 1.1 %moments_y.1 = (f32[2,48,128]{2,1,0:T(8,128)S(1)}, bf16[8,256,128]{2,1,0:T(8,128)(2,1)S(1)}, f32[8,128,128]{2,1,0:T(8,128)S(1)}) custom-call(f32[2,8,128]{2,1,0:T(8,128)S(1)} %get-tuple-element.24.refs_0_, f32[2,8,128]{2,1,0:T(8,128)S(1)} %collective-permute-done.refs_1_.refs_3_, f32[2,48,128]{2,1,0:T(8,128)S(1)} %get-tuple-element.25.refs_2_), custom_call_target="tpu_custom_call" | custom-call | flops 7208960 | bytes 32768 | tf_op jit(solution)/shard_map/moments_y/pallas_call | solution.py:489
  20.9 3.5 %moments_x.1 = (f32[2,48,128]{2,1,0:T(8,128)S(1)}, bf16[24,256,128]{2,1,0:T(8,128)(2,1)S(1)}, f32[24,128,128]{2,1,0:T(8,128)S(1)}) custom-call(f32[2,8,128]{2,1,0:T(8,128)S(1)} %get-tuple-element.24.refs_0_, f32[2,2,8,128]{3,2,1,0:T(8,128)S(1)} %copy.10.refs_1_.refs_4_, f32[2,2,8,128]{3,2,1,0:T(8,128)S(1)} %copy.11.refs_2_.refs_5_, ...), custom_call_target="tpu_custom_call" | custom-call | flops 21626880 | bytes 98304 | tf_op jit(solution)/shard_map/moments_x/pallas_call | solution.py:489
  24.4 0.0 collective-permute-done.4.refs_2_.refs_5_
  24.4 0.0 collective-permute-done.3.refs_1_.refs_4_
  24.4 2.7 %moments_z.1 = (f32[2,8,128]{2,1,0:T(8,128)S(1)}, bf16[18,256,128]{2,1,0:T(8,128)(2,1)S(1)}, f32[18,128,128]{2,1,0:T(8,128)S(1)}) custom-call(f32[2,8,128]{2,1,0:T(8,128)S(1)} %get-tuple-element.24.refs_0_, f32[6,8,128]{2,1,0:T(8,128)S(1)} %collective-permute-done.3.refs_1_.refs_4_, f32[6,8,128]{2,1,0:T(8,128)S(1)} %collective-permute-done.4.refs_2_.refs_5_, ...), custom_call_target="tpu_custom_call" | custom-call | flops 16220160 | bytes 73728 | tf_op jit(solution)/shard_map/moments_z/pallas_call | solution.py:489
  27.1 1.6 %collective-permute-start.5 = (f32[2,8,128]{2,1,0:T(8,128)S(1)}, f32[2,8,128]{2,1,0:T(8,128)S(1)}, u32[]{:S(2)}, u32[]{:S(2)}) collective-permute-start(f32[2,8,128]{2,1,0:T(8,128)S(1)} %get-tuple-element.29.refs_1_), channel_id=1, source_target_pairs={{0,4},{4,0},{1,5},{5,1},{2,6},{6,2},{3,7},{7,3},{8,12},{12,8},{9,1... | collective-permute-start | bytes 24584 | tf_op jit(solution)/shard_map/ppermute | solution.py:33
  28.6 2.2 %collective-permute-done.5.refs_2_ = f32[2,8,128]{2,1,0:T(8,128)S(1)} collective-permute-done((f32[2,8,128]{2,1,0:T(8,128)S(1)}, f32[2,8,128]{2,1,0:T(8,128)S(1)}, u32[]{:S(2)}, u32[]{:S(2)}) %collective-permute-start.5) | collective-permute-done | bytes 8224 | tf_op jit(solution)/shard_map/ppermute | solution.py:33
  30.8 0.0 collective-permute-start.7
  30.8 1.5 %collective-permute-start.6 = (f32[2,2,8,128]{3,2,0,1:T(8,128)S(1)}, f32[2,2,8,128]{3,2,0,1:T(8,128)S(1)}, u32[]{:S(2)}, u32[]{:S(2)}) collective-permute-start(f32[2,2,8,128]{3,2,0,1:T(8,128)S(1)} %pad_maximum_fusion.3), channel_id=1, source_target_pairs={{0,8},{8,0},{16,24},{24,16},{1,9},{9,1},{17,25},{25,17},{2,10},{10... | collective-permute-start | bytes 49160 | tf_op jit(solution)/shard_map/ppermute | solution.py:33
  32.3 1.8 %collective-permute-done.7 = f32[2,2,8,128]{3,2,0,1:T(8,128)S(1)} collective-permute-done((f32[2,2,8,128]{3,2,0,1:T(8,128)S(1)}, f32[2,2,8,128]{3,2,0,1:T(8,128)S(1)}, u32[]{:S(2)}, u32[]{:S(2)}) %collective-permute-start.7) | collective-permute-done | bytes 16416 | tf_op jit(solution)/shard_map/ppermute | solution.py:33
  34.1 0.0 collective-permute-done.6
  34.1 1.0 %collective-permute-start.9 = (f32[6,8,128]{2,1,0:T(8,128)S(1)}, f32[6,8,128]{2,1,0:T(8,128)S(1)}, u32[]{:S(2)}, u32[]{:S(2)}) collective-permute-start(f32[6,8,128]{2,1,0:T(8,128)S(1)} %get-tuple-element.46), channel_id=1, source_target_pairs={{1,2},{2,1},{3,0},{0,3},{5,6},{6,5},{7,4},{4,7},{9,10},{10,9},{11,... | collective-permute-start | bytes 73736 | tf_op jit(solution)/shard_map/ppermute | solution.py:33
  35.1 1.2 %collective-permute-start.8 = (f32[6,8,128]{2,1,0:T(8,128)S(1)}, f32[6,8,128]{2,1,0:T(8,128)S(1)}, u32[]{:S(2)}, u32[]{:S(2)}) collective-permute-start(f32[6,8,128]{2,1,0:T(8,128)S(1)} %get-tuple-element.47), channel_id=1, source_target_pairs={{0,1},{1,0},{2,3},{3,2},{4,5},{5,4},{6,7},{7,6},{8,9},{9,8},{10,11... | collective-permute-start | bytes 73736 | tf_op jit(solution)/shard_map/ppermute | solution.py:33
  36.3 0.6 %force_own.1 = (f32[2,48,128]{2,1,0:T(8,128)S(1)}, f32[2,48,128]{2,1,0:T(8,128)S(1)}) custom-call(f32[2,8,128]{2,1,0:T(8,128)S(1)} %get-tuple-element.24.refs_0_, f32[2,8,128]{2,1,0:T(8,128)S(1)} %get-tuple-element.29.refs_1_, bf16[4,256,128]{2,1,0:T(8,128)(2,1)S(1)} %get-tuple-element.30.refs_2_, f32[4,128,128]{2,1,0:T(8,128)S(1)} %get-tuple-element.31.refs_3_), custom_call_target="tpu_custom_call" | custom-call | flops 2359296 | bytes 16384 | tf_op jit(solution)/shard_map/force_own/pallas_call | solution.py:514
  36.8 0.9 %force_y.1 = (f32[2,48,128]{2,1,0:T(8,128)S(1)}, f32[2,48,128]{2,1,0:T(8,128)S(1)}) custom-call(f32[2,8,128]{2,1,0:T(8,128)S(1)} %get-tuple-element.24.refs_0_, f32[2,8,128]{2,1,0:T(8,128)S(1)} %get-tuple-element.29.refs_1_, f32[2,8,128]{2,1,0:T(8,128)S(1)} %collective-permute-done.5.refs_2_, f32[2,8,128]{2,1,0:T(8,128)S(1)} %collective-permute-done.refs_1_.refs_3_, ...), custom_call_target="tpu_custom_call" | custom-call | flops 4718592 | bytes 32768 | tf_op jit(solution)/shard_map/force_y/pallas_call | solution.py:514
  37.8 2.5 %force_x.1 = (f32[2,48,128]{2,1,0:T(8,128)S(1)}, f32[2,48,128]{2,1,0:T(8,128)S(1)}) custom-call(f32[2,8,128]{2,1,0:T(8,128)S(1)} %get-tuple-element.24.refs_0_, f32[2,8,128]{2,1,0:T(8,128)S(1)} %get-tuple-element.29.refs_1_, f32[2,2,8,128]{3,2,1,0:T(8,128)S(1)} %copy.12.refs_2_, f32[2,2,8,128]{3,2,1,0:T(8,128)S(1)} %copy.13.refs_3_, ...), custom_call_target="tpu_custom_call" | custom-call | flops 14155776 | bytes 98304 | tf_op jit(solution)/shard_map/force_x/pallas_call | solution.py:514
  40.3 0.0 collective-permute-done.9.refs_3_
  40.3 0.0 collective-permute-done.8.refs_2_
  40.3 2.5 %force_z.1 = (f32[1,1,3,2,128]{4,3,2,1,0:T(2,128)}, f32[1,1,2,128]{3,2,1,0:T(2,128)}) custom-call(f32[2,8,128]{2,1,0:T(8,128)S(1)} %get-tuple-element.24.refs_0_, f32[2,8,128]{2,1,0:T(8,128)S(1)} %get-tuple-element.29.refs_1_, f32[6,8,128]{2,1,0:T(8,128)S(1)} %collective-permute-done.8.refs_2_, f32[6,8,128]{2,1,0:T(8,128)S(1)} %collective-permute-done.9.refs_3_, ...), custom_call_target="tpu_custom_call" | custom-call | flops 10616832 | bytes 73728 | tf_op jit(solution)/shard_map/force_z/pallas_call | solution.py:514
  (10 shorter events, 0.0 us)
Async XLA Ops:
  0.6 0.7 %copy-start = (f32[1,1,2,3,128]{4,2,3,1,0:T(2,128)S(1)}, f32[1,1,2,3,128]{4,2,3,1,0:T(2,128)}, u32[]{:S(2)}) copy-start(f32[1,1,2,3,128]{4,2,3,1,0:T(2,128)} %param.8) | copy-start | bytes 9220
  1.3 0.7 %copy-start.1 = (f32[1,1,2,3,128]{4,2,3,1,0:T(2,128)S(1)}, f32[1,1,2,3,128]{4,2,3,1,0:T(2,128)}, u32[]{:S(2)}) copy-start(f32[1,1,2,3,128]{4,2,3,1,0:T(2,128)} %param.9) | copy-start | bytes 9220
  2.0 0.7 %copy-start.2 = (f32[1,1,2,128]{3,2,1,0:T(2,128)S(1)}, f32[1,1,2,128]{3,2,1,0:T(2,128)}, u32[]{:S(2)}) copy-start(f32[1,1,2,128]{3,2,1,0:T(2,128)} %refs_2_.1) | copy-start | bytes 3076
  2.7 0.7 %copy-start.3 = (f32[1,1,2,128]{3,2,1,0:T(2,128)S(1)}, f32[1,1,2,128]{3,2,1,0:T(2,128)}, u32[]{:S(2)}) copy-start(f32[1,1,2,128]{3,2,1,0:T(2,128)} %refs_3_.1) | copy-start | bytes 3076
  3.4 0.7 %copy-start.4 = (f32[1,1,2,128]{3,2,1,0:T(2,128)S(1)}, f32[1,1,2,128]{3,2,1,0:T(2,128)}, u32[]{:S(2)}) copy-start(f32[1,1,2,128]{3,2,1,0:T(2,128)} %refs_4_.1) | copy-start | bytes 3076
  4.0 0.7 %copy-start.5 = (f32[1,1,2,128]{3,2,1,0:T(2,128)S(1)}, f32[1,1,2,128]{3,2,1,0:T(2,128)}, u32[]{:S(2)}) copy-start(f32[1,1,2,128]{3,2,1,0:T(2,128)} %refs_5_.1) | copy-start | bytes 3076
  4.7 0.7 %copy-start.6 = (s32[1,1,2,13]{3,2,1,0:T(2,128)S(1)}, s32[1,1,2,13]{3,2,1,0:T(2,128)}, u32[]{:S(2)}) copy-start(s32[1,1,2,13]{3,2,1,0:T(2,128)} %refs_6_.1) | copy-start | bytes 316
  5.4 0.7 %copy-start.7 = (s32[1,1,2]{2,1,0:T(1,128)S(1)}, s32[1,1,2]{2,1,0:T(1,128)}, u32[]{:S(2)}) copy-start(s32[1,1,2]{2,1,0:T(1,128)} %refs_7_.1) | copy-start | bytes 28
  6.7 4.7 %collective-permute-start = (f32[2,8,128]{2,1,0:T(8,128)S(1)}, f32[2,8,128]{2,1,0:T(8,128)S(1)}, u32[]{:S(2)}, u32[]{:S(2)}) collective-permute-start(f32[2,8,128]{2,1,0:T(8,128)S(1)} %get-tuple-element.24.refs_0_), channel_id=1, source_target_pairs={{0,4},{4,0},{1,5},{5,1},{2,6},{6,2},{3,7},{7,3},{8,12},{12,8},{9,1... | collective-permute-start | bytes 24584 | tf_op jit(solution)/shard_map/ppermute | solution.py:33
  11.4 3.2 %collective-permute-start.2 = (f32[2,2,8,128]{3,2,0,1:T(8,128)S(1)}, f32[2,2,8,128]{3,2,0,1:T(8,128)S(1)}, u32[]{:S(2)}, u32[]{:S(2)}) collective-permute-start(f32[2,2,8,128]{3,2,0,1:T(8,128)S(1)} %pad_maximum_fusion.2), channel_id=1, source_target_pairs={{8,16},{16,8},{24,0},{0,24},{9,17},{17,9},{25,1},{1,25},{10,18},{1... | collective-permute-start | bytes 49160 | tf_op jit(solution)/shard_map/ppermute | solution.py:33
  11.7 2.8 %collective-permute-start.1 = (f32[2,2,8,128]{3,2,0,1:T(8,128)S(1)}, f32[2,2,8,128]{3,2,0,1:T(8,128)S(1)}, u32[]{:S(2)}, u32[]{:S(2)}) collective-permute-start(f32[2,2,8,128]{3,2,0,1:T(8,128)S(1)} %pad_maximum_fusion.2), channel_id=1, source_target_pairs={{0,8},{8,0},{16,24},{24,16},{1,9},{9,1},{17,25},{25,17},{2,10},{10... | collective-permute-start | bytes 49160 | tf_op jit(solution)/shard_map/ppermute | solution.py:33
  14.6 9.8 %collective-permute-start.4 = (f32[6,8,128]{2,1,0:T(8,128)S(1)}, f32[6,8,128]{2,1,0:T(8,128)S(1)}, u32[]{:S(2)}, u32[]{:S(2)}) collective-permute-start(f32[6,8,128]{2,1,0:T(8,128)S(1)} %get-tuple-element.48), channel_id=1, source_target_pairs={{1,2},{2,1},{3,0},{0,3},{5,6},{6,5},{7,4},{4,7},{9,10},{10,9},{11,... | collective-permute-start | bytes 73736 | tf_op jit(solution)/shard_map/ppermute | solution.py:33
  18.9 5.5 %collective-permute-start.3 = (f32[6,8,128]{2,1,0:T(8,128)S(1)}, f32[6,8,128]{2,1,0:T(8,128)S(1)}, u32[]{:S(2)}, u32[]{:S(2)}) collective-permute-start(f32[6,8,128]{2,1,0:T(8,128)S(1)} %get-tuple-element.49), channel_id=1, source_target_pairs={{0,1},{1,0},{2,3},{3,2},{4,5},{5,4},{6,7},{7,6},{8,9},{9,8},{10,11... | collective-permute-start | bytes 73736 | tf_op jit(solution)/shard_map/ppermute | solution.py:33
  27.1 3.7 %collective-permute-start.5 = (f32[2,8,128]{2,1,0:T(8,128)S(1)}, f32[2,8,128]{2,1,0:T(8,128)S(1)}, u32[]{:S(2)}, u32[]{:S(2)}) collective-permute-start(f32[2,8,128]{2,1,0:T(8,128)S(1)} %get-tuple-element.29.refs_1_), channel_id=1, source_target_pairs={{0,4},{4,0},{1,5},{5,1},{2,6},{6,2},{3,7},{7,3},{8,12},{12,8},{9,1... | collective-permute-start | bytes 24584 | tf_op jit(solution)/shard_map/ppermute | solution.py:33
  30.8 3.3 %collective-permute-start.7 = (f32[2,2,8,128]{3,2,0,1:T(8,128)S(1)}, f32[2,2,8,128]{3,2,0,1:T(8,128)S(1)}, u32[]{:S(2)}, u32[]{:S(2)}) collective-permute-start(f32[2,2,8,128]{3,2,0,1:T(8,128)S(1)} %pad_maximum_fusion.3), channel_id=1, source_target_pairs={{8,16},{16,8},{24,0},{0,24},{9,17},{17,9},{25,1},{1,25},{10,18},{1... | collective-permute-start | bytes 49160 | tf_op jit(solution)/shard_map/ppermute | solution.py:33
  30.8 3.3 %collective-permute-start.6 = (f32[2,2,8,128]{3,2,0,1:T(8,128)S(1)}, f32[2,2,8,128]{3,2,0,1:T(8,128)S(1)}, u32[]{:S(2)}, u32[]{:S(2)}) collective-permute-start(f32[2,2,8,128]{3,2,0,1:T(8,128)S(1)} %pad_maximum_fusion.3), channel_id=1, source_target_pairs={{0,8},{8,0},{16,24},{24,16},{1,9},{9,1},{17,25},{25,17},{2,10},{10... | collective-permute-start | bytes 49160 | tf_op jit(solution)/shard_map/ppermute | solution.py:33
  34.1 6.2 %collective-permute-start.9 = (f32[6,8,128]{2,1,0:T(8,128)S(1)}, f32[6,8,128]{2,1,0:T(8,128)S(1)}, u32[]{:S(2)}, u32[]{:S(2)}) collective-permute-start(f32[6,8,128]{2,1,0:T(8,128)S(1)} %get-tuple-element.46), channel_id=1, source_target_pairs={{1,2},{2,1},{3,0},{0,3},{5,6},{6,5},{7,4},{4,7},{9,10},{10,9},{11,... | collective-permute-start | bytes 73736 | tf_op jit(solution)/shard_map/ppermute | solution.py:33
  35.1 5.2 %collective-permute-start.8 = (f32[6,8,128]{2,1,0:T(8,128)S(1)}, f32[6,8,128]{2,1,0:T(8,128)S(1)}, u32[]{:S(2)}, u32[]{:S(2)}) collective-permute-start(f32[6,8,128]{2,1,0:T(8,128)S(1)} %get-tuple-element.47), channel_id=1, source_target_pairs={{0,1},{1,0},{2,3},{3,2},{4,5},{5,4},{6,7},{7,6},{8,9},{9,8},{10,11... | collective-permute-start | bytes 73736 | tf_op jit(solution)/shard_map/ppermute | solution.py:33

commit v3 on v2

--- a/solution.py
+++ b/solution.py
@@ -14,6 +14,7 @@
 pair_scale = -160.0 * kernel_norm
 
 LIMIT = 16 * 1024 * 1024
+PACK_LIMIT = 63 * 1024 * 1024 - 65536
 AXES = ("gx", "gy", "gz")
 X, Y, Z, H, V, M, FLAGS = range(7)
 PR, CA, CX, CY, CZ, VX, VY, VZ = range(8)
@@ -390,17 +391,16 @@
 
 
 def pack_kernel(leaves, per_leaf, *refs):
-    inputs = refs[:6]
-    neighbours, counts = refs[6:8]
-    out, extra = refs[8:10]
-    held = refs[10:16]
-    sems = refs[16]
+    inputs, out, extra, held, sems = refs[:8], refs[8], refs[9], refs[10:18], refs[18]
+    neighbours, counts = held[6:8]
     copies = [
         pltpu.make_async_copy(source, target, sems.at[k])
         for k, (source, target) in enumerate(zip(inputs, held))
     ]
-    for copy in copies:
+    for copy in copies[::-1]:
         copy.start()
+    for copy in copies[6:]:
+        copy.wait()
     lane = lax.broadcasted_iota(jnp.int32, (1, per_leaf), 1)
     for leaf in range(leaves):
         flags = jnp.zeros((1, per_leaf), jnp.float32)
@@ -410,9 +410,9 @@
         out[leaf, FLAGS : FLAGS + 1, :] = flags
         out[leaf, FLAGS + 1 : FLAGS + 2, :] = jnp.zeros((1, per_leaf), jnp.float32)
         extra[leaf, 4:8, :] = jnp.zeros((4, per_leaf), jnp.float32)
-    for copy in copies:
+    for copy in copies[:6]:
         copy.wait()
-    offsets, velocity, masses, volumes, energies, smoothing = held
+    offsets, velocity, masses, volumes, energies, smoothing = held[:6]
     for leaf in range(leaves):
         one = slice(leaf, leaf + 1)
         for part in range(3):
@@ -428,8 +428,7 @@
     leaves, per_leaf = masses.shape[2], masses.shape[3]
     f32, bf16 = jnp.float32, jnp.bfloat16
     vmem = pl.BlockSpec(memory_space=pltpu.VMEM)
-    smem = pl.BlockSpec(memory_space=pltpu.SMEM)
-    anywhere = pl.BlockSpec(memory_space=pl.ANY)
+    hbm = pl.BlockSpec(memory_space=pltpu.HBM)
     params = pltpu.CompilerParams(vmem_limit_bytes=LIMIT)
     parity = lax.axis_index("gz") % 2 == 0
     offsets = jnp.swapaxes(offsets, 2, 3)
@@ -443,12 +442,13 @@
     inputs = (offsets, velocity, masses, volumes, energies, smoothing)
     own, extra = pl.pallas_call(
         functools.partial(pack_kernel, leaves, per_leaf),
-        out_shape=[jax.ShapeDtypeStruct((leaves, 8, per_leaf), f32)] * 2,
-        in_specs=[anywhere] * 6 + [smem] * 2,
+        out_shape=[pltpu.VMEM((leaves, 8, per_leaf), f32)] * 2,
+        in_specs=[hbm] * 8,
         out_specs=[vmem] * 2,
         scratch_shapes=[pltpu.VMEM(array.shape, f32) for array in inputs]
-        + [pltpu.SemaphoreType.DMA((6,))],
-        compiler_params=params,
+        + [pltpu.SMEM(array.shape, jnp.int32) for array in (neighbours, counts)]
+        + [pltpu.SemaphoreType.DMA((8,))],
+        compiler_params=pltpu.CompilerParams(vmem_limit_bytes=PACK_LIMIT),
         name="pack",
     )(*inputs, neighbours, counts)
 
@@ -524,16 +524,20 @@
 
     from_y = exchange_y(own)
     acc, *kept_own = moment_call("own", [], None)
+    from_y, acc = lax.optimization_barrier((from_y, acc))
     from_x = exchange_x(own, from_y)
     acc, *kept_y = moment_call("y", from_y, acc)
+    from_x, acc = lax.optimization_barrier((from_x, acc))
     from_z = exchange_z(own, from_y, from_x)
     acc, *kept_x = moment_call("x", from_x, acc)
     fields, *kept_z = moment_call("z", from_z, acc)
 
     field_y = exchange_y(fields)
     accs = force_call("own", [], [], [], kept_own, fields)
+    field_y, accs = lax.optimization_barrier((field_y, accs))
     field_x = exchange_x(fields, field_y)
     accs = force_call("y", field_y, from_y, accs, kept_y, fields)
+    field_x, accs = lax.optimization_barrier((field_x, accs))
     field_z = exchange_z(fields, field_y, field_x)
     accs = force_call("x", field_x, from_x, accs, kept_x, fields)
     acceleration, heating = force_call("z", field_z, from_z, accs, kept_z, fields)

time: 43.1 us -> 35.8 us (0.83)
  local copies, waits for them, and re-layouts: 5.42 us -> 0.01 us
  waiting for transfers between devices: 6.58 us -> 5.1 us
    unnamed x16 -> x0, local copies, waits for them, and re-layouts: 5.41 us -> none
    ppermute x10, waiting for transfers between devices: 6.58 us -> 5.1 us  [swap(): return lax.ppermute(array, axis, pairs)]
  transfers between devices with their start and end apart: 10 -> 10, of which waited for: 4 -> 6; matrix products, arithmetic and copies ran while one was open for 0% -> 0% of each run, Pallas kernels for 22% -> 26%
where the time goes in v3:
time: 35.8 us; the launch traced here: 35.7 us
  Pallas kernels  15.4 us (43%)
  starting transfers between devices  14.3 us (40%)
  waiting for transfers between devices  5.1 us (14%)
  between operations  0.74 us (2%)
    ppermute x10, starting transfers between devices, swap(): return lax.ppermute(array, axis, pairs)  14.3 us
    pallas_call x4, Pallas kernels, moment_call(): pl.pallas_call(body, out_shape=[first] + kept, in_specs=[vmem] * len(oper...  8.12 us
    pallas_call x4, Pallas kernels, force_call(): pl.pallas_call(body, out_shape=out, in_specs=[vmem] * len(operands), out_...  6.46 us
    ppermute x10, waiting for transfers between devices, swap(): return lax.ppermute(array, axis, pairs)  5.1 us
    pallas_call x1, Pallas kernels, per_device(): pl.pallas_call(functools.partial(pack_kernel, leaves, per_leaf), out_shap...  0.85 us
  transfers between devices with their start and end apart: 10, of which 6 were waited for; matrix products, arithmetic and copies ran while one was open for 0% of the time, Pallas kernels for 26%

profile of v3, /device:TPU:0, one launch (start us, length us, event | category | flops | bytes accessed | tf_op | source)
XLA Modules:
  0.0 35.7 jit_solution(2665931258667349192)
XLA Ops:
  0.6 0.9 %pack.1 = (f32[2,8,128]{2,1,0:T(8,128)S(1)}, f32[2,8,128]{2,1,0:T(8,128)S(1)}) custom-call(f32[1,1,3,2,128]{4,3,2,1,0:T(2,128)} %bitcast.23, f32[1,1,3,2,128]{4,3,2,1,0:T(2,128)} %bitcast.24, f32[1,1,2,128]{3,2,1,0:T(2,128)} %refs_2_.1, f32[1,1,2,128]{3,2,1,0:T(2,128)} %refs_3_.1, f32[1,1,2,128]{3,2,1,0:T(2,128)} %refs_4_.1, f32[1,1,2,128]{3,2,1,0:T(2,128)} %refs_5_.1, ...), custom_call_target="tpu_custom_call" | custom-call | tf_op jit(solution)/shard_map/pack/pallas_call | solution.py:443
  1.5 3.0 %collective-permute-start = (f32[2,8,128]{2,1,0:T(8,128)S(1)}, f32[2,8,128]{2,1,0:T(8,128)S(1)}, u32[]{:S(2)}, u32[]{:S(2)}) collective-permute-start(f32[2,8,128]{2,1,0:T(8,128)S(1)} %get-tuple-element.36.refs_0_), channel_id=1, source_target_pairs={{0,4},{4,0},{1,5},{5,1},{2,6},{6,2},{3,7},{7,3},{8,12},{12,8},{9,1... | collective-permute-start | bytes 24584 | tf_op jit(solution)/shard_map/ppermute | solution.py:34
  4.5 0.9 %moments_own.1 = (f32[2,48,128]{2,1,0:T(8,128)S(1)}, bf16[4,256,128]{2,1,0:T(8,128)(2,1)S(1)}, f32[4,128,128]{2,1,0:T(8,128)S(1)}) custom-call(f32[2,8,128]{2,1,0:T(8,128)S(1)} %get-tuple-element.36.refs_0_), custom_call_target="tpu_custom_call" | custom-call | flops 3604480 | bytes 16384 | tf_op jit(solution)/shard_map/moments_own/pallas_call | solution.py:489
  5.4 0.7 %collective-permute-done.refs_1_.refs_3_ = f32[2,8,128]{2,1,0:T(8,128)S(1)} collective-permute-done((f32[2,8,128]{2,1,0:T(8,128)S(1)}, f32[2,8,128]{2,1,0:T(8,128)S(1)}, u32[]{:S(2)}, u32[]{:S(2)}) %collective-permute-start) | collective-permute-done | bytes 8224 | tf_op jit(solution)/shard_map/ppermute | solution.py:34
  6.2 0.3 collective-permute-start.2
  6.5 1.8 %collective-permute-start.1 = (f32[2,2,8,128]{3,2,0,1:T(8,128)S(1)}, f32[2,2,8,128]{3,2,0,1:T(8,128)S(1)}, u32[]{:S(2)}, u32[]{:S(2)}) collective-permute-start(f32[2,2,8,128]{3,2,0,1:T(8,128)S(1)} %pad_maximum_fusion.2), channel_id=1, source_target_pairs={{0,8},{8,0},{16,24},{24,16},{1,9},{9,1},{17,25},{25,17},{2,10},{10... | collective-permute-start | bytes 49160 | tf_op jit(solution)/shard_map/ppermute | solution.py:34
  8.3 1.1 %moments_y.1 = (f32[2,48,128]{2,1,0:T(8,128)S(1)}, bf16[8,256,128]{2,1,0:T(8,128)(2,1)S(1)}, f32[8,128,128]{2,1,0:T(8,128)S(1)}) custom-call(f32[2,8,128]{2,1,0:T(8,128)S(1)} %get-tuple-element.36.refs_0_, f32[2,8,128]{2,1,0:T(8,128)S(1)} %collective-permute-done.refs_1_.refs_3_, f32[2,48,128]{2,1,0:T(8,128)S(1)} %get-tuple-element.39.refs_2_), custom_call_target="tpu_custom_call" | custom-call | flops 7208960 | bytes 32768 | tf_op jit(solution)/shard_map/moments_y/pallas_call | solution.py:489
  9.4 0.0 collective-permute-done.2
  9.4 0.0 collective-permute-done.1
  9.5 4.2 %collective-permute-start.4 = (f32[6,8,128]{2,1,0:T(8,128)S(1)}, f32[6,8,128]{2,1,0:T(8,128)S(1)}, u32[]{:S(2)}, u32[]{:S(2)}) collective-permute-start(f32[6,8,128]{2,1,0:T(8,128)S(1)} %get-tuple-element.72), channel_id=1, source_target_pairs={{1,2},{2,1},{3,0},{0,3},{5,6},{6,5},{7,4},{4,7},{9,10},{10,9},{11,... | collective-permute-start | bytes 73736 | tf_op jit(solution)/shard_map/ppermute | solution.py:34
  13.6 0.0 collective-permute-start.3
  13.7 3.5 %moments_x.1 = (f32[2,48,128]{2,1,0:T(8,128)S(1)}, bf16[24,256,128]{2,1,0:T(8,128)(2,1)S(1)}, f32[24,128,128]{2,1,0:T(8,128)S(1)}) custom-call(f32[2,8,128]{2,1,0:T(8,128)S(1)} %get-tuple-element.36.refs_0_, f32[2,2,8,128]{3,2,1,0:T(8,128)S(1)} %copy.10.refs_1_.refs_4_, f32[2,2,8,128]{3,2,1,0:T(8,128)S(1)} %copy.11.refs_2_.refs_5_, ...), custom_call_target="tpu_custom_call" | custom-call | flops 21626880 | bytes 98304 | tf_op jit(solution)/shard_map/moments_x/pallas_call | solution.py:489
  17.1 0.0 collective-permute-done.4.refs_2_.refs_5_
  17.1 0.3 collective-permute-done.3.refs_1_.refs_4_
  17.5 2.7 %moments_z.1 = (f32[2,8,128]{2,1,0:T(8,128)S(1)}, bf16[18,256,128]{2,1,0:T(8,128)(2,1)S(1)}, f32[18,128,128]{2,1,0:T(8,128)S(1)}) custom-call(f32[2,8,128]{2,1,0:T(8,128)S(1)} %get-tuple-element.36.refs_0_, f32[6,8,128]{2,1,0:T(8,128)S(1)} %collective-permute-done.3.refs_1_.refs_4_, f32[6,8,128]{2,1,0:T(8,128)S(1)} %collective-permute-done.4.refs_2_.refs_5_, ...), custom_call_target="tpu_custom_call" | custom-call | flops 16220160 | bytes 73728 | tf_op jit(solution)/shard_map/moments_z/pallas_call | solution.py:489
  20.1 1.6 %collective-permute-start.5 = (f32[2,8,128]{2,1,0:T(8,128)S(1)}, f32[2,8,128]{2,1,0:T(8,128)S(1)}, u32[]{:S(2)}, u32[]{:S(2)}) collective-permute-start(f32[2,8,128]{2,1,0:T(8,128)S(1)} %get-tuple-element.46.refs_1_), channel_id=1, source_target_pairs={{0,4},{4,0},{1,5},{5,1},{2,6},{6,2},{3,7},{7,3},{8,12},{12,8},{9,1... | collective-permute-start | bytes 24584 | tf_op jit(solution)/shard_map/ppermute | solution.py:34
  21.7 0.6 %force_own.1 = (f32[2,48,128]{2,1,0:T(8,128)S(1)}, f32[2,48,128]{2,1,0:T(8,128)S(1)}) custom-call(f32[2,8,128]{2,1,0:T(8,128)S(1)} %get-tuple-element.36.refs_0_, f32[2,8,128]{2,1,0:T(8,128)S(1)} %get-tuple-element.46.refs_1_, bf16[4,256,128]{2,1,0:T(8,128)(2,1)S(1)} %get-tuple-element.47.refs_2_, f32[4,128,128]{2,1,0:T(8,128)S(1)} %get-tuple-element.48.refs_3_), custom_call_target="tpu_custom_call" | custom-call | flops 2359296 | bytes 16384 | tf_op jit(solution)/shard_map/force_own/pallas_call | solution.py:514
  22.3 1.6 %collective-permute-done.5.refs_2_ = f32[2,8,128]{2,1,0:T(8,128)S(1)} collective-permute-done((f32[2,8,128]{2,1,0:T(8,128)S(1)}, f32[2,8,128]{2,1,0:T(8,128)S(1)}, u32[]{:S(2)}, u32[]{:S(2)}) %collective-permute-start.5) | collective-permute-done | bytes 8224 | tf_op jit(solution)/shard_map/ppermute | solution.py:34
  23.9 0.0 collective-permute-start.7
  23.9 1.5 %collective-permute-start.6 = (f32[2,2,8,128]{3,2,0,1:T(8,128)S(1)}, f32[2,2,8,128]{3,2,0,1:T(8,128)S(1)}, u32[]{:S(2)}, u32[]{:S(2)}) collective-permute-start(f32[2,2,8,128]{3,2,0,1:T(8,128)S(1)} %pad_maximum_fusion.3), channel_id=1, source_target_pairs={{0,8},{8,0},{16,24},{24,16},{1,9},{9,1},{17,25},{25,17},{2,10},{10... | collective-permute-start | bytes 49160 | tf_op jit(solution)/shard_map/ppermute | solution.py:34
  25.4 0.9 %force_y.1 = (f32[2,48,128]{2,1,0:T(8,128)S(1)}, f32[2,48,128]{2,1,0:T(8,128)S(1)}) custom-call(f32[2,8,128]{2,1,0:T(8,128)S(1)} %get-tuple-element.36.refs_0_, f32[2,8,128]{2,1,0:T(8,128)S(1)} %get-tuple-element.46.refs_1_, f32[2,8,128]{2,1,0:T(8,128)S(1)} %collective-permute-done.5.refs_2_, f32[2,8,128]{2,1,0:T(8,128)S(1)} %collective-permute-done.refs_1_.refs_3_, ...), custom_call_target="tpu_custom_call" | custom-call | flops 4718592 | bytes 32768 | tf_op jit(solution)/shard_map/force_y/pallas_call | solution.py:514
  26.3 0.8 %collective-permute-done.7 = f32[2,2,8,128]{3,2,0,1:T(8,128)S(1)} collective-permute-done((f32[2,2,8,128]{3,2,0,1:T(8,128)S(1)}, f32[2,2,8,128]{3,2,0,1:T(8,128)S(1)}, u32[]{:S(2)}, u32[]{:S(2)}) %collective-permute-start.7) | collective-permute-done | bytes 16416 | tf_op jit(solution)/shard_map/ppermute | solution.py:34
  27.2 0.0 collective-permute-done.6
  27.2 1.9 %collective-permute-start.9 = (f32[6,8,128]{2,1,0:T(8,128)S(1)}, f32[6,8,128]{2,1,0:T(8,128)S(1)}, u32[]{:S(2)}, u32[]{:S(2)}) collective-permute-start(f32[6,8,128]{2,1,0:T(8,128)S(1)} %get-tuple-element.70), channel_id=1, source_target_pairs={{1,2},{2,1},{3,0},{0,3},{5,6},{6,5},{7,4},{4,7},{9,10},{10,9},{11,... | collective-permute-start | bytes 73736 | tf_op jit(solution)/shard_map/ppermute | solution.py:34
  29.1 0.0 collective-permute-start.8
  29.1 2.5 %force_x.1 = (f32[2,48,128]{2,1,0:T(8,128)S(1)}, f32[2,48,128]{2,1,0:T(8,128)S(1)}) custom-call(f32[2,8,128]{2,1,0:T(8,128)S(1)} %get-tuple-element.36.refs_0_, f32[2,8,128]{2,1,0:T(8,128)S(1)} %get-tuple-element.46.refs_1_, f32[2,2,8,128]{3,2,1,0:T(8,128)S(1)} %copy.12.refs_2_, f32[2,2,8,128]{3,2,1,0:T(8,128)S(1)} %copy.13.refs_3_, ...), custom_call_target="tpu_custom_call" | custom-call | flops 14155776 | bytes 98304 | tf_op jit(solution)/shard_map/force_x/pallas_call | solution.py:514
  31.5 1.4 %collective-permute-done.9.refs_3_ = f32[6,8,128]{2,1,0:T(8,128)S(1)} collective-permute-done((f32[6,8,128]{2,1,0:T(8,128)S(1)}, f32[6,8,128]{2,1,0:T(8,128)S(1)}, u32[]{:S(2)}, u32[]{:S(2)}) %collective-permute-start.9) | collective-permute-done | bytes 24608 | tf_op jit(solution)/shard_map/ppermute | solution.py:34
  32.9 0.2 collective-permute-done.8.refs_2_
  33.2 2.5 %force_z.1 = (f32[1,1,3,2,128]{4,3,2,1,0:T(2,128)}, f32[1,1,2,128]{3,2,1,0:T(2,128)}) custom-call(f32[2,8,128]{2,1,0:T(8,128)S(1)} %get-tuple-element.36.refs_0_, f32[2,8,128]{2,1,0:T(8,128)S(1)} %get-tuple-element.46.refs_1_, f32[6,8,128]{2,1,0:T(8,128)S(1)} %collective-permute-done.8.refs_2_, f32[6,8,128]{2,1,0:T(8,128)S(1)} %collective-permute-done.9.refs_3_, ...), custom_call_target="tpu_custom_call" | custom-call | flops 10616832 | bytes 73728 | tf_op jit(solution)/shard_map/force_z/pallas_call | solution.py:514
  (10 shorter events, 0.0 us)
Async XLA Ops:
  1.5 4.7 %collective-permute-start = (f32[2,8,128]{2,1,0:T(8,128)S(1)}, f32[2,8,128]{2,1,0:T(8,128)S(1)}, u32[]{:S(2)}, u32[]{:S(2)}) collective-permute-start(f32[2,8,128]{2,1,0:T(8,128)S(1)} %get-tuple-element.36.refs_0_), channel_id=1, source_target_pairs={{0,4},{4,0},{1,5},{5,1},{2,6},{6,2},{3,7},{7,3},{8,12},{12,8},{9,1... | collective-permute-start | bytes 24584 | tf_op jit(solution)/shard_map/ppermute | solution.py:34
  6.2 3.3 %collective-permute-start.2 = (f32[2,2,8,128]{3,2,0,1:T(8,128)S(1)}, f32[2,2,8,128]{3,2,0,1:T(8,128)S(1)}, u32[]{:S(2)}, u32[]{:S(2)}) collective-permute-start(f32[2,2,8,128]{3,2,0,1:T(8,128)S(1)} %pad_maximum_fusion.2), channel_id=1, source_target_pairs={{8,16},{16,8},{24,0},{0,24},{9,17},{17,9},{25,1},{1,25},{10,18},{1... | collective-permute-start | bytes 49160 | tf_op jit(solution)/shard_map/ppermute | solution.py:34
  6.5 2.9 %collective-permute-start.1 = (f32[2,2,8,128]{3,2,0,1:T(8,128)S(1)}, f32[2,2,8,128]{3,2,0,1:T(8,128)S(1)}, u32[]{:S(2)}, u32[]{:S(2)}) collective-permute-start(f32[2,2,8,128]{3,2,0,1:T(8,128)S(1)} %pad_maximum_fusion.2), channel_id=1, source_target_pairs={{0,8},{8,0},{16,24},{24,16},{1,9},{9,1},{17,25},{25,17},{2,10},{10... | collective-permute-start | bytes 49160 | tf_op jit(solution)/shard_map/ppermute | solution.py:34
  9.5 7.7 %collective-permute-start.4 = (f32[6,8,128]{2,1,0:T(8,128)S(1)}, f32[6,8,128]{2,1,0:T(8,128)S(1)}, u32[]{:S(2)}, u32[]{:S(2)}) collective-permute-start(f32[6,8,128]{2,1,0:T(8,128)S(1)} %get-tuple-element.72), channel_id=1, source_target_pairs={{1,2},{2,1},{3,0},{0,3},{5,6},{6,5},{7,4},{4,7},{9,10},{10,9},{11,... | collective-permute-start | bytes 73736 | tf_op jit(solution)/shard_map/ppermute | solution.py:34
  13.6 3.8 %collective-permute-start.3 = (f32[6,8,128]{2,1,0:T(8,128)S(1)}, f32[6,8,128]{2,1,0:T(8,128)S(1)}, u32[]{:S(2)}, u32[]{:S(2)}) collective-permute-start(f32[6,8,128]{2,1,0:T(8,128)S(1)} %get-tuple-element.73), channel_id=1, source_target_pairs={{0,1},{1,0},{2,3},{3,2},{4,5},{5,4},{6,7},{7,6},{8,9},{9,8},{10,11... | collective-permute-start | bytes 73736 | tf_op jit(solution)/shard_map/ppermute | solution.py:34
  20.1 3.7 %collective-permute-start.5 = (f32[2,8,128]{2,1,0:T(8,128)S(1)}, f32[2,8,128]{2,1,0:T(8,128)S(1)}, u32[]{:S(2)}, u32[]{:S(2)}) collective-permute-start(f32[2,8,128]{2,1,0:T(8,128)S(1)} %get-tuple-element.46.refs_1_), channel_id=1, source_target_pairs={{0,4},{4,0},{1,5},{5,1},{2,6},{6,2},{3,7},{7,3},{8,12},{12,8},{9,1... | collective-permute-start | bytes 24584 | tf_op jit(solution)/shard_map/ppermute | solution.py:34
  23.9 3.3 %collective-permute-start.7 = (f32[2,2,8,128]{3,2,0,1:T(8,128)S(1)}, f32[2,2,8,128]{3,2,0,1:T(8,128)S(1)}, u32[]{:S(2)}, u32[]{:S(2)}) collective-permute-start(f32[2,2,8,128]{3,2,0,1:T(8,128)S(1)} %pad_maximum_fusion.3), channel_id=1, source_target_pairs={{8,16},{16,8},{24,0},{0,24},{9,17},{17,9},{25,1},{1,25},{10,18},{1... | collective-permute-start | bytes 49160 | tf_op jit(solution)/shard_map/ppermute | solution.py:34
  23.9 3.3 %collective-permute-start.6 = (f32[2,2,8,128]{3,2,0,1:T(8,128)S(1)}, f32[2,2,8,128]{3,2,0,1:T(8,128)S(1)}, u32[]{:S(2)}, u32[]{:S(2)}) collective-permute-start(f32[2,2,8,128]{3,2,0,1:T(8,128)S(1)} %pad_maximum_fusion.3), channel_id=1, source_target_pairs={{0,8},{8,0},{16,24},{24,16},{1,9},{9,1},{17,25},{25,17},{2,10},{10... | collective-permute-start | bytes 49160 | tf_op jit(solution)/shard_map/ppermute | solution.py:34
  27.2 5.7 %collective-permute-start.9 = (f32[6,8,128]{2,1,0:T(8,128)S(1)}, f32[6,8,128]{2,1,0:T(8,128)S(1)}, u32[]{:S(2)}, u32[]{:S(2)}) collective-permute-start(f32[6,8,128]{2,1,0:T(8,128)S(1)} %get-tuple-element.70), channel_id=1, source_target_pairs={{1,2},{2,1},{3,0},{0,3},{5,6},{6,5},{7,4},{4,7},{9,10},{10,9},{11,... | collective-permute-start | bytes 73736 | tf_op jit(solution)/shard_map/ppermute | solution.py:34
  29.1 4.1 %collective-permute-start.8 = (f32[6,8,128]{2,1,0:T(8,128)S(1)}, f32[6,8,128]{2,1,0:T(8,128)S(1)}, u32[]{:S(2)}, u32[]{:S(2)}) collective-permute-start(f32[6,8,128]{2,1,0:T(8,128)S(1)} %get-tuple-element.71), channel_id=1, source_target_pairs={{0,1},{1,0},{2,3},{3,2},{4,5},{5,4},{6,7},{7,6},{8,9},{9,8},{10,11... | collective-permute-start | bytes 73736 | tf_op jit(solution)/shard_map/ppermute | solution.py:34

commit v4 on v3

v4 whole, which is shorter than its diff:
```python
import functools
import math

import jax
import jax.numpy as jnp
from jax import lax
from jax.experimental import pallas as pl
from jax.experimental.pallas import tpu as pltpu
from jax.sharding import PartitionSpec as P

kernel_norm = 21.0 / (16.0 * math.pi)
pressure_factor = 2.0 / 3.0
ridge_factor = 0.1
pair_scale = -160.0 * kernel_norm

LIMIT = 16 * 1024 * 1024
PACK_LIMIT = 63 * 1024 * 1024 - 65536
AXES = ("gx", "gy", "gz")
X, Y, Z, H, V, M, FLAGS = range(7)
VX, VY, VZ, PR, CA, CX, CY, CZ = range(8)


def code_of(step):
    index = (step[0] + 1) * 9 + (step[1] + 1) * 3 + step[2] + 1
    return index if index < 13 else index - 1


def swap(array, axis, phase):
    count = lax.axis_size(axis)
    pairs = []
    for first in range(phase, count, 2):
        second = (first + 1) % count
        pairs += [(first, second), (second, first)]
    return lax.ppermute(array, axis, pairs)


def swaps(array, axis):
    count = lax.axis_size(axis)
    if count == 2:
        return [swap(array, axis, 0)]
    return [swap(array, axis, 1), swap(array, axis, 0)][::-1]


def beside(get, step, axis):
    if step == 0:
        return get(0)
    if lax.axis_size(axis) == 2:
        return get(1)
    even = lax.axis_index(axis) % 2 == 0
    first, second = (1, 2) if step == 1 else (2, 1)
    return jnp.where(even, get(first), get(second))


def split(values, parts):
    pieces = []
    for _ in range(parts - 1):
        piece = values.astype(jnp.bfloat16).astype(jnp.float32)
        pieces.append(piece)
        values = values - piece
    return pieces + [values]


def stacked(parts):
    return jnp.concatenate(parts, axis=0).astype(jnp.bfloat16)


def left_form(features):
    high, middle, low = split(features, 3)
    return stacked([high, high, middle, high, low, middle]).T


def right_form(features):
    high, middle, low = split(features, 3)
    return stacked([high, middle, high, low, high, middle])


def pair_matrix(values):
    return jnp.concatenate(split(values, 2), axis=0).astype(jnp.bfloat16)


def feature_rows(first, second):
    pieces = [piece for pair in zip(split(first, 3), split(second, 3)) for piece in pair]
    rows = stacked(pieces)
    return jnp.concatenate([rows, rows], axis=1)


def dot(left, right):
    return jnp.dot(left, right, preferred_element_type=jnp.float32)


def row_index(per_leaf):
    return lax.broadcasted_iota(jnp.int32, (8, per_leaf), 0)


def chosen(pairs, other):
    for condition, value in pairs[::-1]:
        other = jnp.where(condition, value, other)
    return other


def front_sum(tile, row):
    return jnp.sum(jnp.where(row < 3, tile, 0.0), axis=0, keepdims=True)


def at_front(row, values):
    x, y, z = values
    return chosen([(row == 0, x), (row == 1, y), (row == 2, z)], 0.0)


def rows_of(tile, first, count=1):
    return [tile[k : k + 1] for k in range(first, first + count)]


STAGES = ("own", "y", "x", "z")


def columns_of(stage):
    return {"own": (0,), "y": (0,), "x": (-1, 1), "z": (-1, 0, 1)}[stage]


def slots_of(stage, leaves):
    slots = {}
    for dy in (-1, 0, 1):
        for leaf in range(leaves):
            for level in range(leaf - 1, leaf + 2):
                outside = level < 0 or level >= leaves
                if outside != (stage == "z"):
                    continue
                if (stage == "own" and dy) or (stage == "y" and not dy):
                    continue
                key = (abs(dy) if lax.axis_size("gy") == 2 else dy, level)
                slots.setdefault(key, []).append((leaf, dy))
    return list(slots.items())


def slot_blocks(stage, leaves):
    slots = slots_of(stage, leaves)
    return [(k, level, leaf, dy) for k, ((_, level), blocks) in enumerate(slots) for leaf, dy in blocks]


def tile_at(refs, stage, dx, dy, level, leaves):
    def along_x(kx):
        def along_y(ky):
            if stage == "own":
                return refs[0][level]
            if stage == "y":
                return refs[ky - 1][level]
            if stage == "x":
                return refs[kx - 1][ky, level]
            ny = 1 if lax.axis_size("gy") == 2 else 2
            column = kx * (1 + ny) + ky
            even = lax.axis_index("gz") % 2 == 0
            above = level >= leaves
            return jnp.where(
                even, refs[0 if above else 1][column], refs[1 if above else 0][column]
            )

        return beside(along_y, dy, "gy")

    return beside(along_x, dx, "gx")


def place_shift(dx, dy, level, leaves):
    return (dx, float(dy), float(level) - 0.5 * (leaves - 1))


def centred(tile, row):
    return tile - jnp.where(row < 3, 0.5, 0.0)


def gather_tiles(tiles, sources, stage, leaves):
    slots = slots_of(stage, leaves)
    for column, dx in enumerate(columns_of(stage)):
        for k, ((dy, level), _) in enumerate(slots):
            tiles[column * len(slots) + k] = tile_at(sources, stage, dx, dy, level, leaves)


def find_weights(weights, own, tiles, stage, leaves):
    slots = slots_of(stage, leaves)
    blocks = slot_blocks(stage, leaves)
    for column, dx in enumerate(columns_of(stage)):
        for b, (k, level, leaf, dy) in enumerate(blocks):
            step = (dx, dy, level - leaf)
            if step == (0, 0, 0):
                weight = jnp.ones((1, 1), jnp.float32)
            else:
                code = code_of(step)
                tile = tiles[column * len(slots) + k]
                weight = (
                    own[leaf][FLAGS : FLAGS + 1, code : code + 1]
                    + tile[FLAGS : FLAGS + 1, 25 - code : 26 - code]
                )
            weights[column * len(blocks) + b] = jnp.broadcast_to(weight, weights.shape[1:])


def add_weighted(acc, leaf, sums, weight):
    for k in range(6):
        part = slice(8 * k, 8 * k + 8)
        acc[leaf, part, :] = acc[leaf, part, :] + sums[part] * weight


def over_columns(stage, step_fn):
    columns = columns_of(stage)
    if len(columns) == 1:
        step_fn(0, float(columns[0]))
        return
    pace = columns[1] - columns[0]

    def body(column, carry):
        step_fn(column, (column * pace + columns[0]).astype(jnp.float32))
        return carry

    lax.fori_loop(0, len(columns), body, 0)


def moment_rights(own, leaves, row, rights):
    for stage, right in zip(STAGES, rights):
        blocks = slot_blocks(stage, leaves)
        for column, dx in enumerate(columns_of(stage)):
            for b, (_, level, leaf, dy) in enumerate(blocks):
                shift = at_front(row, (0.5 + dx, 0.5 + dy, 0.5 + level - leaf))
                spot = own[leaf] - shift
                far = front_sum(spot * spot, row)
                right[column * len(blocks) + b] = right_form(
                    chosen([(row < 3, -2.0 * spot), (row == 4, 1.0), (row == 5, far)], 0.0)
                )


def moment_body(stage, leaves, per_leaf, own, sources, right, acc, w_out, g_out, tiles, weights):
    row = row_index(per_leaf)
    gather_tiles(tiles, sources, stage, leaves)
    find_weights(weights, own, tiles, stage, leaves)
    widths = [
        right_form(chosen([(row == 3, 1.0), (row == 5, own[leaf][H : H + 1])], 0.0))
        for leaf in range(leaves)
    ]
    slots = slots_of(stage, leaves)
    count = len(slot_blocks(stage, leaves))

    def step_fn(column, dx):
        number = column * count
        for k, ((_, level), blocks) in enumerate(slots):
            tile = tiles[column * len(slots) + k]
            spot = centred(tile, row)
            near = front_sum(spot * spot, row)
            left = left_form(chosen([(row < 4, spot), (row == 4, near), (row == 5, 1.0)], 0.0))
            volume, mass = tile[V : V + 1], tile[M : M + 1]
            inverses, features = {}, {}
            for leaf, dy in blocks:
                if leaf not in inverses:
                    inverses[leaf] = 1.0 / dot(left, widths[leaf])
                if dy not in features:
                    x, y, z = [
                        part + shift
                        for part, shift in zip(
                            rows_of(spot, X, 3), place_shift(dx, dy, level, leaves)
                        )
                    ]
                    first = chosen(
                        [(row == 0, 1.0), ((row == 2) | (row == 7), y), (row == 3, z)], x
                    ) * chosen(
                        [(row < 4, 1.0), (row == 4, x), (row == 6, z)], y
                    )
                    second = chosen([(row == 0, y), (row == 1, z)], 1.0) * jnp.where(
                        row < 2, z, 1.0
                    )
                    features[dy] = feature_rows(
                        first * volume,
                        second * chosen([(row < 2, volume), (row == 2, mass)], 0.0),
                    )
                inverse = inverses[leaf]
                inverse_sq = inverse * inverse
                dist_sq = jnp.maximum(dot(left, right[number]), 1e-30)
                dist = dist_sq * lax.rsqrt(dist_sq)
                remain = jnp.maximum(1.0 - dist * inverse, 0.0)
                edge = (inverse_sq * inverse) * (remain * remain * remain)
                pair_w = pair_matrix(edge * (remain * (remain - 1.25)))
                w_out[number] = pair_w
                g_out[number] = edge * inverse_sq
                add_weighted(acc, leaf, dot(features[dy], pair_w), weights[number])
                number = number + 1

    over_columns(stage, step_fn)


def moment_own_kernel(leaves, per_leaf, own, acc, w_out, g_out, *refs):
    rights, (tiles, weights) = refs[:4], refs[4:]
    acc[...] = jnp.zeros_like(acc)
    moment_rights(own, leaves, row_index(per_leaf), rights)
    moment_body(
        "own", leaves, per_leaf, own, (own,), rights[0], acc, w_out, g_out, tiles, weights
    )


def moment_kernel(stage, leaves, per_leaf, count, *refs):
    own, sources = refs[0], refs[1 : 1 + count]
    right, acc_in, acc, w_out, g_out, tiles, weights = refs[1 + count :]
    acc[...] = acc_in[...]
    moment_body(
        stage, leaves, per_leaf, own, sources, right, acc, w_out, g_out, tiles, weights
    )


def corrections(moments, smooth, energy):
    density, zeroth, first_x, first_y, first_z, s_xx, s_xy, s_xz, s_yy, s_yz, s_zz = moments
    ridge_term = ridge_factor * smooth * smooth * zeroth
    s_xx = s_xx + ridge_term
    s_yy = s_yy + ridge_term
    s_zz = s_zz + ridge_term
    c_xx = s_yy * s_zz - s_yz * s_yz
    c_xy = s_yz * s_xz - s_xy * s_zz
    c_xz = s_xy * s_yz - s_yy * s_xz
    c_yy = s_xx * s_zz - s_xz * s_xz
    c_yz = s_xy * s_xz - s_xx * s_yz
    c_zz = s_xx * s_yy - s_xy * s_xy
    determinant = s_xx * c_xx + s_xy * c_xy + s_xz * c_xz
    solve_x = (c_xx * first_x + c_xy * first_y + c_xz * first_z) / determinant
    solve_y = (c_xy * first_x + c_yy * first_y + c_yz * first_z) / determinant
    solve_z = (c_xz * first_x + c_yz * first_y + c_zz * first_z) / determinant
    coef_a = 1.0 / (zeroth - (first_x * solve_x + first_y * solve_y + first_z * solve_z))
    pressure = pressure_factor * density * energy
    return [pressure, coef_a, -coef_a * solve_x, -coef_a * solve_y, -coef_a * solve_z]

def gathered(acc, leaf):
    sums = acc[leaf]
    return sums[0:16] + (sums[16:32] + sums[32:48])


def own_place(tile, leaf, leaves):
    shift = place_shift(0.0, 0, leaf, leaves)
    return [part + (move - 0.5) for part, move in zip(rows_of(tile, X, 3), shift)]


def field_kernel(leaves, per_leaf, count, *refs):
    own, sources = refs[0], refs[1 : 1 + count]
    right, acc_in, extra, fields_out, w_out, g_out, tiles, weights, acc = refs[1 + count :]
    acc[...] = acc_in[...]
    moment_body("z", leaves, per_leaf, own, sources, right, acc, w_out, g_out, tiles, weights)
    columns = []
    for leaf in range(leaves):
        sums = gathered(acc, leaf)
        zeroth, fx, fy, fz, sxx, sxy, sxz, syy, syz, szz, density = rows_of(sums, 0, 11)
        x, y, z = own_place(own[leaf], leaf, leaves)
        mx, my, mz = x * zeroth - fx, y * zeroth - fy, z * zeroth - fz
        columns.append(
            [
                density,
                zeroth,
                mx,
                my,
                mz,
                x * mx - x * fx + sxx,
                x * my - y * fx + sxy,
                x * mz - z * fx + sxz,
                y * my - y * fy + syy,
                y * mz - z * fy + syz,
                z * mz - z * fz + szz,
                own[leaf][H : H + 1],
                extra[leaf][3:4],
            ]
        )
    rows = [jnp.concatenate(parts, axis=0) for parts in zip(*columns)]
    fields = corrections([0.2 * part for part in rows[:11]], rows[11], rows[12])
    for leaf in range(leaves):
        fields_out[leaf, VX : VZ + 1, :] = extra[leaf][0:3]
        for k, value in enumerate(fields):
            fields_out[leaf, PR + k : PR + k + 1, :] = value[leaf : leaf + 1]


def force_rights(own, fields, leaves, row, rights):
    for stage, right in zip(STAGES, rights):
        blocks = slot_blocks(stage, leaves)
        for column, dx in enumerate(columns_of(stage)):
            for b, (_, level, leaf, dy) in enumerate(blocks):
                shift = at_front(row, (0.5 + dx, 0.5 + dy, 0.5 + level - leaf))
                spot = own[leaf] - shift
                coefs = pltpu.roll(fields[leaf], 3, 0)
                full = fields[leaf][CA : CA + 1] + front_sum(coefs * spot, row)
                right[column * len(blocks) + b] = right_form(
                    chosen(
                        [(row < 3, -coefs), (row == 3, full), (row == 4, 1.0)],
                        -pltpu.roll(spot, 5, 0),
                    )
                )


def force_body(stage, leaves, per_leaf, own, sources, places, right, accs, w_in, g_in, scratch):
    row = row_index(per_leaf)
    tiles, field_tiles, weights = scratch
    acc_w, acc_g = accs
    gather_tiles(tiles, places, stage, leaves)
    gather_tiles(field_tiles, sources, stage, leaves)
    find_weights(weights, own, tiles, stage, leaves)
    slots = slots_of(stage, leaves)
    count = len(slot_blocks(stage, leaves))

    def step_fn(column, dx):
        number = column * count
        for k, ((_, level), blocks) in enumerate(slots):
            tile = tiles[column * len(slots) + k]
            field = field_tiles[column * len(slots) + k]
            spot = centred(tile, row)
            coefs = pltpu.roll(field, 3, 0)
            volume, pressure = tile[V : V + 1], field[PR : PR + 1]
            full = field[CA : CA + 1] + front_sum(coefs * spot, row)
            left = left_form(
                chosen([(row < 3, spot), (row == 3, 1.0), (row == 4, full)], field)
            )

            def weighted(front, back, factor):
                first = (factor * volume) * chosen(
                    [
                        (row < 3, field),
                        (row == 3, 1.0),
                        (row == 4, front_sum(front * field, row)),
                    ],
                    back,
                )
                return feature_rows(first, pressure * first)

            with_w = weighted(coefs, field, 0.2)
            with_g = {}
            for leaf, dy in blocks:
                if dy not in with_g:
                    front = spot + at_front(row, place_shift(dx, dy, level, leaves))
                    with_g[dy] = weighted(front, pltpu.roll(front, 5, 0), 1.0)
                radial = pair_matrix(g_in[number] * dot(left, right[number]))
                weight = weights[number]
                add_weighted(acc_w, leaf, dot(with_w, w_in[number]), weight)
                add_weighted(acc_g, leaf, dot(with_g[dy], radial), weight)
                number = number + 1

    over_columns(stage, step_fn)


def force_own_kernel(leaves, per_leaf, own, fields, w_in, g_in, acc_w, acc_g, *refs):
    rights, scratch = refs[:4], refs[4:]
    acc_w[...] = jnp.zeros_like(acc_w)
    acc_g[...] = jnp.zeros_like(acc_g)
    force_rights(own, fields, leaves, row_index(per_leaf), rights)
    force_body(
        "own",
        leaves,
        per_leaf,
        own,
        (fields,),
        (own,),
        rights[0],
        (acc_w, acc_g),
        w_in,
        g_in,
        scratch,
    )


def force_kernel(stage, leaves, per_leaf, count, *refs):
    own, sources, places = refs[0], refs[1 : 1 + count], refs[1 + count : 1 + 2 * count]
    right, w_before, g_before, w_in, g_in, acc_w, acc_g, *scratch = refs[1 + 2 * count :]
    acc_w[...] = w_before[...]
    acc_g[...] = g_before[...]
    accs = (acc_w, acc_g)
    force_body(
        stage, leaves, per_leaf, own, sources, places, right, accs, w_in, g_in, scratch
    )


def finish_kernel(leaves, per_leaf, count, *refs):
    own, sources, places = refs[0], refs[1 : 1 + count], refs[1 + count : 1 + 2 * count]
    rest = refs[1 + 2 * count :]
    right, w_before, g_before, w_in, g_in, fields, acceleration, heating = rest[:8]
    scratch, accs = rest[8:11], rest[11:13]
    accs[0][...] = w_before[...]
    accs[1][...] = g_before[...]
    force_body("z", leaves, per_leaf, own, sources, places, right, accs, w_in, g_in, scratch)
    for leaf in range(leaves):
        tile = own[leaf]
        vx, vy, vz, pressure, _, cx, cy, cz = rows_of(fields[leaf], 0, 8)
        sums_w, sums_g = [gathered(acc, leaf) for acc in accs]
        w_rows = rows_of(pressure * sums_w[0:8] + sums_w[8:16], 0, 8)
        g_rows = rows_of(pressure * sums_g[0:8] + sums_g[8:16], 0, 8)
        spots = own_place(tile, leaf, leaves)
        ratio = tile[V : V + 1] / tile[M : M + 1]
        work = w_rows[4] + g_rows[4]
        for k, (coef, spot, speed) in enumerate(zip((cx, cy, cz), spots, (vx, vy, vz))):
            force = (coef * w_rows[3] - w_rows[5 + k]) + (spot * g_rows[3] - g_rows[5 + k])
            work = work + speed * force - coef * w_rows[k] - spot * g_rows[k]
            acceleration[0, 0, k, leaf : leaf + 1, :] = (-0.5 * ratio) * force
        heating[0, 0, leaf : leaf + 1, :] = (0.25 * ratio) * work


def pack_kernel(leaves, per_leaf, *refs):
    inputs, out, extra, held, sems = refs[:8], refs[8], refs[9], refs[10:18], refs[18]
    neighbours, counts = held[6:8]
    copies = [
        pltpu.make_async_copy(source, target, sems.at[k])
        for k, (source, target) in enumerate(zip(inputs, held))
    ]
    for copy in copies[::-1]:
        copy.start()
    for copy in copies[6:]:
        copy.wait()
    lane = lax.broadcasted_iota(jnp.int32, (1, per_leaf), 1)
    for leaf in range(leaves):
        flags = jnp.zeros((1, per_leaf), jnp.float32)
        for slot in range(neighbours.shape[3]):
            code = jnp.where(slot < counts[0, 0, leaf], neighbours[0, 0, leaf, slot], -1)
            flags = flags + jnp.where(lane == code, 1.0, 0.0)
        out[leaf, FLAGS : FLAGS + 1, :] = flags
        out[leaf, FLAGS + 1 : FLAGS + 2, :] = jnp.zeros((1, per_leaf), jnp.float32)
        extra[leaf, 4:8, :] = jnp.zeros((4, per_leaf), jnp.float32)
    for copy in copies[:6]:
        copy.wait()
    offsets, velocity, masses, volumes, energies, smoothing = held[:6]
    for leaf in range(leaves):
        one = slice(leaf, leaf + 1)
        for part in range(3):
            out[leaf, part : part + 1, :] = offsets[0, 0, part, one]
            extra[leaf, part : part + 1, :] = velocity[0, 0, part, one]
        out[leaf, H : H + 1, :] = smoothing[0, 0, one]
        out[leaf, V : V + 1, :] = pair_scale * volumes[0, 0, one]
        out[leaf, M : M + 1, :] = pair_scale * masses[0, 0, one]
        extra[leaf, 3:4, :] = energies[0, 0, one]


def per_device(offsets, velocity, masses, volumes, energies, smoothing, neighbours, counts):
    leaves, per_leaf = masses.shape[2], masses.shape[3]
    f32, bf16 = jnp.float32, jnp.bfloat16
    vmem = pl.BlockSpec(memory_space=pltpu.VMEM)
    hbm = pl.BlockSpec(memory_space=pltpu.HBM)
    params = pltpu.CompilerParams(vmem_limit_bytes=LIMIT)
    parity = lax.axis_index("gz") % 2 == 0
    offsets = jnp.swapaxes(offsets, 2, 3)
    velocity = jnp.swapaxes(velocity, 2, 3)

    def cost(blocks, ops):
        return pl.CostEstimate(
            flops=blocks * per_leaf * per_leaf * ops, bytes_accessed=blocks * 4096, transcendentals=0
        )

    inputs = (offsets, velocity, masses, volumes, energies, smoothing)
    own, extra = pl.pallas_call(
        functools.partial(pack_kernel, leaves, per_leaf),
        out_shape=[pltpu.VMEM((leaves, 8, per_leaf), f32)] * 2,
        in_specs=[hbm] * 8,
        out_specs=[vmem] * 2,
        scratch_shapes=[pltpu.VMEM(array.shape, f32) for array in inputs]
        + [pltpu.SMEM(array.shape, jnp.int32) for array in (neighbours, counts)]
        + [pltpu.SemaphoreType.DMA((8,))],
        compiler_params=pltpu.CompilerParams(vmem_limit_bytes=PACK_LIMIT),
        name="pack",
    )(*inputs, neighbours, counts)

    def exchange_y(tile):
        return swaps(tile, "gy")

    def exchange_x(tile, from_y):
        return swaps(jnp.stack([tile] + from_y, axis=0), "gx")

    def exchange_z(tile, from_y, from_x):
        column = jnp.concatenate([jnp.stack([tile] + from_y, axis=0)] + from_x, axis=0)
        bottom, top = column[:, 0], column[:, leaves - 1]
        far = swap(jnp.where(parity, bottom, top), "gz", 1)
        near = swap(jnp.where(parity, top, bottom), "gz", 0)
        return [near, far]

    sizes = {
        stage: len(columns_of(stage)) * len(slot_blocks(stage, leaves)) for stage in STAGES
    }
    tile_counts = {
        stage: len(columns_of(stage)) * len(slots_of(stage, leaves)) for stage in STAGES
    }
    acc_shape = jax.ShapeDtypeStruct((leaves, 48, per_leaf), f32)
    acc_scratch = pltpu.VMEM((leaves, 48, per_leaf), f32)
    right_shapes = [
        jax.ShapeDtypeStruct((sizes[stage], 48, per_leaf), bf16) for stage in STAGES
    ]

    def tile_scratch(stage):
        return pltpu.VMEM((tile_counts[stage], 8, per_leaf), f32)

    def weight_scratch(stage):
        return pltpu.VMEM((sizes[stage], 8, per_leaf), f32)

    def call(body, name, operands, out, scratch, size, ops):
        return pl.pallas_call(
            body,
            out_shape=out,
            in_specs=[vmem] * len(operands),
            out_specs=[vmem] * len(out),
            scratch_shapes=scratch,
            compiler_params=params,
            cost_estimate=cost(size, ops),
            name=name,
        )(*operands)

    def moment_call(stage, sources, right=None, acc=None):
        size = sizes[stage]
        out = [
            acc_shape,
            jax.ShapeDtypeStruct((size, 2 * per_leaf, per_leaf), bf16),
            jax.ShapeDtypeStruct((size, per_leaf, per_leaf), f32),
        ]
        scratch = [tile_scratch(stage), weight_scratch(stage)]
        operands = [own] + list(sources)
        if stage == "own":
            body = functools.partial(moment_own_kernel, leaves, per_leaf)
            out += right_shapes
        elif stage == "z":
            body = functools.partial(field_kernel, leaves, per_leaf, len(sources))
            operands += [right, acc, extra]
            out[0] = jax.ShapeDtypeStruct((leaves, 8, per_leaf), f32)
            scratch += [acc_scratch]
        else:
            body = functools.partial(moment_kernel, stage, leaves, per_leaf, len(sources))
            operands += [right, acc]
        return call(body, "moments_" + stage, operands, out, scratch, size, 55)

    def force_call(stage, sources, places, right, accs, kept, fields):
        size = sizes[stage]
        out = [acc_shape] * 2
        scratch = [tile_scratch(stage)] * 2 + [weight_scratch(stage)]
        operands = [own] + list(sources) + list(places)
        if stage == "own":
            body = functools.partial(force_own_kernel, leaves, per_leaf)
            operands += [fields] + list(kept)
            out += right_shapes
        elif stage == "z":
            body = functools.partial(finish_kernel, leaves, per_leaf, len(sources))
            operands += [right] + list(accs) + list(kept) + [fields]
            out = [
                jax.ShapeDtypeStruct((1, 1, 3, leaves, per_leaf), f32),
                jax.ShapeDtypeStruct((1, 1, leaves, per_leaf), f32),
            ]
            scratch += [acc_scratch] * 2
        else:
            body = functools.partial(force_kernel, stage, leaves, per_leaf, len(sources))
            operands += [right] + list(accs) + list(kept)
        return call(body, "force_" + stage, operands, out, scratch, size, 36)

    from_y = exchange_y(own)
    acc, w_own, g_own, *rights = moment_call("own", [])
    from_y, acc = lax.optimization_barrier((from_y, acc))
    from_x = exchange_x(own, from_y)
    acc, *kept_y = moment_call("y", from_y, rights[1], acc)
    from_x, acc = lax.optimization_barrier((from_x, acc))
    from_z = exchange_z(own, from_y, from_x)
    acc, *kept_x = moment_call("x", from_x, rights[2], acc)
    fields, *kept_z = moment_call("z", from_z, rights[3], acc)

    field_y = exchange_y(fields)
    *accs, _, right_y, right_x, right_z = force_call(
        "own", [], [], None, None, (w_own, g_own), fields
    )
    field_y, accs = lax.optimization_barrier((field_y, accs))
    field_x = exchange_x(fields, field_y)
    accs = force_call("y", field_y, from_y, right_y, accs, kept_y, fields)
    field_x, accs = lax.optimization_barrier((field_x, accs))
    field_z = exchange_z(fields, field_y, field_x)
    accs = force_call("x", field_x, from_x, right_x, accs, kept_x, fields)
    acceleration, heating = force_call("z", field_z, from_z, right_z, accs, kept_z, fields)
    return (jnp.swapaxes(acceleration, 2, 3), heating)


def solution(mesh):
    in_specs = (
        P("gx", "gy", "gz", None, None),
        P("gx", "gy", "gz", None, None),
        P("gx", "gy", "gz", None),
        P("gx", "gy", "gz", None),
        P("gx", "gy", "gz", None),
        P("gx", "gy", "gz", None),
        P("gx", "gy", "gz", None),
        P("gx", "gy", "gz"),
    )
    out_specs = (P("gx", "gy", "gz", None, None), P("gx", "gy", "gz", None))
    return jax.shard_map(
        per_device, mesh=mesh, in_specs=in_specs, out_specs=out_specs, check_vma=False
    )
```

time: 35.8 us -> 37.4 us (1.045)
  Pallas kernels: 15.4 us -> 17.8 us
  waiting for transfers between devices: 5.1 us -> 4.17 us
    pallas_call x8, Pallas kernels: 14.6 us -> 16.9 us  [call(): pl.pallas_call(body, out_shape=out, in_specs=[vmem] * len(operands), out_...]
    ppermute x10, waiting for transfers between devices: 5.1 us -> 4.17 us  [swap(): return lax.ppermute(array, axis, pairs)]
  transfers between devices with their start and end apart: 10 -> 10, of which waited for: 6 -> 5; matrix products, arithmetic and copies ran while one was open for 0% -> 0% of each run, Pallas kernels for 26% -> 29%
where the time goes in v4:
time: 37.4 us; the launch traced here: 37.3 us
  Pallas kernels  17.8 us (48%)
  starting transfers between devices  14.6 us (39%)
  waiting for transfers between devices  4.17 us (11%)
  between operations  0.72 us (2%)
    pallas_call x8, Pallas kernels, call(): pl.pallas_call(body, out_shape=out, in_specs=[vmem] * len(operands), out_...  16.9 us
    ppermute x10, starting transfers between devices, swap(): return lax.ppermute(array, axis, pairs)  14.6 us
    ppermute x10, waiting for transfers between devices, swap(): return lax.ppermute(array, axis, pairs)  4.17 us
    pallas_call x1, Pallas kernels, per_device(): pl.pallas_call(functools.partial(pack_kernel, leaves, per_leaf), out_shap...  0.85 us
  transfers between devices with their start and end apart: 10, of which 5 were waited for; matrix products, arithmetic and copies ran while one was open for 0% of the time, Pallas kernels for 29%

profile of v4, /device:TPU:0, one launch (start us, length us, event | category | flops | bytes accessed | tf_op | source)
XLA Modules:
  0.0 37.3 jit_solution(17793135180167098201)
XLA Ops:
  0.6 0.9 %pack.1 = (f32[2,8,128]{2,1,0:T(8,128)S(1)}, f32[2,8,128]{2,1,0:T(8,128)S(1)}) custom-call(f32[1,1,3,2,128]{4,3,2,1,0:T(2,128)} %bitcast.23, f32[1,1,3,2,128]{4,3,2,1,0:T(2,128)} %bitcast.24, f32[1,1,2,128]{3,2,1,0:T(2,128)} %refs_2_.1, f32[1,1,2,128]{3,2,1,0:T(2,128)} %refs_3_.1, f32[1,1,2,128]{3,2,1,0:T(2,128)} %refs_4_.1, f32[1,1,2,128]{3,2,1,0:T(2,128)} %refs_5_.1, ...), custom_call_target="tpu_custom_call" | custom-call | tf_op jit(solution)/shard_map/pack/pallas_call | solution.py:541
  1.5 3.0 %collective-permute-start = (f32[2,8,128]{2,1,0:T(8,128)S(1)}, f32[2,8,128]{2,1,0:T(8,128)S(1)}, u32[]{:S(2)}, u32[]{:S(2)}) collective-permute-start(f32[2,8,128]{2,1,0:T(8,128)S(1)} %get-tuple-element.42.own.refs_0_), channel_id=1, source_target_pairs={{0,4},{4,0},{1,5},{5,1},{2,6},{6,2},{3,7},{7,3},{8,12},{12,8},{9,1... | collective-permute-start | bytes 24584 | tf_op jit(solution)/shard_map/ppermute | solution.py:34
  4.5 1.2 %moments_own.1 = (f32[2,48,128]{2,1,0:T(8,128)S(1)}, bf16[4,256,128]{2,1,0:T(8,128)(2,1)S(1)}, f32[4,128,128]{2,1,0:T(8,128)S(1)}, bf16[4,48,128]{2,1,0:T(8,128)...) custom-call(f32[2,8,128]{2,1,0:T(8,128)S(1)} %get-tuple-element.42.own.re, ...), custom_call_target="tpu_custom_call" | custom-call | flops 3604480 | bytes 16384 | tf_op jit(solution)/shard_map/moments_own/pallas_call | solution.py:585
  5.7 0.4 %collective-permute-done.refs_1_.refs_2_ = f32[2,8,128]{2,1,0:T(8,128)S(1)} collective-permute-done((f32[2,8,128]{2,1,0:T(8,128)S(1)}, f32[2,8,128]{2,1,0:T(8,128)S(1)}, u32[]{:S(2)}, u32[]{:S(2)}) %collective-permute-start) | collective-permute-done | bytes 8224 | tf_op jit(solution)/shard_map/ppermute | solution.py:34
  6.2 0.0 collective-permute-start.1
  6.2 2.2 %collective-permute-start.2 = (f32[2,2,8,128]{3,2,0,1:T(8,128)S(1)}, f32[2,2,8,128]{3,2,0,1:T(8,128)S(1)}, u32[]{:S(2)}, u32[]{:S(2)}) collective-permute-start(f32[2,2,8,128]{3,2,0,1:T(8,128)S(1)} %pad_maximum_fusion.2), channel_id=1, source_target_pairs={{8,16},{16,8},{24,0},{0,24},{9,17},{17,9},{25,1},{1,25},{10,18},{1... | collective-permute-start | bytes 49160 | tf_op jit(solution)/shard_map/ppermute | solution.py:34
  8.3 1.1 %moments_y.1 = (f32[2,48,128]{2,1,0:T(8,128)S(1)}, bf16[8,256,128]{2,1,0:T(8,128)(2,1)S(1)}, f32[8,128,128]{2,1,0:T(8,128)S(1)}) custom-call(f32[2,8,128]{2,1,0:T(8,128)S(1)} %get-tuple-element.42.own.refs_0_, f32[2,8,128]{2,1,0:T(8,128)S(1)} %collective-permute-done.refs_1_.refs_2_, bf16[8,48,128]{2,1,0:T(8,128)(2,1)S(1)} %get-tuple-element.45.refs_2_, ...), custom_call_target="tpu_custom_call" | custom-call | flops 7208960 | bytes 32768 | tf_op jit(solution)/shard_map/moments_y/pallas_call | solution.py:585
  9.4 0.0 collective-permute-done.1
  9.4 0.4 collective-permute-done.2
  9.8 1.7 %collective-permute-start.3 = (f32[6,8,128]{2,1,0:T(8,128)S(1)}, f32[6,8,128]{2,1,0:T(8,128)S(1)}, u32[]{:S(2)}, u32[]{:S(2)}) collective-permute-start(f32[6,8,128]{2,1,0:T(8,128)S(1)} %get-tuple-element.85), channel_id=1, source_target_pairs={{0,1},{1,0},{2,3},{3,2},{4,5},{5,4},{6,7},{7,6},{8,9},{9,8},{10,11... | collective-permute-start | bytes 73736 | tf_op jit(solution)/shard_map/ppermute | solution.py:34
  11.5 2.5 %collective-permute-start.4 = (f32[6,8,128]{2,1,0:T(8,128)S(1)}, f32[6,8,128]{2,1,0:T(8,128)S(1)}, u32[]{:S(2)}, u32[]{:S(2)}) collective-permute-start(f32[6,8,128]{2,1,0:T(8,128)S(1)} %get-tuple-element.84), channel_id=1, source_target_pairs={{1,2},{2,1},{3,0},{0,3},{5,6},{6,5},{7,4},{4,7},{9,10},{10,9},{11,... | collective-permute-start | bytes 73736 | tf_op jit(solution)/shard_map/ppermute | solution.py:34
  14.0 3.8 %moments_x.1 = (f32[2,48,128]{2,1,0:T(8,128)S(1)}, bf16[24,256,128]{2,1,0:T(8,128)(2,1)S(1)}, f32[24,128,128]{2,1,0:T(8,128)S(1)}) custom-call(f32[2,8,128]{2,1,0:T(8,128)S(1)} %get-tuple-element.42.own.refs_0_, f32[2,2,8,128]{3,2,1,0:T(8,128)S(1)} %copy.10.refs_1_.refs_3_, f32[2,2,8,128]{3,2,1,0:T(8,128)S(1)} %copy.11.refs_2_.refs_4_, ...), custom_call_target="tpu_custom_call" | custom-call | flops 21626880 | bytes 98304 | tf_op jit(solution)/shard_map/moments_x/pallas_call | solution.py:585
  17.8 0.0 collective-permute-done.3.refs_1_.refs_3_
  17.8 0.0 collective-permute-done.4.refs_2_.refs_4_
  17.8 3.2 %moments_z.1 = (f32[2,8,128]{2,1,0:T(8,128)S(1)}, bf16[18,256,128]{2,1,0:T(8,128)(2,1)S(1)}, f32[18,128,128]{2,1,0:T(8,128)S(1)}) custom-call(f32[2,8,128]{2,1,0:T(8,128)S(1)} %get-tuple-element.42.own.refs_0_, f32[6,8,128]{2,1,0:T(8,128)S(1)} %collective-permute-done.3.refs_1_.refs_3_, f32[6,8,128]{2,1,0:T(8,128)S(1)} %collective-permute-done.4.refs_2_.refs_4_, ...), custom_call_target="tpu_custom_call" | custom-call | flops 16220160 | bytes 73728 | tf_op jit(solution)/shard_map/moments_z/pallas_call | solution.py:585
  20.9 1.6 %collective-permute-start.5 = (f32[2,8,128]{2,1,0:T(8,128)S(1)}, f32[2,8,128]{2,1,0:T(8,128)S(1)}, u32[]{:S(2)}, u32[]{:S(2)}) collective-permute-start(f32[2,8,128]{2,1,0:T(8,128)S(1)} %get-tuple-element.55.fields.refs_10_), channel_id=1, source_target_pairs={{0,4},{4,0},{1,5},{5,1},{2,6},{6,2},{3,7},{7,3},{8,12},{12,8},{9,1... | collective-permute-start | bytes 24584 | tf_op jit(solution)/shard_map/ppermute | solution.py:34
  22.5 0.9 %force_own.1 = (f32[2,48,128]{2,1,0:T(8,128)S(1)}, f32[2,48,128]{2,1,0:T(8,128)S(1)}, bf16[4,48,128]{2,1,0:T(8,128)(2,1)}, bf16[8,48,128]{2,1,0:T(8,128)(2,1)S(1...) custom-call(f32[2,8,128]{2,1,0:T(8,128)S(1)} %get-tuple-element.42.own.refs_0_, ...), custom_call_target="tpu_custom_call" | custom-call | flops 2359296 | bytes 16384 | tf_op jit(solution)/shard_map/force_own/pallas_call | solution.py:585
  23.4 1.2 %collective-permute-done.5.refs_1_ = f32[2,8,128]{2,1,0:T(8,128)S(1)} collective-permute-done((f32[2,8,128]{2,1,0:T(8,128)S(1)}, f32[2,8,128]{2,1,0:T(8,128)S(1)}, u32[]{:S(2)}, u32[]{:S(2)}) %collective-permute-start.5) | collective-permute-done | bytes 8224 | tf_op jit(solution)/shard_map/ppermute | solution.py:34
  24.7 0.0 collective-permute-start.6
  24.7 1.6 %collective-permute-start.7 = (f32[2,2,8,128]{3,2,0,1:T(8,128)S(1)}, f32[2,2,8,128]{3,2,0,1:T(8,128)S(1)}, u32[]{:S(2)}, u32[]{:S(2)}) collective-permute-start(f32[2,2,8,128]{3,2,0,1:T(8,128)S(1)} %pad_maximum_fusion.3), channel_id=1, source_target_pairs={{8,16},{16,8},{24,0},{0,24},{9,17},{17,9},{25,1},{1,25},{10,18},{1... | collective-permute-start | bytes 49160 | tf_op jit(solution)/shard_map/ppermute | solution.py:34
  26.3 0.9 %force_y.1 = (f32[2,48,128]{2,1,0:T(8,128)S(1)}, f32[2,48,128]{2,1,0:T(8,128)S(1)}) custom-call(f32[2,8,128]{2,1,0:T(8,128)S(1)} %get-tuple-element.42.own.refs_0_, f32[2,8,128]{2,1,0:T(8,128)S(1)} %collective-permute-done.5.refs_1_, f32[2,8,128]{2,1,0:T(8,128)S(1)} %collective-permute-done.refs_1_.refs_2_, ...), custom_call_target="tpu_custom_call" | custom-call | flops 4718592 | bytes 32768 | tf_op jit(solution)/shard_map/force_y/pallas_call | solution.py:585
  27.2 0.0 collective-permute-done.6
  27.2 0.6 %collective-permute-done.7 = f32[2,2,8,128]{3,2,0,1:T(8,128)S(1)} collective-permute-done((f32[2,2,8,128]{3,2,0,1:T(8,128)S(1)}, f32[2,2,8,128]{3,2,0,1:T(8,128)S(1)}, u32[]{:S(2)}, u32[]{:S(2)}) %collective-permute-start.7) | collective-permute-done | bytes 16416 | tf_op jit(solution)/shard_map/ppermute | solution.py:34
  27.8 0.7 %collective-permute-start.8 = (f32[6,8,128]{2,1,0:T(8,128)S(1)}, f32[6,8,128]{2,1,0:T(8,128)S(1)}, u32[]{:S(2)}, u32[]{:S(2)}) collective-permute-start(f32[6,8,128]{2,1,0:T(8,128)S(1)} %get-tuple-element.83), channel_id=1, source_target_pairs={{0,1},{1,0},{2,3},{3,2},{4,5},{5,4},{6,7},{7,6},{8,9},{9,8},{10,11... | collective-permute-start | bytes 73736 | tf_op jit(solution)/shard_map/ppermute | solution.py:34
  28.6 1.2 %collective-permute-start.9 = (f32[6,8,128]{2,1,0:T(8,128)S(1)}, f32[6,8,128]{2,1,0:T(8,128)S(1)}, u32[]{:S(2)}, u32[]{:S(2)}) collective-permute-start(f32[6,8,128]{2,1,0:T(8,128)S(1)} %get-tuple-element.82), channel_id=1, source_target_pairs={{1,2},{2,1},{3,0},{0,3},{5,6},{6,5},{7,4},{4,7},{9,10},{10,9},{11,... | collective-permute-start | bytes 73736 | tf_op jit(solution)/shard_map/ppermute | solution.py:34
  29.8 2.8 %force_x.1 = (f32[2,48,128]{2,1,0:T(8,128)S(1)}, f32[2,48,128]{2,1,0:T(8,128)S(1)}) custom-call(f32[2,8,128]{2,1,0:T(8,128)S(1)} %get-tuple-element.42.own.refs_0_, f32[2,2,8,128]{3,2,1,0:T(8,128)S(1)} %copy.12.refs_1_, f32[2,2,8,128]{3,2,1,0:T(8,128)S(1)} %copy.13.refs_2_, f32[2,2,8,128]{3,2,1,0:T(8,128)S(1)} %copy.10.refs_1_.refs_3_, ...), custom_call_target="tpu_custom_call" | custom-call | flops 14155776 | bytes 98304 | tf_op jit(solution)/shard_map/force_x/pallas_call | solution.py:585
  32.7 0.0 collective-permute-done.8.refs_1_
  32.7 1.5 %collective-permute-done.9.refs_2_ = f32[6,8,128]{2,1,0:T(8,128)S(1)} collective-permute-done((f32[6,8,128]{2,1,0:T(8,128)S(1)}, f32[6,8,128]{2,1,0:T(8,128)S(1)}, u32[]{:S(2)}, u32[]{:S(2)}) %collective-permute-start.9) | collective-permute-done | bytes 24608 | tf_op jit(solution)/shard_map/ppermute | solution.py:34
  34.2 3.1 %force_z.1 = (f32[1,1,3,2,128]{4,3,2,1,0:T(2,128)}, f32[1,1,2,128]{3,2,1,0:T(2,128)}) custom-call(f32[2,8,128]{2,1,0:T(8,128)S(1)} %get-tuple-element.42.own.refs_0_, f32[6,8,128]{2,1,0:T(8,128)S(1)} %collective-permute-done.8.refs_1_, f32[6,8,128]{2,1,0:T(8,128)S(1)} %collective-permute-done.9.refs_2_, ...), custom_call_target="tpu_custom_call" | custom-call | flops 10616832 | bytes 73728 | tf_op jit(solution)/shard_map/force_z/pallas_call | solution.py:585
  (10 shorter events, 0.0 us)
Async XLA Ops:
  1.5 4.7 %collective-permute-start = (f32[2,8,128]{2,1,0:T(8,128)S(1)}, f32[2,8,128]{2,1,0:T(8,128)S(1)}, u32[]{:S(2)}, u32[]{:S(2)}) collective-permute-start(f32[2,8,128]{2,1,0:T(8,128)S(1)} %get-tuple-element.42.own.refs_0_), channel_id=1, source_target_pairs={{0,4},{4,0},{1,5},{5,1},{2,6},{6,2},{3,7},{7,3},{8,12},{12,8},{9,1... | collective-permute-start | bytes 24584 | tf_op jit(solution)/shard_map/ppermute | solution.py:34
  6.2 3.2 %collective-permute-start.1 = (f32[2,2,8,128]{3,2,0,1:T(8,128)S(1)}, f32[2,2,8,128]{3,2,0,1:T(8,128)S(1)}, u32[]{:S(2)}, u32[]{:S(2)}) collective-permute-start(f32[2,2,8,128]{3,2,0,1:T(8,128)S(1)} %pad_maximum_fusion.2), channel_id=1, source_target_pairs={{0,8},{8,0},{16,24},{24,16},{1,9},{9,1},{17,25},{25,17},{2,10},{10... | collective-permute-start | bytes 49160 | tf_op jit(solution)/shard_map/ppermute | solution.py:34
  6.2 3.6 %collective-permute-start.2 = (f32[2,2,8,128]{3,2,0,1:T(8,128)S(1)}, f32[2,2,8,128]{3,2,0,1:T(8,128)S(1)}, u32[]{:S(2)}, u32[]{:S(2)}) collective-permute-start(f32[2,2,8,128]{3,2,0,1:T(8,128)S(1)} %pad_maximum_fusion.2), channel_id=1, source_target_pairs={{8,16},{16,8},{24,0},{0,24},{9,17},{17,9},{25,1},{1,25},{10,18},{1... | collective-permute-start | bytes 49160 | tf_op jit(solution)/shard_map/ppermute | solution.py:34
  9.8 8.0 %collective-permute-start.3 = (f32[6,8,128]{2,1,0:T(8,128)S(1)}, f32[6,8,128]{2,1,0:T(8,128)S(1)}, u32[]{:S(2)}, u32[]{:S(2)}) collective-permute-start(f32[6,8,128]{2,1,0:T(8,128)S(1)} %get-tuple-element.85), channel_id=1, source_target_pairs={{0,1},{1,0},{2,3},{3,2},{4,5},{5,4},{6,7},{7,6},{8,9},{9,8},{10,11... | collective-permute-start | bytes 73736 | tf_op jit(solution)/shard_map/ppermute | solution.py:34
  11.5 6.3 %collective-permute-start.4 = (f32[6,8,128]{2,1,0:T(8,128)S(1)}, f32[6,8,128]{2,1,0:T(8,128)S(1)}, u32[]{:S(2)}, u32[]{:S(2)}) collective-permute-start(f32[6,8,128]{2,1,0:T(8,128)S(1)} %get-tuple-element.84), channel_id=1, source_target_pairs={{1,2},{2,1},{3,0},{0,3},{5,6},{6,5},{7,4},{4,7},{9,10},{10,9},{11,... | collective-permute-start | bytes 73736 | tf_op jit(solution)/shard_map/ppermute | solution.py:34
  20.9 3.7 %collective-permute-start.5 = (f32[2,8,128]{2,1,0:T(8,128)S(1)}, f32[2,8,128]{2,1,0:T(8,128)S(1)}, u32[]{:S(2)}, u32[]{:S(2)}) collective-permute-start(f32[2,8,128]{2,1,0:T(8,128)S(1)} %get-tuple-element.55.fields.refs_10_), channel_id=1, source_target_pairs={{0,4},{4,0},{1,5},{5,1},{2,6},{6,2},{3,7},{7,3},{8,12},{12,8},{9,1... | collective-permute-start | bytes 24584 | tf_op jit(solution)/shard_map/ppermute | solution.py:34
  24.7 2.6 %collective-permute-start.6 = (f32[2,2,8,128]{3,2,0,1:T(8,128)S(1)}, f32[2,2,8,128]{3,2,0,1:T(8,128)S(1)}, u32[]{:S(2)}, u32[]{:S(2)}) collective-permute-start(f32[2,2,8,128]{3,2,0,1:T(8,128)S(1)} %pad_maximum_fusion.3), channel_id=1, source_target_pairs={{0,8},{8,0},{16,24},{24,16},{1,9},{9,1},{17,25},{25,17},{2,10},{10... | collective-permute-start | bytes 49160 | tf_op jit(solution)/shard_map/ppermute | solution.py:34
  24.7 3.2 %collective-permute-start.7 = (f32[2,2,8,128]{3,2,0,1:T(8,128)S(1)}, f32[2,2,8,128]{3,2,0,1:T(8,128)S(1)}, u32[]{:S(2)}, u32[]{:S(2)}) collective-permute-start(f32[2,2,8,128]{3,2,0,1:T(8,128)S(1)} %pad_maximum_fusion.3), channel_id=1, source_target_pairs={{8,16},{16,8},{24,0},{0,24},{9,17},{17,9},{25,1},{1,25},{10,18},{1... | collective-permute-start | bytes 49160 | tf_op jit(solution)/shard_map/ppermute | solution.py:34
  27.8 4.8 %collective-permute-start.8 = (f32[6,8,128]{2,1,0:T(8,128)S(1)}, f32[6,8,128]{2,1,0:T(8,128)S(1)}, u32[]{:S(2)}, u32[]{:S(2)}) collective-permute-start(f32[6,8,128]{2,1,0:T(8,128)S(1)} %get-tuple-element.83), channel_id=1, source_target_pairs={{0,1},{1,0},{2,3},{3,2},{4,5},{5,4},{6,7},{7,6},{8,9},{9,8},{10,11... | collective-permute-start | bytes 73736 | tf_op jit(solution)/shard_map/ppermute | solution.py:34
  28.6 5.6 %collective-permute-start.9 = (f32[6,8,128]{2,1,0:T(8,128)S(1)}, f32[6,8,128]{2,1,0:T(8,128)S(1)}, u32[]{:S(2)}, u32[]{:S(2)}) collective-permute-start(f32[6,8,128]{2,1,0:T(8,128)S(1)} %get-tuple-element.82), channel_id=1, source_target_pairs={{1,2},{2,1},{3,0},{0,3},{5,6},{6,5},{7,4},{4,7},{9,10},{10,9},{11,... | collective-permute-start | bytes 73736 | tf_op jit(solution)/shard_map/ppermute | solution.py:34
